TPU v7x, 256 devices: a whole 4x4x8 slice. The times are simulated.
256 devices in a mesh: seq: 16 (over y_hi, z), tp: 16 (over x, y_lo, core).
Axes of the slice: x: 4, y: 4 (y_hi: 2, y_lo: 2; y = y_hi * 2 + y_lo), z: 8, core: 2. Of those that a mesh axis runs over, the one named last changes fastest.
Arguments:
- tokens: bfloat16 [65536, 1024], P(('seq', 'tp')), may hold values from -6 to 6
- fine_gain: float32 [1024], replicated, may hold values from 0.1 to 1.9
- fine_query: bfloat16 [1024, 1024], replicated, may hold values from -2.0625 to 2.0625
- fine_keyval: bfloat16 [1024, 2048], replicated, may hold values from -0.125 to 0.125
- fine_out: bfloat16 [1024, 1024], replicated, may hold values from -0.1875 to 0.1875
- down_weight: bfloat16 [1024, 4096], P(None, 'tp'), may hold values from -0.1875 to 0.1875
- coarse_gain: float32 [4096], replicated, may hold values from 0.1 to 1.9
- coarse_query: bfloat16 [4096, 4096], P('seq', 'tp'), may hold values from -1.03125 to 1.03125
- coarse_keyval: bfloat16 [4096, 2, 4096], P('seq', None, 'tp'), may hold values from -0.0625 to 0.0625
- coarse_out: bfloat16 [4096, 4096], P('tp'), may hold values from -0.09375 to 0.09375
- up_weight: bfloat16 [4096, 1024], P('tp'), may hold values from -0.09375 to 0.09375
Outputs:
- result: bfloat16 [65536, 1024], P(('seq', 'tp'))
All inputs are finite; a program needn't handle non-finite values.
Results may differ from a plain program's by a relative error of at most 0.02.
Values may be sent and summed in bfloat16 or wider, within the bound.
No kernel may reach another device: no remote copies, remote signals or barrier semaphores. Data moves between devices by JAX's collectives and lax.ppermute only.
A program may use at most 192 MiB of HBM per device.

v0:
```python
import functools
import math

import jax
import jax.numpy as jnp
from jax import lax
from jax.experimental import pallas as pl
from jax.experimental.pallas import tpu as pltpu
from jax.sharding import Mesh, PartitionSpec as P

HEAD = 128
WINDOW = 256
SHORT = 8

epsilon = 1e-06
big_negative = -1e30

ALL = ("yh", "z", "x", "yl", "c")
SEQ = ("yh", "z")
TP = ("x", "yl", "c")
f32 = jnp.float32
bf16 = jnp.bfloat16


def from_behind(array, axis, by):
    size = lax.axis_size(axis)
    pairs = [(i, i + by) for i in range(size) if 0 <= i + by < size]
    return lax.ppermute(array, axis, pairs)


def rotated(array, axis, by):
    size = lax.axis_size(axis)
    return lax.ppermute(array, axis, [(i, (i + by) % size) for i in range(size)])


def around_four(array, axes):
    above, below = rotated(array, axes, 3), rotated(array, axes, 1)
    half = array.shape[0] // 2
    top, bottom = rotated(above[:half], axes, 3), rotated(below[half:], axes, 1)
    return [array, above, top, bottom, below]


def gathered(array, axes):
    copies = jnp.broadcast_to(array, (lax.axis_size(axes), *array.shape))
    return lax.all_to_all(copies, axes, split_axis=0, concat_axis=0, tiled=True)


def exchanged(pieces, axes):
    return lax.all_to_all(pieces, axes, split_axis=0, concat_axis=0, tiled=True)


def normalize(values, scale_gain):
    mean_square = jnp.mean(values * values, axis=-1, keepdims=True)
    return values * lax.rsqrt(mean_square + epsilon) * scale_gain


def dot(a, b):
    return jnp.dot(a, b, preferred_element_type=f32)


def fine_kernel(
    first_ref, tokens_ref, normed_ref, before_ref, query_ref, key_ref, value_ref, out_ref,
    state_ref, pooled_ref, total_ref,
):
    rows = tokens_ref.shape[0]
    step = pl.program_id(0)

    @pl.when(step == 0)
    def _():
        total_ref[...] = tokens_ref[...].astype(f32)

    normed, before = normed_ref[...], before_ref[...]
    factor = math.log2(math.e) / math.sqrt(HEAD)
    query = dot(normed, query_ref[...]).astype(bf16)
    key, value = key_ref[...], value_ref[...]
    keys = jnp.concatenate([dot(before, key).astype(bf16), dot(normed, key).astype(bf16)], 0)
    values = jnp.concatenate([dot(before, value).astype(bf16), dot(normed, value).astype(bf16)], 0)
    row = lax.broadcasted_iota(jnp.int32, (rows, 2 * rows), 0)
    col = lax.broadcasted_iota(jnp.int32, (rows, 2 * rows), 1)
    allowed = (col > row) & (col <= row + WINDOW) & (col >= first_ref[0])
    heads = []
    for k in range(query.shape[1] // HEAD):
        lanes = slice(k * HEAD, (k + 1) * HEAD)
        scores = lax.dot_general(
            query[:, lanes], keys[:, lanes], (((1,), (1,)), ((), ())), preferred_element_type=f32
        )
        scores = jnp.where(allowed, scores * factor, big_negative)
        terms = jnp.exp2(scores - jnp.max(scores, axis=-1, keepdims=True))
        denom = jnp.sum(terms, axis=-1, keepdims=True)
        heads.append((dot(terms.astype(bf16), values[:, lanes]) / denom).astype(bf16))
    total_ref[...] += dot(jnp.concatenate(heads, 1), out_ref[...])

    @pl.when(step == pl.num_programs(0) - 1)
    def _():
        state = total_ref[...].astype(bf16)
        state_ref[...] = state
        runs = state.astype(f32).reshape(rows // SHORT, SHORT, state.shape[1])
        pooled_ref[...] = (jnp.sum(runs, axis=1) * (1.0 / SHORT)).astype(bf16)


def fine_layer(tokens, normed, before, fine_query, fine_keyval, fine_out):
    rows, width = tokens.shape
    pair = 2 * HEAD
    steps = width // pair
    whole = pl.BlockSpec((rows, width), lambda i: (0, 0))
    first = jnp.where(lax.axis_index(ALL) == 0, rows, 0).astype(jnp.int32).reshape(1)
    return pl.pallas_call(
        fine_kernel,
        out_shape=(
            jax.ShapeDtypeStruct((rows, width), bf16),
            jax.ShapeDtypeStruct((rows // SHORT, width), bf16),
        ),
        grid=(steps,),
        in_specs=[pl.BlockSpec(memory_space=pltpu.SMEM), whole, whole, whole]
        + [
            pl.BlockSpec((width, pair), lambda i: (0, i)),
            pl.BlockSpec((width, pair), lambda i: (0, i)),
            pl.BlockSpec((width, pair), lambda i: (0, steps + i)),
            pl.BlockSpec((pair, width), lambda i: (i, 0)),
        ],
        out_specs=(whole, pl.BlockSpec((rows // SHORT, width), lambda i: (0, 0))),
        scratch_shapes=[pltpu.VMEM((rows, width), f32)],
        compiler_params=pltpu.CompilerParams(vmem_limit_bytes=40 << 20),
    )(first, tokens, normed, before, fine_query, fine_keyval, fine_keyval, fine_out)


def attention_kernel(place_ref, q_ref, inverse_ref, *refs):
    chunks, out_ref = refs[:-1], refs[-1]
    tile = q_ref.shape[0]
    step = pl.program_id(0)
    q = q_ref[...]
    row = step * tile + lax.broadcasted_iota(jnp.int32, (tile, tile), 0)
    col = step * tile + lax.broadcasted_iota(jnp.int32, (tile, tile), 1)

    def position(index):
        return (index >> 6) * 512 + ((index >> 5) & 1) * 64 + (index & 31)

    ahead = position(row) - position(col)

    def update(kt, state):
        peak, total, acc = state
        rows = pl.ds(pl.multiple_of(kt * tile, tile), tile)
        inverses, scores = [], []
        for j, chunk in enumerate(chunks):
            s = lax.dot_general(
                q, chunk[rows, :HEAD], (((1,), (1,)), ((), ())), preferred_element_type=f32
            )
            inverses.append(inverse_ref[pl.ds(place_ref[len(chunks) + j], 1), rows])
            bound = jnp.where(kt < step, -(1 << 24), place_ref[j])
            scores.append(jnp.where(ahead >= bound, s * inverses[j], big_negative))
        top = functools.reduce(jnp.maximum, scores)
        new_peak = jnp.maximum(peak, jnp.max(top, axis=-1, keepdims=True))
        fade = jnp.exp2(peak - new_peak)
        acc = acc * fade
        sums = None
        for j, chunk in enumerate(chunks):
            p = jnp.exp2(scores[j] - new_peak)
            sums = p if sums is None else sums + p
            acc = acc + dot((p * inverses[j]).astype(bf16), chunk[rows, HEAD:])
        total = total * fade + jnp.sum(sums, axis=-1, keepdims=True)
        return new_peak, total, acc

    state = (
        jnp.full((tile, 1), big_negative, f32),
        jnp.zeros((tile, 1), f32),
        jnp.zeros((tile, HEAD), f32),
    )
    _, total, acc = lax.fori_loop(0, step + 1, update, state)
    out_ref[...] = (acc / total).astype(bf16)


def coarse_attention(q, inverses, chunks, places, tile=256):
    rows = q.shape[0]
    whole = pl.BlockSpec(chunks[0].shape, lambda i, place: (0, 0))
    return pl.pallas_call(
        attention_kernel,
        out_shape=jax.ShapeDtypeStruct((rows, HEAD), bf16),
        grid_spec=pltpu.PrefetchScalarGridSpec(
            num_scalar_prefetch=1,
            grid=(rows // tile,),
            in_specs=[
                pl.BlockSpec((tile, HEAD), lambda i, place: (i, 0)),
                pl.BlockSpec(inverses.shape, lambda i, place: (0, 0)),
            ]
            + [whole] * len(chunks),
            out_specs=pl.BlockSpec((tile, HEAD), lambda i, place: (i, 0)),
        ),
        compiler_params=pltpu.CompilerParams(vmem_limit_bytes=48 << 20),
    )(places, q, inverses, *chunks)


def gate(array, earlier):
    return lax.optimization_barrier((array, earlier))[0]


def product_kernel(where_ref, down_ref, up_ref, pack_ref, give_ref, keep_ref):
    core, gram_at = where_ref[0], where_ref[1]
    cols = pack_ref.shape[1]
    scaled = [pack_ref[j * cols : (j + 1) * cols, :] for j in range(3)]
    gram_rows = down_ref[pl.ds(pl.multiple_of(gram_at, 128), 128), :]
    right, left = [], []
    for k in range(2):
        lanes = slice(k * HEAD, (k + 1) * HEAD)
        right.append(jnp.concatenate([w[:, lanes] for w in scaled], 1))
        direct = down_ref[pl.ds(pl.multiple_of(where_ref[2 + k], 32), 32), :]
        start = 3 * cols + k * HEAD
        left.append(jnp.concatenate([pack_ref[start : start + HEAD, :], direct], 0))
    half = down_ref.shape[0] // 2
    for out_ref, side in ((give_ref, 1 - core), (keep_ref, core)):
        rows = pl.ds(pl.multiple_of(side * half, half), half)
        one, two = down_ref[rows, :], up_ref[:, rows]
        gram = lax.dot_general(
            one, gram_rows, (((1,), (1,)), ((), ())), preferred_element_type=f32
        ).astype(bf16)
        for k in range(2):
            proj = dot(one, right[k]).astype(bf16)
            lift = dot(left[k], two).astype(bf16)
            head = (k + where_ref[5]) % 2
            for q in range(4):
                block = slice(q * 128, (q + 1) * 128)
                at = (q + 4 - where_ref[4]) % 4
                for j in range(3):
                    lanes = slice(j * 128, (j + 1) * 128)
                    out_ref[at, head, lanes, :] = proj[block, lanes]
                out_ref[at, head, 3 * 128 : 4 * 128, :] = gram[block]
                out_ref[at, head, 4 * 128 :, :] = lift[:, block]


def weight_products(where, down, up, pack):
    width = down.shape[0]
    out = jax.ShapeDtypeStruct((4, 2, 4 * 128 + HEAD + 32, width // 8), bf16)
    whole = pl.BlockSpec(memory_space=pltpu.VMEM)
    return pl.pallas_call(
        product_kernel,
        out_shape=(out, out),
        in_specs=[pl.BlockSpec(memory_space=pltpu.SMEM)] + [whole] * 3,
        out_specs=(whole, whole),
        compiler_params=pltpu.CompilerParams(vmem_limit_bytes=40 << 20),
    )(where, down, up, pack)


def body(
    tokens,
    fine_gain,
    fine_query,
    fine_keyval,
    fine_out,
    down_weight,
    coarse_gain,
    coarse_query,
    coarse_keyval,
    coarse_out,
    up_weight,
):
    width = tokens.shape[1]
    wide = coarse_gain.shape[0]
    cols = coarse_query.shape[1]
    yh, z, x, yl, c = (lax.axis_index(a) for a in ALL)
    y = yh * 2 + yl
    s, t = lax.axis_index(SEQ), lax.axis_index(TP)
    n_seq, n_tp = lax.axis_size(SEQ), lax.axis_size(TP)
    swap = [(b * n_tp + a, a * n_tp + b) for a in range(n_seq) for b in range(n_tp)]

    normed = normalize(tokens.astype(f32), fine_gain).astype(bf16)
    earlier_rows = from_behind(normed, ALL, 1)

    with jax.named_scope("weights"):
        out_sent = lax.dynamic_slice(coarse_out, (0, s * cols), (cols, cols))
        sent = (coarse_query, coarse_keyval[:, 0], coarse_keyval[:, 1], out_sent)
        sent = gate(jnp.concatenate(sent, 0), normed)
        pack = lax.ppermute(sent, ALL, swap)

    fine_state, pooled = fine_layer(
        tokens, normed, earlier_rows, fine_query, fine_keyval, fine_out
    )
    run_count = tokens.shape[0] // SHORT

    with jax.named_scope("gather_rows"):
        across = rotated(pooled, "z", 4)
        pair = jnp.where(z < 4, jnp.stack([pooled, across]), jnp.stack([across, pooled]))
        around = [pair] + [rotated(pair, "z", by) for by in (7, 6, 1)]
        around = jnp.stack(around + around[:3])
        z_rows = lax.dynamic_slice_in_dim(around, (4 - z % 4) % 4, 4, 0).reshape(-1, width)
        y_rows = around_four(z_rows, ("yh", "yl"))
        all_rows = jnp.concatenate(y_rows, 0)
        n = all_rows.shape[0]

    with jax.named_scope("weights"):
        gain = lax.dynamic_slice(coarse_gain, (t * cols,), (cols,))[:, None]
        direct_at = 128 * z + 64 * yh
        where = [c, 128 * z, direct_at, direct_at + 32, x, yl]
        where = jnp.stack(where).astype(jnp.int32)
        ones = jnp.ones((cols, 1), f32)
        pack = gate(pack, pair).astype(f32) * jnp.concatenate([gain] * 3 + [ones], 0)
        pack = gate(pack.astype(bf16), z_rows)
        give, keep = weight_products(where, down_weight, up_weight, pack)
        got = rotated(give, "c", 1)
        both = [keep[i].astype(f32) + got[i].astype(f32) for i in range(4)]
        total = both[0]
        for by in (1, 3, 2):
            total = total + rotated(both[by].astype(bf16), "x", by).astype(f32)
        piece = (total[0] + rotated(total[1].astype(bf16), "yl", 1).astype(f32)).astype(bf16)
        near_half = gathered(gate(piece, tuple(y_rows)), ("x",))
        far_half = rotated(near_half, "c", 1)
        summed = jnp.stack(
            [jnp.where(c == 0, near_half, far_half), jnp.where(c == 0, far_half, near_half)]
        ).reshape(8, *piece.shape)
        proj = summed[:, : 4 * HEAD].reshape(8, 4, HEAD, 128)
        proj = jnp.swapaxes(proj, 1, 2).reshape(width, 4 * HEAD)
        second = jnp.swapaxes(summed[:, 4 * HEAD :], 0, 1).reshape(-1, width)
        below, above = rotated(second, ("yh", "yl"), 1), rotated(second, ("yh", "yl"), 3)
        seconds = [second, below, rotated(below, ("yh", "yl"), 1), above]

    with jax.named_scope("project"):
        half = 3 * HEAD
        qkv = dot(all_rows, proj)

        def in_order(parts):
            twice = jnp.concatenate([parts, parts[:3]], 0)
            return lax.dynamic_slice_in_dim(twice, (4 - y) % 4, 4, 0)

        def by_row(values):
            parts = in_order(values.reshape(4, 8, run_count, -1))
            parts = parts.reshape(2, 2, 4, 2, run_count, -1)
            return jnp.transpose(parts, (0, 3, 2, 1, 4, 5)).reshape(n, -1)

        kv = by_row(qkv[:, HEAD:half].astype(bf16))
        near = [kv] + [rotated(kv, "x", by) for by in (3, 2, 1)]
        slot = lax.dynamic_slice(all_rows, (0, 128 * z), (n, 128))
        squares = jnp.sum(qkv[:, half:] * slot.astype(f32), axis=-1)
        squares = jnp.sum(gathered(squares[None], ("z",)), axis=(0, 1))
        inverse = by_row(lax.rsqrt(jnp.maximum(squares, 0.0) / wide + epsilon))
        factor = math.log2(math.e) / math.sqrt(HEAD)
        q = (by_row(qkv[:, :HEAD]) * (inverse * factor)).astype(bf16)
        every_inverse = gathered(inverse.reshape(1, n), ("x", "c")).reshape(8, n)

    with jax.named_scope("attention"):
        chunks, places, sources = [], [], []
        for by in (0, 1, 3, 2):
            mine = near[by]
            other = rotated(mine, "c", 1)
            source = (x + by) % 4
            shift = 128 * (source - x)
            chunks += [mine, other]
            places += [shift, shift + 32 * (1 - 2 * c)]
            sources += [2 * source + c, 2 * source + 1 - c]
        places = jnp.stack(places + sources).astype(jnp.int32)
        q = gate(q, (below, above))
        heads = coarse_attention(q, every_inverse, chunks, places)

    with jax.named_scope("lift"):
        heads = jnp.swapaxes(heads.reshape(2, 8, 2, run_count, HEAD), 1, 2)
        heads = heads.reshape(4, 8 * run_count, HEAD)
        slot = lax.dynamic_slice(z_rows, (0, 128 * z), (8 * run_count, 128))
        slot = slot.reshape(4, 2, run_count, 4, 32)
        slots = jnp.transpose(slot, (3, 1, 0, 2, 4)).reshape(4, 8 * run_count, 32)
        total = None
        for by in range(4):
            part = lax.dynamic_index_in_dim(heads, (y + by) % 4, 0, keepdims=False)
            if by:
                part = rotated(part, ("yh", "yl"), by)
            slot = lax.dynamic_index_in_dim(slots, (y + 4 - by) % 4, 0, keepdims=False)
            product = dot(jnp.concatenate([part, slot], 1), seconds[by])
            total = product if total is None else total + product
        lifted = exchanged(total.astype(bf16).reshape(8, run_count, width), ("z",))
        lifted = jnp.sum(lifted.astype(f32), axis=0)
        before = from_behind(lifted[run_count - 1 :], ALL, 1)
        lifted = jnp.concatenate([before, lifted[: run_count - 1]], 0)
        result = fine_state.astype(f32) + jnp.repeat(lifted, SHORT, axis=0)
    return result.astype(bf16)


def solution(mesh):
    fine = Mesh(mesh.devices.reshape(2, 8, 4, 2, 2), ALL)
    return jax.shard_map(
        body,
        mesh=fine,
        in_specs=(
            P(ALL, None),
            P(),
            P(),
            P(),
            P(),
            P(None, TP),
            P(),
            P(SEQ, TP),
            P(SEQ, None, TP),
            P(TP, None),
            P(TP, None),
        ),
        out_specs=P(ALL, None),
        check_vma=False,
    )
```

profile of v0, /device:TPU:16, one launch (start us, length us, event | category | flops | bytes accessed | tf_op | source)
XLA Modules:
  0.0 226.3 jit_solution(8079389371463185375)
XLA Ops:
  0.0 1.4 fusion.2
  1.4 1.3 fusion.4.normed_ref
  2.7 1.9 collective-permute-start
  4.6 2.2 fusion.40
  6.9 1.0 copy_bitcast_fusion.1
  8.7 4.7 %collective-permute-start.9 = (bf16[1024,256]{1,0:T(8,128)(2,1)}, bf16[1024,256]{1,0:T(8,128)(2,1)}, u32[]{:S(2)}, u32[]{:S(2)}) collective-permute-start(bf16[1024,256]{1,0:T(8,128)(2,1)} %pad_maximum_fusion.1), channel_id=1, source_target_pairs={{0,0},{16,1},{32,2},{48,3},{64,4},{80,5},{96,6},{112,7},{128,8},{1... | collective-permute-start | bytes 1572872 | tf_op jit(solution)/shard_map/weights/ppermute | solution.py:271
  14.3 5.1 %collective-permute-done.before_ref = bf16[256,1024]{1,0:T(8,128)(2,1)} collective-permute-done((bf16[256,1024]{1,0:T(8,128)(2,1)S(1)}, bf16[256,1024]{1,0:T(8,128)(2,1)}, u32[]{:S(2)}, u32[]{:S(2)}) %collective-permute-start) | collective-permute-done | bytes 524320 | tf_op jit(solution)/shard_map/ppermute | solution.py:28
  19.4 2.2 copy-done.1
  21.6 1.6 copy-done.3
  23.2 1.6 copy-done.4
  24.8 9.1 %shard_map.109 = (bf16[256,1024]{1,0:T(8,128)(2,1)S(1)}, bf16[32,1024]{1,0:T(8,128)(2,1)S(1)}) custom-call(s32[1]{0:T(128)} %bitcast.first_ref, bf16[256,1024]{1,0:T(8,128)(2,1)S(1)} %copy-done.2, bf16[256,1024]{1,0:T(8,128)(2,1)S(1)} %fusion.4.normed_ref, bf16[256,1024]{1,0:T(8,128)(2,1)} %collective-permute-done.before_ref, ...), custom_call_target="tpu_custom_call" | custom-call | tf_op jit(solution)/shard_map/pallas_call | solution.py:107
  34.6 5.3 %collective-permute-start.1 = (bf16[32,1024]{1,0:T(8,128)(2,1)S(1)}, bf16[32,1024]{1,0:T(8,128)(2,1)S(1)}, u32[]{:S(2)}, u32[]{:S(2)}) collective-permute-start(bf16[32,1024]{1,0:T(8,128)(2,1)S(1)} %get-tuple-element.15), channel_id=1, source_target_pairs={{0,64},{16,80},{32,96},{48,112},{64,0},{80,16},{96,32},{112,48},{1... | collective-permute-start | bytes 196616 | tf_op jit(solution)/shard_map/gather_rows/ppermute | solution.py:33
  40.1 2.9 %collective-permute-done.1 = bf16[32,1024]{1,0:T(8,128)(2,1)S(1)} collective-permute-done((bf16[32,1024]{1,0:T(8,128)(2,1)S(1)}, bf16[32,1024]{1,0:T(8,128)(2,1)S(1)}, u32[]{:S(2)}, u32[]{:S(2)}) %collective-permute-start.1) | collective-permute-done | bytes 65568 | tf_op jit(solution)/shard_map/gather_rows/ppermute | solution.py:33
  43.0 4.8 %collective-permute-start.2 = (bf16[2,32,1024]{2,1,0:T(8,128)(2,1)S(1)}, bf16[2,32,1024]{2,1,0:T(8,128)(2,1)S(1)}, u32[]{:S(2)}, u32[]{:S(2)}) collective-permute-start(bf16[2,32,1024]{2,1,0:T(8,128)(2,1)S(1)} %maximum_select_fusion.1), channel_id=1, source_target_pairs={{0,112},{16,0},{32,16},{48,32},{64,48},{80,64},{96,80},{112,96},{1... | collective-permute-start | bytes 393224 | tf_op jit(solution)/shard_map/gather_rows/ppermute | solution.py:33
  47.8 2.5 %collective-permute-start.3 = (bf16[2,32,1024]{2,1,0:T(8,128)(2,1)S(1)}, bf16[2,32,1024]{2,1,0:T(8,128)(2,1)S(1)}, u32[]{:S(2)}, u32[]{:S(2)}) collective-permute-start(bf16[2,32,1024]{2,1,0:T(8,128)(2,1)S(1)} %maximum_select_fusion.1), channel_id=1, source_target_pairs={{0,96},{16,112},{32,0},{48,16},{64,32},{80,48},{96,64},{112,80},{1... | collective-permute-start | bytes 393224 | tf_op jit(solution)/shard_map/gather_rows/ppermute | solution.py:33
  50.3 1.2 multiply_convert_fusion.pack_ref
  51.6 2.9 %collective-permute-done.2 = bf16[2,32,1024]{2,1,0:T(8,128)(2,1)S(1)} collective-permute-done((bf16[2,32,1024]{2,1,0:T(8,128)(2,1)S(1)}, bf16[2,32,1024]{2,1,0:T(8,128)(2,1)S(1)}, u32[]{:S(2)}, u32[]{:S(2)}) %collective-permute-start.2) | collective-permute-done | bytes 131104 | tf_op jit(solution)/shard_map/gather_rows/ppermute | solution.py:33
  54.5 8.0 %collective-permute-done.3 = bf16[2,32,1024]{2,1,0:T(8,128)(2,1)S(1)} collective-permute-done((bf16[2,32,1024]{2,1,0:T(8,128)(2,1)S(1)}, bf16[2,32,1024]{2,1,0:T(8,128)(2,1)S(1)}, u32[]{:S(2)}, u32[]{:S(2)}) %collective-permute-start.3) | collective-permute-done | bytes 131104 | tf_op jit(solution)/shard_map/gather_rows/ppermute | solution.py:33
  62.7 1.7 weights.1
  64.5 3.1 %collective-permute-done.10 = bf16[4,2,672,128]{3,2,1,0:T(8,128)(2,1)S(1)} collective-permute-done((bf16[4,2,672,128]{3,2,1,0:T(8,128)(2,1)S(1)}, bf16[4,2,672,128]{3,2,1,0:T(8,128)(2,1)S(1)}, u32[]{:S(2)}, u32[]{:S(2)}) %collective-permute-start.10) | collective-permute-done | bytes 1376288 | tf_op jit(solution)/shard_map/weights/ppermute | solution.py:33
  67.9 1.2 collective-permute-start.13
  69.1 2.0 collective-permute-start.11
  71.1 1.5 collective-permute-start.5
  72.6 1.0 collective-permute-start.7
  73.6 6.8 %collective-permute-done.13 = bf16[2,672,128]{2,1,0:T(8,128)(2,1)S(1)} collective-permute-done((bf16[2,672,128]{2,1,0:T(8,128)(2,1)S(1)}, bf16[2,672,128]{2,1,0:T(8,128)(2,1)S(1)}, u32[]{:S(2)}, u32[]{:S(2)}) %collective-permute-start.13) | collective-permute-done | bytes 344096 | tf_op jit(solution)/shard_map/weights/ppermute | solution.py:33
  80.9 6.0 %collective-permute-done.11 = bf16[2,672,128]{2,1,0:T(8,128)(2,1)S(1)} collective-permute-done((bf16[2,672,128]{2,1,0:T(8,128)(2,1)S(1)}, bf16[2,672,128]{2,1,0:T(8,128)(2,1)S(1)}, u32[]{:S(2)}, u32[]{:S(2)}) %collective-permute-start.11) | collective-permute-done | bytes 344096 | tf_op jit(solution)/shard_map/weights/ppermute | solution.py:33
  87.2 1.6 collective-permute-start.14
  88.9 2.1 collective-permute-start.8
  91.0 3.5 %collective-permute-done.14 = bf16[672,128]{1,0:T(8,128)(2,1)S(1)} collective-permute-done((bf16[672,128]{1,0:T(8,128)(2,1)S(1)}, bf16[672,128]{1,0:T(8,128)(2,1)S(1)}, u32[]{:S(2)}, u32[]{:S(2)}) %collective-permute-start.14) | collective-permute-done | bytes 172064 | tf_op jit(solution)/shard_map/weights/ppermute | solution.py:33
  94.5 4.6 %collective-permute-done.6 = bf16[128,1024]{1,0:T(8,128)(2,1)S(1)} collective-permute-done((bf16[128,1024]{1,0:T(8,128)(2,1)S(1)}, bf16[128,1024]{1,0:T(8,128)(2,1)S(1)}, u32[]{:S(2)}, u32[]{:S(2)}) %collective-permute-start.6) | collective-permute-done | bytes 262176 | tf_op jit(solution)/shard_map/gather_rows/ppermute | solution.py:33
  100.6 1.0 broadcast_in_dim.23
  101.5 3.7 %all-to-all-start = ((bf16[4,672,128]{2,1,0:T(8,128)(2,1)}), bf16[4,672,128]{2,1,0:T(8,128)(2,1)S(1)}, u32[]{:S(2)}, u32[]{:S(2)}) async-start(bf16[4,672,128]{2,1,0:T(8,128)(2,1)} %broadcast_in_dim.23), calls=%async_computation | async-start | bytes 1376256 | tf_op jit(solution)/shard_map/weights/all_to_all | solution.py:45
  105.3 0.9 reshape.207
  106.2 1.9 copy.82
  108.1 1.2 reshape.208
  109.3 6.8 %all-to-all-done = bf16[4,672,128]{2,1,0:T(8,128)(2,1)S(1)} async-done(((bf16[4,672,128]{2,1,0:T(8,128)(2,1)}), bf16[4,672,128]{2,1,0:T(8,128)(2,1)S(1)}, u32[]{:S(2)}, u32[]{:S(2)}) %all-to-all-start) | async-done | bytes 688160 | tf_op jit(solution)/shard_map/weights/all_to_all | solution.py:45
  117.8 1.2 constant_dynamic-update-slice_fusion.5
  119.2 1.3 copy-done.13
  120.5 1.2 select_bitcast_fusion.1
  123.1 1.5 copy.75
  124.6 3.1 %fusion.41 = (bf16[1024,512]{1,0:T(8,128)(2,1)S(1)}, f32[1024,512]{1,0:T(8,128)S(1)}) fusion(bf16[1024,1024]{1,0:T(8,128)(2,1)} %copy-done.13, bf16[64,8,8,128]{3,2,1,0:T(8,128)(2,1)} %bitcast.172), kind=kOutput, calls=%fused_computation.101 | convolution fusion | flops 1074266112 | bytes 6291456 | tf_op jit(solution)/shard_map/project/dot_general | solution.py:58
  128.6 1.2 collective-permute-start.19
  129.8 0.9 collective-permute-start.21
  132.1 1.9 fusion.13
  134.6 6.7 %all-to-all-start.1 = ((f32[8,1,1024]{2,1,0:T(1,128)}), f32[8,1,1024]{2,1,0:T(1,128)S(1)}, u32[]{:S(2)}, u32[]{:S(2)}) async-start(f32[8,1,1024]{2,1,0:T(1,128)} %broadcast_in_dim.24), calls=%async_computation.1 | async-start | bytes 65536 | tf_op jit(solution)/shard_map/project/all_to_all | solution.py:45
  141.3 1.1 fusion.12
  143.3 6.1 %all-to-all-done.1 = f32[8,1,1024]{2,1,0:T(1,128)S(1)} async-done(((f32[8,1,1024]{2,1,0:T(1,128)}), f32[8,1,1024]{2,1,0:T(1,128)S(1)}, u32[]{:S(2)}, u32[]{:S(2)}) %all-to-all-start.1) | async-done | bytes 32800 | tf_op jit(solution)/shard_map/project/all_to_all | solution.py:45
  149.6 6.4 %collective-permute-done.21.refs_4_ = bf16[1024,256]{1,0:T(8,128)(2,1)} collective-permute-done((bf16[1024,256]{1,0:T(8,128)(2,1)S(1)}, bf16[1024,256]{1,0:T(8,128)(2,1)}, u32[]{:S(2)}, u32[]{:S(2)}) %collective-permute-start.21) | collective-permute-done | bytes 524320 | tf_op jit(solution)/shard_map/project/ppermute | solution.py:33
  156.6 1.0 collective-permute-start.16
  158.2 4.0 %all-to-all-start.2 = ((f32[8,1,1024]{2,1,0:T(1,128)}), f32[8,1,1024]{2,1,0:T(1,128)}, u32[]{:S(2)}, u32[]{:S(2)}) async-start(f32[8,1,1024]{2,1,0:T(1,128)} %broadcast_in_dim.25), calls=%async_computation.2 | async-start | bytes 65536 | tf_op jit(solution)/shard_map/project/all_to_all | solution.py:45
  162.2 1.2 fusion.14.q_ref
  163.4 4.2 %all-to-all-done.2 = f32[8,1,1024]{2,1,0:T(1,128)} async-done(((f32[8,1,1024]{2,1,0:T(1,128)}), f32[8,1,1024]{2,1,0:T(1,128)}, u32[]{:S(2)}, u32[]{:S(2)}) %all-to-all-start.2) | async-done | bytes 32800 | tf_op jit(solution)/shard_map/project/all_to_all | solution.py:45
  168.4 1.2 collective-permute-start.27
  169.7 15.4 %attention.1 = bf16[1024,128]{1,0:T(8,128)(2,1)S(1)} custom-call(s32[16]{0:T(128)S(1)} %stack.135.place_ref, bf16[1024,128]{1,0:T(8,128)(2,1)S(1)} %fusion.14.q_ref, f32[8,1024]{1,0:T(8,128)S(1)} %bitcast.155, bf16[1024,256]{1,0:T(8,128)(2,1)S(1)} %bitcast.150, bf16[1024,256]{1,0:T(8,128)(2,1)S(1)} %collective-permute-done.18.refs_1_, ...), custom_call_target="tpu_custom_call" | custom-call | tf_op jit(solution)/shard_map/attention/pallas_call | solution.py:175
  185.1 0.9 collective-permute-start.28
  186.1 1.2 collective-permute-start.25
  187.2 1.6 collective-permute-start.26
  188.9 1.3 fusion.21
  190.4 1.3 convolution_add_fusion.1
  191.6 1.3 fusion.31
  193.3 22.8 %all_to_all.20 = bf16[8,32,1024]{2,1,0:T(8,128)(2,1)S(1)} all-to-all(bf16[8,32,1024]{2,1,0:T(8,128)(2,1)S(1)} %bitcast.168), channel_id=1, replica_groups=mesh['yh'=2,'z'=8,'x'=4,'yl'=2,'c'=2] {'z'}, dimensions={0} | all-to-all | bytes 1048576 | tf_op jit(solution)/shard_map/lift/all_to_all | solution.py:49
  216.2 1.9 collective-permute-start.29
  218.2 7.2 %collective-permute-done.29 = f32[1,1024]{1,0:T(1,128)S(1)} collective-permute-done((f32[1,1024]{1,0:T(1,128)S(1)}, f32[1,1024]{1,0:T(1,128)S(1)}, u32[]{:S(2)}, u32[]{:S(2)}) %collective-permute-start.29) | collective-permute-done | bytes 4128 | tf_op jit(solution)/shard_map/lift/ppermute | solution.py:28
  225.4 0.9 fusion.8
  (128 shorter events, 15.6 us)
Async XLA Ops:
  0.0 6.9 %copy-start = (bf16[256,4096]{1,0:T(8,128)(2,1)S(1)}, bf16[256,4096]{1,0:T(8,128)(2,1)}, u32[]{:S(2)}) copy-start(bf16[256,4096]{1,0:T(8,128)(2,1)} %param.20) | copy-start | bytes 6291460
  0.0 7.9 %copy-start.20 = (bf16[256,256]{1,0:T(8,128)(2,1)S(1)}, bf16[256,256]{1,0:T(8,128)(2,1)}, u32[]{:S(2)}) copy-start(bf16[256,256]{1,0:T(8,128)(2,1)} %param.18) | copy-start | bytes 393220
  1.4 18.0 %copy-start.2 = (bf16[256,1024]{1,0:T(8,128)(2,1)S(1)}, bf16[256,1024]{1,0:T(8,128)(2,1)}, u32[]{:S(2)}) copy-start(bf16[256,1024]{1,0:T(8,128)(2,1)} %tokens_ref.1) | copy-start | bytes 1572868
  2.7 16.7 %collective-permute-start = (bf16[256,1024]{1,0:T(8,128)(2,1)S(1)}, bf16[256,1024]{1,0:T(8,128)(2,1)}, u32[]{:S(2)}, u32[]{:S(2)}) collective-permute-start(bf16[256,1024]{1,0:T(8,128)(2,1)S(1)} %fusion.4.normed_ref), channel_id=1, source_target_pairs={{0,1},{1,2},{2,3},{3,4},{4,5},{5,6},{6,7},{7,8},{8,9},{9,10},{10,1... | collective-permute-start | bytes 1572872 | tf_op jit(solution)/shard_map/ppermute | solution.py:28
  8.7 41.6 %collective-permute-start.9 = (bf16[1024,256]{1,0:T(8,128)(2,1)}, bf16[1024,256]{1,0:T(8,128)(2,1)}, u32[]{:S(2)}, u32[]{:S(2)}) collective-permute-start(bf16[1024,256]{1,0:T(8,128)(2,1)} %pad_maximum_fusion.1), channel_id=1, source_target_pairs={{0,0},{16,1},{32,2},{48,3},{64,4},{80,5},{96,6},{112,7},{128,8},{1... | collective-permute-start | bytes 1572872 | tf_op jit(solution)/shard_map/weights/ppermute | solution.py:271
  19.4 2.2 copy-start.1
  21.6 1.6 copy-start.3
  23.2 1.6 copy-start.4
  33.8 0.8 copy-start.7
  34.6 8.3 %collective-permute-start.1 = (bf16[32,1024]{1,0:T(8,128)(2,1)S(1)}, bf16[32,1024]{1,0:T(8,128)(2,1)S(1)}, u32[]{:S(2)}, u32[]{:S(2)}) collective-permute-start(bf16[32,1024]{1,0:T(8,128)(2,1)S(1)} %get-tuple-element.15), channel_id=1, source_target_pairs={{0,64},{16,80},{32,96},{48,112},{64,0},{80,16},{96,32},{112,48},{1... | collective-permute-start | bytes 196616 | tf_op jit(solution)/shard_map/gather_rows/ppermute | solution.py:33
  43.0 19.7 %copy-start.5 = (bf16[1024,256]{1,0:T(8,128)(2,1)S(1)}, bf16[1024,256]{1,0:T(8,128)(2,1)}, u32[]{:S(2)}) copy-start(bf16[1024,256]{1,0:T(8,128)(2,1)} %down_ref.1) | copy-start | bytes 1572868
  43.0 19.7 %copy-start.6 = (bf16[256,1024]{1,0:T(8,128)(2,1)S(1)}, bf16[256,1024]{1,0:T(8,128)(2,1)}, u32[]{:S(2)}) copy-start(bf16[256,1024]{1,0:T(8,128)(2,1)} %up_ref.1) | copy-start | bytes 1572868
  43.0 11.5 %collective-permute-start.2 = (bf16[2,32,1024]{2,1,0:T(8,128)(2,1)S(1)}, bf16[2,32,1024]{2,1,0:T(8,128)(2,1)S(1)}, u32[]{:S(2)}, u32[]{:S(2)}) collective-permute-start(bf16[2,32,1024]{2,1,0:T(8,128)(2,1)S(1)} %maximum_select_fusion.1), channel_id=1, source_target_pairs={{0,112},{16,0},{32,16},{48,32},{64,48},{80,64},{96,80},{112,96},{1... | collective-permute-start | bytes 393224 | tf_op jit(solution)/shard_map/gather_rows/ppermute | solution.py:33
  47.8 14.7 %collective-permute-start.3 = (bf16[2,32,1024]{2,1,0:T(8,128)(2,1)S(1)}, bf16[2,32,1024]{2,1,0:T(8,128)(2,1)S(1)}, u32[]{:S(2)}, u32[]{:S(2)}) collective-permute-start(bf16[2,32,1024]{2,1,0:T(8,128)(2,1)S(1)} %maximum_select_fusion.1), channel_id=1, source_target_pairs={{0,96},{16,112},{32,0},{48,16},{64,32},{80,48},{96,64},{112,80},{1... | collective-permute-start | bytes 393224 | tf_op jit(solution)/shard_map/gather_rows/ppermute | solution.py:33
  50.3 12.2 %collective-permute-start.4 = (bf16[2,32,1024]{2,1,0:T(8,128)(2,1)S(1)}, bf16[2,32,1024]{2,1,0:T(8,128)(2,1)S(1)}, u32[]{:S(2)}, u32[]{:S(2)}) collective-permute-start(bf16[2,32,1024]{2,1,0:T(8,128)(2,1)S(1)} %maximum_select_fusion.1), channel_id=1, source_target_pairs={{0,16},{16,32},{32,48},{48,64},{64,80},{80,96},{96,112},{112,0},{1... | collective-permute-start | bytes 393224 | tf_op jit(solution)/shard_map/gather_rows/ppermute | solution.py:33
  64.4 3.2 %collective-permute-start.10 = (bf16[4,2,672,128]{3,2,1,0:T(8,128)(2,1)S(1)}, bf16[4,2,672,128]{3,2,1,0:T(8,128)(2,1)S(1)}, u32[]{:S(2)}, u32[]{:S(2)}) collective-permute-start(bf16[4,2,672,128]{3,2,1,0:T(8,128)(2,1)S(1)} %get-tuple-element.20), channel_id=1, source_target_pairs={{0,1},{1,0},{2,3},{3,2},{4,5},{5,4},{6,7},{7,6},{8,9},{9,8},{10,11... | collective-permute-start | bytes 4128776 | tf_op jit(solution)/shard_map/weights/ppermute | solution.py:33
  67.9 12.5 %collective-permute-start.13 = (bf16[2,672,128]{2,1,0:T(8,128)(2,1)S(1)}, bf16[2,672,128]{2,1,0:T(8,128)(2,1)S(1)}, u32[]{:S(2)}, u32[]{:S(2)}) collective-permute-start(bf16[2,672,128]{2,1,0:T(8,128)(2,1)S(1)} %get-tuple-element.24), channel_id=1, source_target_pairs={{0,8},{4,12},{8,0},{12,4},{1,9},{5,13},{9,1},{13,5},{2,10},{6,14},... | collective-permute-start | bytes 1032200 | tf_op jit(solution)/shard_map/weights/ppermute | solution.py:33
  69.1 11.8 %collective-permute-start.12 = (bf16[2,672,128]{2,1,0:T(8,128)(2,1)S(1)}, bf16[2,672,128]{2,1,0:T(8,128)(2,1)S(1)}, u32[]{:S(2)}, u32[]{:S(2)}) collective-permute-start(bf16[2,672,128]{2,1,0:T(8,128)(2,1)S(1)} %get-tuple-element.25), channel_id=1, source_target_pairs={{0,12},{4,0},{8,4},{12,8},{1,13},{5,1},{9,5},{13,9},{2,14},{6,2},{... | collective-permute-start | bytes 1032200 | tf_op jit(solution)/shard_map/weights/ppermute | solution.py:33
  69.1 17.8 %collective-permute-start.11 = (bf16[2,672,128]{2,1,0:T(8,128)(2,1)S(1)}, bf16[2,672,128]{2,1,0:T(8,128)(2,1)S(1)}, u32[]{:S(2)}, u32[]{:S(2)}) collective-permute-start(bf16[2,672,128]{2,1,0:T(8,128)(2,1)S(1)} %get-tuple-element.23), channel_id=1, source_target_pairs={{0,4},{4,8},{8,12},{12,0},{1,5},{5,9},{9,13},{13,1},{2,6},{6,10},{... | collective-permute-start | bytes 1032200 | tf_op jit(solution)/shard_map/weights/ppermute | solution.py:33
  71.1 17.6 %collective-permute-start.5 = (bf16[256,1024]{1,0:T(8,128)(2,1)S(1)}, bf16[256,1024]{1,0:T(8,128)(2,1)S(1)}, u32[]{:S(2)}, u32[]{:S(2)}) collective-permute-start(bf16[256,1024]{1,0:T(8,128)(2,1)S(1)} %bitcast.160), channel_id=1, source_target_pairs={{0,130},{2,0},{128,2},{130,128},{1,131},{3,1},{129,3},{131,129},{4... | collective-permute-start | bytes 1572872 | tf_op jit(solution)/shard_map/gather_rows/ppermute | solution.py:33
  72.6 16.3 %collective-permute-start.7 = (bf16[256,1024]{1,0:T(8,128)(2,1)S(1)}, bf16[256,1024]{1,0:T(8,128)(2,1)S(1)}, u32[]{:S(2)}, u32[]{:S(2)}) collective-permute-start(bf16[256,1024]{1,0:T(8,128)(2,1)S(1)} %bitcast.161), channel_id=1, source_target_pairs={{0,2},{2,128},{128,130},{130,0},{1,3},{3,129},{129,131},{131,1},{4... | collective-permute-start | bytes 1572872 | tf_op jit(solution)/shard_map/gather_rows/ppermute | solution.py:33
  87.2 7.3 %collective-permute-start.14 = (bf16[672,128]{1,0:T(8,128)(2,1)S(1)}, bf16[672,128]{1,0:T(8,128)(2,1)S(1)}, u32[]{:S(2)}, u32[]{:S(2)}) collective-permute-start(bf16[672,128]{1,0:T(8,128)(2,1)S(1)} %fusion.20), channel_id=1, source_target_pairs={{0,2},{2,0},{1,3},{3,1},{4,6},{6,4},{5,7},{7,5},{8,10},{10,8},{9,1... | collective-permute-start | bytes 516104 | tf_op jit(solution)/shard_map/weights/ppermute | solution.py:33
  88.7 10.4 %copy-start.12 = (bf16[256,1024]{1,0:T(8,128)(2,1)}, bf16[256,1024]{1,0:T(8,128)(2,1)S(1)}, u32[]{:S(2)}) copy-start(bf16[256,1024]{1,0:T(8,128)(2,1)S(1)} %collective-permute-done.5) | copy-start | bytes 1572868
  88.8 10.4 %collective-permute-start.6 = (bf16[128,1024]{1,0:T(8,128)(2,1)S(1)}, bf16[128,1024]{1,0:T(8,128)(2,1)S(1)}, u32[]{:S(2)}, u32[]{:S(2)}) collective-permute-start(bf16[128,1024]{1,0:T(8,128)(2,1)S(1)} %slice.114), channel_id=1, source_target_pairs={{0,130},{2,0},{128,2},{130,128},{1,131},{3,1},{129,3},{131,129},{4... | collective-permute-start | bytes 786440 | tf_op jit(solution)/shard_map/gather_rows/ppermute | solution.py:33
  88.9 5.7 %copy-start.10 = (bf16[256,1024]{1,0:T(8,128)(2,1)}, bf16[256,1024]{1,0:T(8,128)(2,1)S(1)}, u32[]{:S(2)}) copy-start(bf16[256,1024]{1,0:T(8,128)(2,1)S(1)} %collective-permute-done.7) | copy-start | bytes 1572868
  88.9 10.3 %collective-permute-start.8 = (bf16[128,1024]{1,0:T(8,128)(2,1)S(1)}, bf16[128,1024]{1,0:T(8,128)(2,1)S(1)}, u32[]{:S(2)}, u32[]{:S(2)}) collective-permute-start(bf16[128,1024]{1,0:T(8,128)(2,1)S(1)} %slice.115), channel_id=1, source_target_pairs={{0,2},{2,128},{128,130},{130,0},{1,3},{3,129},{129,131},{131,1},{4... | collective-permute-start | bytes 786440 | tf_op jit(solution)/shard_map/gather_rows/ppermute | solution.py:33
  99.2 0.7 copy-start.16
  99.9 0.7 copy-start.18
  101.5 14.5 %all-to-all-start = ((bf16[4,672,128]{2,1,0:T(8,128)(2,1)}), bf16[4,672,128]{2,1,0:T(8,128)(2,1)S(1)}, u32[]{:S(2)}, u32[]{:S(2)}) async-start(bf16[4,672,128]{2,1,0:T(8,128)(2,1)} %broadcast_in_dim.23), calls=%async_computation | async-start | bytes 1376256 | tf_op jit(solution)/shard_map/weights/all_to_all | solution.py:45
  116.1 4.4 %collective-permute-start.15 = (bf16[4,672,128]{2,1,0:T(8,128)(2,1)S(1)}, bf16[4,672,128]{2,1,0:T(8,128)(2,1)}, u32[]{:S(2)}, u32[]{:S(2)}) collective-permute-start(bf16[4,672,128]{2,1,0:T(8,128)(2,1)S(1)} %all-to-all-done), channel_id=1, source_target_pairs={{0,1},{1,0},{2,3},{3,2},{4,5},{5,4},{6,7},{7,6},{8,9},{9,8},{10,11... | collective-permute-start | bytes 2064392 | tf_op jit(solution)/shard_map/weights/ppermute | solution.py:33
  117.8 1.2 copy-start.17
  117.8 1.3 copy-start.19
  117.8 1.4 copy-start.11
  119.2 1.3 copy-start.13
  121.8 1.2 copy-start.9
  128.0 41.6 %collective-permute-start.18 = (bf16[1024,256]{1,0:T(8,128)(2,1)S(1)}, bf16[1024,256]{1,0:T(8,128)(2,1)S(1)}, u32[]{:S(2)}, u32[]{:S(2)}) collective-permute-start(bf16[1024,256]{1,0:T(8,128)(2,1)S(1)} %bitcast.146), channel_id=1, source_target_pairs={{0,1},{1,0},{2,3},{3,2},{4,5},{5,4},{6,7},{7,6},{8,9},{9,8},{10,11... | collective-permute-start | bytes 1572872 | tf_op jit(solution)/shard_map/attention/ppermute | solution.py:33
  128.6 20.9 %collective-permute-start.19 = (bf16[1024,256]{1,0:T(8,128)(2,1)S(1)}, bf16[1024,256]{1,0:T(8,128)(2,1)}, u32[]{:S(2)}, u32[]{:S(2)}) collective-permute-start(bf16[1024,256]{1,0:T(8,128)(2,1)S(1)} %bitcast.147), channel_id=1, source_target_pairs={{0,12},{4,0},{8,4},{12,8},{1,13},{5,1},{9,5},{13,9},{2,14},{6,2},{... | collective-permute-start | bytes 1572872 | tf_op jit(solution)/shard_map/project/ppermute | solution.py:33
  129.8 26.2 %collective-permute-start.21 = (bf16[1024,256]{1,0:T(8,128)(2,1)S(1)}, bf16[1024,256]{1,0:T(8,128)(2,1)}, u32[]{:S(2)}, u32[]{:S(2)}) collective-permute-start(bf16[1024,256]{1,0:T(8,128)(2,1)S(1)} %bitcast.148), channel_id=1, source_target_pairs={{0,4},{4,8},{8,12},{12,0},{1,5},{5,9},{9,13},{13,1},{2,6},{6,10},{... | collective-permute-start | bytes 1572872 | tf_op jit(solution)/shard_map/project/ppermute | solution.py:33
  130.7 25.3 %collective-permute-start.23 = (bf16[1024,256]{1,0:T(8,128)(2,1)S(1)}, bf16[1024,256]{1,0:T(8,128)(2,1)}, u32[]{:S(2)}, u32[]{:S(2)}) collective-permute-start(bf16[1024,256]{1,0:T(8,128)(2,1)S(1)} %bitcast.149), channel_id=1, source_target_pairs={{0,8},{4,12},{8,0},{12,4},{1,9},{5,13},{9,1},{13,5},{2,10},{6,14},... | collective-permute-start | bytes 1572872 | tf_op jit(solution)/shard_map/project/ppermute | solution.py:33
  131.3 25.4 %collective-permute-start.17 = (bf16[160,1024]{1,0:T(8,128)(2,1)}, bf16[160,1024]{1,0:T(8,128)(2,1)}, u32[]{:S(2)}, u32[]{:S(2)}) collective-permute-start(bf16[160,1024]{1,0:T(8,128)(2,1)} %copy_bitcast_fusion), channel_id=1, source_target_pairs={{0,130},{2,0},{128,2},{130,128},{1,131},{3,1},{129,3},{131,129},{4... | collective-permute-start | bytes 983048 | tf_op jit(solution)/shard_map/weights/ppermute | solution.py:33
  134.6 14.7 %all-to-all-start.1 = ((f32[8,1,1024]{2,1,0:T(1,128)}), f32[8,1,1024]{2,1,0:T(1,128)S(1)}, u32[]{:S(2)}, u32[]{:S(2)}) async-start(f32[8,1,1024]{2,1,0:T(1,128)} %broadcast_in_dim.24), calls=%async_computation.1 | async-start | bytes 65536 | tf_op jit(solution)/shard_map/project/all_to_all | solution.py:45
  149.6 20.1 %collective-permute-start.20 = (bf16[1024,256]{1,0:T(8,128)(2,1)}, bf16[1024,256]{1,0:T(8,128)(2,1)}, u32[]{:S(2)}, u32[]{:S(2)}) collective-permute-start(bf16[1024,256]{1,0:T(8,128)(2,1)} %collective-permute-done.19.refs_2_), channel_id=1, source_target_pairs={{0,1},{1,0},{2,3},{3,2},{4,5},{5,4},{6,7},{7,6},{8,9},{9,8},{10,11... | collective-permute-start | bytes 1572872 | tf_op jit(solution)/shard_map/attention/ppermute | solution.py:33
  156.0 13.6 %collective-permute-start.22 = (bf16[1024,256]{1,0:T(8,128)(2,1)}, bf16[1024,256]{1,0:T(8,128)(2,1)}, u32[]{:S(2)}, u32[]{:S(2)}) collective-permute-start(bf16[1024,256]{1,0:T(8,128)(2,1)} %collective-permute-done.21.refs_4_), channel_id=1, source_target_pairs={{0,1},{1,0},{2,3},{3,2},{4,5},{5,4},{6,7},{7,6},{8,9},{9,8},{10,11... | collective-permute-start | bytes 1572872 | tf_op jit(solution)/shard_map/attention/ppermute | solution.py:33
  156.0 13.6 %collective-permute-start.24 = (bf16[1024,256]{1,0:T(8,128)(2,1)}, bf16[1024,256]{1,0:T(8,128)(2,1)}, u32[]{:S(2)}, u32[]{:S(2)}) collective-permute-start(bf16[1024,256]{1,0:T(8,128)(2,1)} %collective-permute-done.23.refs_6_), channel_id=1, source_target_pairs={{0,1},{1,0},{2,3},{3,2},{4,5},{5,4},{6,7},{7,6},{8,9},{9,8},{10,11... | collective-permute-start | bytes 1572872 | tf_op jit(solution)/shard_map/attention/ppermute | solution.py:33
  156.6 11.8 %collective-permute-start.16 = (bf16[160,1024]{1,0:T(8,128)(2,1)}, bf16[160,1024]{1,0:T(8,128)(2,1)}, u32[]{:S(2)}, u32[]{:S(2)}) collective-permute-start(bf16[160,1024]{1,0:T(8,128)(2,1)} %copy_bitcast_fusion), channel_id=1, source_target_pairs={{0,2},{2,128},{128,130},{130,0},{1,3},{3,129},{129,131},{131,1},{4... | collective-permute-start | bytes 983048 | tf_op jit(solution)/shard_map/weights/ppermute | solution.py:33
  158.2 9.4 %all-to-all-start.2 = ((f32[8,1,1024]{2,1,0:T(1,128)}), f32[8,1,1024]{2,1,0:T(1,128)}, u32[]{:S(2)}, u32[]{:S(2)}) async-start(f32[8,1,1024]{2,1,0:T(1,128)} %broadcast_in_dim.25), calls=%async_computation.2 | async-start | bytes 65536 | tf_op jit(solution)/shard_map/project/all_to_all | solution.py:45
  168.4 24.5 %collective-permute-start.27 = (bf16[160,1024]{1,0:T(8,128)(2,1)}, bf16[160,1024]{1,0:T(8,128)(2,1)S(1)}, u32[]{:S(2)}, u32[]{:S(2)}) collective-permute-start(bf16[160,1024]{1,0:T(8,128)(2,1)} %collective-permute-done.16), channel_id=1, source_target_pairs={{0,2},{2,128},{128,130},{130,0},{1,3},{3,129},{129,131},{131,1},{4... | collective-permute-start | bytes 983048 | tf_op jit(solution)/shard_map/weights/ppermute | solution.py:33
  169.7 19.2 %copy-start.15 = (bf16[256,32]{1,0:T(8,128)(2,1)S(1)}, bf16[256,32]{1,0:T(8,128)(2,1)}, u32[]{:S(2)}) copy-start(bf16[256,32]{1,0:T(8,128)(2,1)} %copy.83) | copy-start | bytes 49156
  185.1 5.3 %copy-start.14 = (bf16[256,32]{1,0:T(8,128)(2,1)S(1)}, bf16[256,32]{1,0:T(8,128)(2,1)}, u32[]{:S(2)}) copy-start(bf16[256,32]{1,0:T(8,128)(2,1)} %copy.84) | copy-start | bytes 49156
  185.1 6.5 %collective-permute-start.28 = (bf16[256,128]{1,0:T(8,128)(2,1)S(1)}, bf16[256,128]{1,0:T(8,128)(2,1)S(1)}, u32[]{:S(2)}, u32[]{:S(2)}) collective-permute-start(bf16[256,128]{1,0:T(8,128)(2,1)S(1)} %get-tuple-element.31), channel_id=1, source_target_pairs={{0,130},{2,0},{128,2},{130,128},{1,131},{3,1},{129,3},{131,129},{4... | collective-permute-start | bytes 196616 | tf_op jit(solution)/shard_map/lift/ppermute | solution.py:33
  186.1 4.3 %collective-permute-start.25 = (bf16[256,128]{1,0:T(8,128)(2,1)S(1)}, bf16[256,128]{1,0:T(8,128)(2,1)S(1)}, u32[]{:S(2)}, u32[]{:S(2)}) collective-permute-start(bf16[256,128]{1,0:T(8,128)(2,1)S(1)} %get-tuple-element.32), channel_id=1, source_target_pairs={{0,2},{2,128},{128,130},{130,0},{1,3},{3,129},{129,131},{131,1},{4... | collective-permute-start | bytes 196616 | tf_op jit(solution)/shard_map/lift/ppermute | solution.py:33
  187.2 5.8 %collective-permute-start.26 = (bf16[256,128]{1,0:T(8,128)(2,1)S(1)}, bf16[256,128]{1,0:T(8,128)(2,1)S(1)}, u32[]{:S(2)}, u32[]{:S(2)}) collective-permute-start(bf16[256,128]{1,0:T(8,128)(2,1)S(1)} %get-tuple-element.30), channel_id=1, source_target_pairs={{0,128},{2,130},{128,0},{130,2},{1,129},{3,131},{129,1},{131,3},{4... | collective-permute-start | bytes 196616 | tf_op jit(solution)/shard_map/lift/ppermute | solution.py:33
  192.9 32.5 %copy-start.8 = (bf16[256,1024]{1,0:T(8,128)(2,1)S(1)}, bf16[256,1024]{1,0:T(8,128)(2,1)}, u32[]{:S(2)}) copy-start(bf16[256,1024]{1,0:T(8,128)(2,1)} %copy-done.7) | copy-start | bytes 1572868
  216.2 9.1 %collective-permute-start.29 = (f32[1,1024]{1,0:T(1,128)S(1)}, f32[1,1024]{1,0:T(1,128)S(1)}, u32[]{:S(2)}, u32[]{:S(2)}) collective-permute-start(f32[1,1024]{1,0:T(1,128)S(1)} %slice.129), channel_id=1, source_target_pairs={{0,1},{1,2},{2,3},{3,4},{4,5},{5,6},{6,7},{7,8},{8,9},{9,10},{10,1... | collective-permute-start | bytes 12296 | tf_op jit(solution)/shard_map/lift/ppermute | solution.py:28
where the time goes:
time: 228 us; the launch traced here: 226 us
  waiting for transfers between devices  74.5 us (33%)
  starting transfers between devices  54.8 us (24%)
  local copies, waits for them, and re-layouts  28 us (12%)
  Pallas kernels  26.1 us (11%)
  blocking collectives  22.8 us (10%)
  other arithmetic  12.2 us (5%)
  matrix products  7.22 us (3%)
    ppermute x27, waiting for transfers between devices, rotated(): lax.ppermute(array, axis, [(i, (i + by) % size) for i in range(size)])  45.1 us
    ppermute x27, starting transfers between devices, rotated(): lax.ppermute(array, axis, [(i, (i + by) % size) for i in range(size)])  31.9 us
    all_to_all x1, blocking collectives, exchanged(): return lax.all_to_all(pieces, axes, split_axis=0, concat_axis=0, tiled=True)  22.8 us
    all_to_all x3, waiting for transfers between devices, gathered(): return lax.all_to_all(copies, axes, split_axis=0, concat_axis=0, tiled=True)  17.1 us
    pallas_call x1, Pallas kernels, coarse_attention(): pl.pallas_call(attention_kernel, out_shape=jax.ShapeDtypeStruct((rows, HE...  15.4 us
    all_to_all x3, starting transfers between devices, gathered(): return lax.all_to_all(copies, axes, split_axis=0, concat_axis=0, tiled=True)  14.3 us
    ppermute x2, waiting for transfers between devices, from_behind(): return lax.ppermute(array, axis, pairs)  12.3 us
    unnamed x51, local copies, waits for them, and re-layouts  11.4 us
  transfers between devices with their start and end apart: 33, of which 17 were waited for; matrix products, arithmetic and copies ran while one was open for 11% of the time, Pallas kernels for 11%

commit v1 on v0

--- a/solution.py
+++ b/solution.py
@@ -96,6 +96,10 @@
         state_ref[...] = state
         runs = state.astype(f32).reshape(rows // SHORT, SHORT, state.shape[1])
         pooled_ref[...] = (jnp.sum(runs, axis=1) * (1.0 / SHORT)).astype(bf16)
+
+
+def in_hbm(array):
+    return pltpu.with_memory_space_constraint(array, pltpu.MemorySpace.HBM)
 
 
 def fine_layer(tokens, normed, before, fine_query, fine_keyval, fine_out):
@@ -121,7 +125,7 @@
         out_specs=(whole, pl.BlockSpec((rows // SHORT, width), lambda i: (0, 0))),
         scratch_shapes=[pltpu.VMEM((rows, width), f32)],
         compiler_params=pltpu.CompilerParams(vmem_limit_bytes=40 << 20),
-    )(first, tokens, normed, before, fine_query, fine_keyval, fine_keyval, fine_out)
+    )(first, tokens, normed, before, *[in_hbm(w) for w in (fine_query, fine_keyval, fine_keyval, fine_out)])
 
 
 def attention_kernel(place_ref, q_ref, inverse_ref, *refs):
@@ -137,7 +141,7 @@
 
     ahead = position(row) - position(col)
 
-    def update(kt, state):
+    def update(kt, state, masked):
         peak, total, acc = state
         rows = pl.ds(pl.multiple_of(kt * tile, tile), tile)
         inverses, scores = [], []
@@ -146,8 +150,8 @@
                 q, chunk[rows, :HEAD], (((1,), (1,)), ((), ())), preferred_element_type=f32
             )
             inverses.append(inverse_ref[pl.ds(place_ref[len(chunks) + j], 1), rows])
-            bound = jnp.where(kt < step, -(1 << 24), place_ref[j])
-            scores.append(jnp.where(ahead >= bound, s * inverses[j], big_negative))
+            s = s * inverses[j]
+            scores.append(jnp.where(ahead >= place_ref[j], s, big_negative) if masked else s)
         top = functools.reduce(jnp.maximum, scores)
         new_peak = jnp.maximum(peak, jnp.max(top, axis=-1, keepdims=True))
         fade = jnp.exp2(peak - new_peak)
@@ -165,7 +169,8 @@
         jnp.zeros((tile, 1), f32),
         jnp.zeros((tile, HEAD), f32),
     )
-    _, total, acc = lax.fori_loop(0, step + 1, update, state)
+    state = lax.fori_loop(0, step, lambda kt, st: update(kt, st, False), state)
+    _, total, acc = update(step, state, True)
     out_ref[...] = (acc / total).astype(bf16)
 
 
@@ -239,6 +244,68 @@
     )(where, down, up, pack)
 
 
+def project_kernel(
+    where_ref, own_ref, above_ref, top_ref, bottom_ref, below_ref, near_ref, far_ref,
+    kv_ref, q_ref, squares_ref, weight_ref,
+):
+    core, slot_at, y = where_ref[0], where_ref[1], where_ref[2]
+    half = weight_ref.shape[0] // 2
+    for side, piece_ref in ((core, near_ref), (1 - core, far_ref)):
+        for x in range(4):
+            rows = pl.ds(pl.multiple_of(side * half + x * 128, 128), 128)
+            for j in range(4):
+                lanes = slice(j * 128, (j + 1) * 128)
+                weight_ref[rows, lanes] = piece_ref[x, lanes, :]
+    weight = weight_ref[...]
+    ones = jnp.ones((8, 128), f32)
+    opposite = jnp.concatenate([top_ref[...], bottom_ref[...]], 0)
+    lanes = pl.ds(pl.multiple_of(slot_at, 128), 128)
+    opposite_slot = jnp.concatenate([top_ref[:, lanes], bottom_ref[:, lanes]], 0)
+    groups = (
+        (own_ref[...], own_ref[:, lanes]),
+        (above_ref[...], above_ref[:, lanes]),
+        (opposite, opposite_slot),
+        (below_ref[...], below_ref[:, lanes]),
+    )
+    for i, (rows, slot) in enumerate(groups):
+        product = dot(rows, weight)
+        squares = product[:, 3 * HEAD :] * slot.astype(f32)
+        squares_ref[i] = lax.dot_general(
+            ones,
+            squares,
+            (((1,), (1,)), ((), ())),
+            precision=lax.Precision.HIGHEST,
+            preferred_element_type=f32,
+        )
+        kv = product[:, HEAD : 3 * HEAD].astype(bf16)
+        source = (y + i) % 4
+        start = (source // 2) * 512 + (source % 2) * 32
+        for a in range(4):
+            for h in range(2):
+                at = pl.ds(pl.multiple_of(start + (h * 4 + a) * 64, 32), 32)
+                part = slice((a * 2 + h) * 32, (a * 2 + h) * 32 + 32)
+                kv_ref[at, :] = kv[part]
+                q_ref[at, :] = product[part, :HEAD]
+
+
+def projected(where, rows, near, far):
+    width = rows[0].shape[1]
+    n = 4 * rows[0].shape[0]
+    whole = pl.BlockSpec(memory_space=pltpu.VMEM)
+    return pl.pallas_call(
+        project_kernel,
+        out_shape=(
+            jax.ShapeDtypeStruct((n, 2 * HEAD), bf16),
+            jax.ShapeDtypeStruct((n, HEAD), f32),
+            jax.ShapeDtypeStruct((4, 8, n // 4), f32),
+        ),
+        in_specs=[pl.BlockSpec(memory_space=pltpu.SMEM)] + [whole] * 7,
+        out_specs=(whole, whole, whole),
+        scratch_shapes=[pltpu.VMEM((width, 4 * HEAD), bf16)],
+        compiler_params=pltpu.CompilerParams(vmem_limit_bytes=40 << 20),
+    )(where, *rows, near, far)
+
+
 def body(
     tokens,
     fine_gain,
@@ -282,8 +349,6 @@
         around = jnp.stack(around + around[:3])
         z_rows = lax.dynamic_slice_in_dim(around, (4 - z % 4) % 4, 4, 0).reshape(-1, width)
         y_rows = around_four(z_rows, ("yh", "yl"))
-        all_rows = jnp.concatenate(y_rows, 0)
-        n = all_rows.shape[0]
 
     with jax.named_scope("weights"):
         gain = lax.dynamic_slice(coarse_gain, (t * cols,), (cols,))[:, None]
@@ -302,18 +367,18 @@
         piece = (total[0] + rotated(total[1].astype(bf16), "yl", 1).astype(f32)).astype(bf16)
         near_half = gathered(gate(piece, tuple(y_rows)), ("x",))
         far_half = rotated(near_half, "c", 1)
-        summed = jnp.stack(
-            [jnp.where(c == 0, near_half, far_half), jnp.where(c == 0, far_half, near_half)]
-        ).reshape(8, *piece.shape)
-        proj = summed[:, : 4 * HEAD].reshape(8, 4, HEAD, 128)
-        proj = jnp.swapaxes(proj, 1, 2).reshape(width, 4 * HEAD)
-        second = jnp.swapaxes(summed[:, 4 * HEAD :], 0, 1).reshape(-1, width)
+        lifts = near_half[:, 4 * HEAD :], far_half[:, 4 * HEAD :]
+        summed = jnp.concatenate(
+            [jnp.where(c == 0, lifts[0], lifts[1]), jnp.where(c == 0, lifts[1], lifts[0])], 0
+        )
+        second = jnp.swapaxes(summed, 0, 1).reshape(-1, width)
         below, above = rotated(second, ("yh", "yl"), 1), rotated(second, ("yh", "yl"), 3)
         seconds = [second, below, rotated(below, ("yh", "yl"), 1), above]
 
     with jax.named_scope("project"):
-        half = 3 * HEAD
-        qkv = dot(all_rows, proj)
+        where = jnp.stack([c, 128 * z, y]).astype(jnp.int32)
+        kv, q, squares = projected(where, y_rows, near_half, far_half)
+        n = kv.shape[0]
 
         def in_order(parts):
             twice = jnp.concatenate([parts, parts[:3]], 0)
@@ -324,14 +389,12 @@
             parts = parts.reshape(2, 2, 4, 2, run_count, -1)
             return jnp.transpose(parts, (0, 3, 2, 1, 4, 5)).reshape(n, -1)
 
-        kv = by_row(qkv[:, HEAD:half].astype(bf16))
         near = [kv] + [rotated(kv, "x", by) for by in (3, 2, 1)]
-        slot = lax.dynamic_slice(all_rows, (0, 128 * z), (n, 128))
-        squares = jnp.sum(qkv[:, half:] * slot.astype(f32), axis=-1)
+        squares = squares[:, 0].reshape(n)
         squares = jnp.sum(gathered(squares[None], ("z",)), axis=(0, 1))
         inverse = by_row(lax.rsqrt(jnp.maximum(squares, 0.0) / wide + epsilon))
         factor = math.log2(math.e) / math.sqrt(HEAD)
-        q = (by_row(qkv[:, :HEAD]) * (inverse * factor)).astype(bf16)
+        q = (q * (inverse * factor)).astype(bf16)
         every_inverse = gathered(inverse.reshape(1, n), ("x", "c")).reshape(8, n)
 
     with jax.named_scope("attention"):

time: 228 us -> 228 us (level)
  blocking collectives: 22.8 us -> 37.5 us
  local copies, waits for them, and re-layouts: 28 us -> 18.2 us
  matrix products: 7.22 us -> 3.1 us
  Pallas kernels: 26.1 us -> 30.2 us
  other arithmetic: 12.2 us -> 9.46 us
  starting transfers between devices: 54.8 us -> 52.2 us
    all_to_all x0 -> x1, blocking collectives: none -> 14.4 us  [gathered(): return lax.all_to_all(copies, axes, split_axis=0, concat_axis=0, tiled=True)]
    all_to_all x3 -> x2, waiting for transfers between devices: 17.1 us -> 9.73 us  [gathered(): return lax.all_to_all(copies, axes, split_axis=0, concat_axis=0, tiled=True)]
    ppermute x27, waiting for transfers between devices: 45.1 us -> 50.5 us  [rotated(): lax.ppermute(array, axis, [(i, (i + by) % size) for i in range(size)])]
    all_to_all x3 -> x2, starting transfers between devices: 14.3 us -> 9.54 us  [gathered(): return lax.all_to_all(copies, axes, split_axis=0, concat_axis=0, tiled=True)]
    unnamed x51 -> x49, local copies, waits for them, and re-layouts: 11.4 us -> 6.93 us
    pallas_call x0 -> x1, Pallas kernels: none -> 4.35 us  [projected(): pl.pallas_call(project_kernel, out_shape=(jax.ShapeDtypeStruct((n, 2 * HE...]
    dot_general x5 -> x4, matrix products: 7.22 us -> 3.1 us  [dot(): return jnp.dot(a, b, preferred_element_type=f32)]
  transfers between devices with their start and end apart: 33 -> 32, of which waited for: 17 -> 15; matrix products, arithmetic and copies ran while one was open for 11% -> 9% of each run, Pallas kernels for 11% -> 11%
where the time goes in v1:
time: 228 us; the launch traced here: 226 us
  waiting for transfers between devices  74.3 us (33%)
  starting transfers between devices  52.2 us (23%)
  blocking collectives  37.5 us (16%)
  Pallas kernels  30.2 us (13%)
  local copies, waits for them, and re-layouts  18.2 us (8%)
  other arithmetic  9.46 us (4%)
  matrix products  3.1 us (1%)
    ppermute x27, waiting for transfers between devices, rotated(): lax.ppermute(array, axis, [(i, (i + by) % size) for i in range(size)])  50.5 us
    ppermute x27, starting transfers between devices, rotated(): lax.ppermute(array, axis, [(i, (i + by) % size) for i in range(size)])  34.1 us
    all_to_all x1, blocking collectives, exchanged(): return lax.all_to_all(pieces, axes, split_axis=0, concat_axis=0, tiled=True)  23.1 us
    pallas_call x1, Pallas kernels, coarse_attention(): pl.pallas_call(attention_kernel, out_shape=jax.ShapeDtypeStruct((rows, HE...  14.7 us
    all_to_all x1, blocking collectives, gathered(): return lax.all_to_all(copies, axes, split_axis=0, concat_axis=0, tiled=True)  14.4 us
    ppermute x2, waiting for transfers between devices, from_behind(): return lax.ppermute(array, axis, pairs)  14.1 us
    all_to_all x2, waiting for transfers between devices, gathered(): return lax.all_to_all(copies, axes, split_axis=0, concat_axis=0, tiled=True)  9.73 us
    all_to_all x2, starting transfers between devices, gathered(): return lax.all_to_all(copies, axes, split_axis=0, concat_axis=0, tiled=True)  9.54 us
  transfers between devices with their start and end apart: 32, of which 15 were waited for; matrix products, arithmetic and copies ran while one was open for 9% of the time, Pallas kernels for 11%

profile of v1, /device:TPU:16, one launch (start us, length us, event | category | flops | bytes accessed | tf_op | source)
XLA Modules:
  0.0 225.8 jit_solution(10639720266571692588)
XLA Ops:
  0.0 1.4 fusion.2
  1.4 1.3 fusion.4.normed_ref
  2.7 1.9 collective-permute-start
  4.6 1.2 fusion.35
  5.8 1.1 copy_bitcast_fusion.1
  6.9 0.8 pad_maximum_fusion
  7.7 4.7 %collective-permute-start.9 = (bf16[1024,256]{1,0:T(8,128)(2,1)}, bf16[1024,256]{1,0:T(8,128)(2,1)}, u32[]{:S(2)}, u32[]{:S(2)}) collective-permute-start(bf16[1024,256]{1,0:T(8,128)(2,1)} %pad_maximum_fusion), channel_id=1, source_target_pairs={{0,0},{16,1},{32,2},{48,3},{64,4},{80,5},{96,6},{112,7},{128,8},{1... | collective-permute-start | bytes 1572872 | tf_op jit(solution)/shard_map/weights/ppermute | solution.py:338
  12.5 0.8 dynamic_slice.43
  13.3 6.9 %collective-permute-done.before_ref = bf16[256,1024]{1,0:T(8,128)(2,1)} collective-permute-done((bf16[256,1024]{1,0:T(8,128)(2,1)S(1)}, bf16[256,1024]{1,0:T(8,128)(2,1)}, u32[]{:S(2)}, u32[]{:S(2)}) %collective-permute-start) | collective-permute-done | bytes 524320 | tf_op jit(solution)/shard_map/ppermute | solution.py:28
  20.1 9.5 %shard_map.109 = (bf16[256,1024]{1,0:T(8,128)(2,1)S(1)}, bf16[32,1024]{1,0:T(8,128)(2,1)S(1)}) custom-call(s32[1]{0:T(128)} %bitcast.first_ref, bf16[256,1024]{1,0:T(8,128)(2,1)S(1)} %copy-done.1, bf16[256,1024]{1,0:T(8,128)(2,1)S(1)} %fusion.4.normed_ref, bf16[256,1024]{1,0:T(8,128)(2,1)} %collective-permute-done.before_ref, bf16[1024,1024]{1,0:T(8,128)(2,1)} %query_ref.1, ...), custom_call_target="tpu_custom_call" | custom-call | tf_op jit(solution)/shard_map/pallas_call | solution.py:111
  29.6 0.8 copy-done.9
  30.4 4.6 %collective-permute-start.1 = (bf16[32,1024]{1,0:T(8,128)(2,1)S(1)}, bf16[32,1024]{1,0:T(8,128)(2,1)S(1)}, u32[]{:S(2)}, u32[]{:S(2)}) collective-permute-start(bf16[32,1024]{1,0:T(8,128)(2,1)S(1)} %get-tuple-element.18), channel_id=1, source_target_pairs={{0,64},{16,80},{32,96},{48,112},{64,0},{80,16},{96,32},{112,48},{1... | collective-permute-start | bytes 196616 | tf_op jit(solution)/shard_map/gather_rows/ppermute | solution.py:33
  35.1 3.7 %collective-permute-done.1 = bf16[32,1024]{1,0:T(8,128)(2,1)S(1)} collective-permute-done((bf16[32,1024]{1,0:T(8,128)(2,1)S(1)}, bf16[32,1024]{1,0:T(8,128)(2,1)S(1)}, u32[]{:S(2)}, u32[]{:S(2)}) %collective-permute-start.1) | collective-permute-done | bytes 65568 | tf_op jit(solution)/shard_map/gather_rows/ppermute | solution.py:33
  38.8 8.0 %collective-permute-start.2 = (bf16[2,32,1024]{2,1,0:T(8,128)(2,1)S(1)}, bf16[2,32,1024]{2,1,0:T(8,128)(2,1)S(1)}, u32[]{:S(2)}, u32[]{:S(2)}) collective-permute-start(bf16[2,32,1024]{2,1,0:T(8,128)(2,1)S(1)} %maximum_select_fusion.1), channel_id=1, source_target_pairs={{0,112},{16,0},{32,16},{48,32},{64,48},{80,64},{96,80},{112,96},{1... | collective-permute-start | bytes 393224 | tf_op jit(solution)/shard_map/gather_rows/ppermute | solution.py:33
  46.8 1.5 collective-permute-start.4
  48.3 1.2 multiply_convert_fusion.pack_ref
  49.6 3.7 %collective-permute-done.2 = bf16[2,32,1024]{2,1,0:T(8,128)(2,1)S(1)} collective-permute-done((bf16[2,32,1024]{2,1,0:T(8,128)(2,1)S(1)}, bf16[2,32,1024]{2,1,0:T(8,128)(2,1)S(1)}, u32[]{:S(2)}, u32[]{:S(2)}) %collective-permute-start.2) | collective-permute-done | bytes 131104 | tf_op jit(solution)/shard_map/gather_rows/ppermute | solution.py:33
  53.3 8.2 %collective-permute-done.3 = bf16[2,32,1024]{2,1,0:T(8,128)(2,1)S(1)} collective-permute-done((bf16[2,32,1024]{2,1,0:T(8,128)(2,1)S(1)}, bf16[2,32,1024]{2,1,0:T(8,128)(2,1)S(1)}, u32[]{:S(2)}, u32[]{:S(2)}) %collective-permute-start.3) | collective-permute-done | bytes 131104 | tf_op jit(solution)/shard_map/gather_rows/ppermute | solution.py:33
  61.7 1.7 weights.1
  63.4 3.1 %collective-permute-done.10 = bf16[4,2,672,128]{3,2,1,0:T(8,128)(2,1)S(1)} collective-permute-done((bf16[4,2,672,128]{3,2,1,0:T(8,128)(2,1)S(1)}, bf16[4,2,672,128]{3,2,1,0:T(8,128)(2,1)S(1)}, u32[]{:S(2)}, u32[]{:S(2)}) %collective-permute-start.10) | collective-permute-done | bytes 1376288 | tf_op jit(solution)/shard_map/weights/ppermute | solution.py:33
  66.8 1.3 collective-permute-start.13
  68.1 2.0 collective-permute-start.11
  70.2 1.4 collective-permute-start.5
  71.6 1.0 collective-permute-start.7
  72.6 6.7 %collective-permute-done.13 = bf16[2,672,128]{2,1,0:T(8,128)(2,1)S(1)} collective-permute-done((bf16[2,672,128]{2,1,0:T(8,128)(2,1)S(1)}, bf16[2,672,128]{2,1,0:T(8,128)(2,1)S(1)}, u32[]{:S(2)}, u32[]{:S(2)}) %collective-permute-start.13) | collective-permute-done | bytes 344096 | tf_op jit(solution)/shard_map/weights/ppermute | solution.py:33
  79.9 6.0 %collective-permute-done.11 = bf16[2,672,128]{2,1,0:T(8,128)(2,1)S(1)} collective-permute-done((bf16[2,672,128]{2,1,0:T(8,128)(2,1)S(1)}, bf16[2,672,128]{2,1,0:T(8,128)(2,1)S(1)}, u32[]{:S(2)}, u32[]{:S(2)}) %collective-permute-start.11) | collective-permute-done | bytes 344096 | tf_op jit(solution)/shard_map/weights/ppermute | solution.py:33
  86.1 1.6 collective-permute-start.14
  87.9 2.1 collective-permute-start.8
  90.0 3.5 %collective-permute-done.14 = bf16[672,128]{1,0:T(8,128)(2,1)S(1)} collective-permute-done((bf16[672,128]{1,0:T(8,128)(2,1)S(1)}, bf16[672,128]{1,0:T(8,128)(2,1)S(1)}, u32[]{:S(2)}, u32[]{:S(2)}) %collective-permute-start.14) | collective-permute-done | bytes 172064 | tf_op jit(solution)/shard_map/weights/ppermute | solution.py:33
  93.5 4.6 %collective-permute-done.6.top_ref = bf16[128,1024]{1,0:T(8,128)(2,1)S(1)} collective-permute-done((bf16[128,1024]{1,0:T(8,128)(2,1)S(1)}, bf16[128,1024]{1,0:T(8,128)(2,1)S(1)}, u32[]{:S(2)}, u32[]{:S(2)}) %collective-permute-start.6) | collective-permute-done | bytes 262176 | tf_op jit(solution)/shard_map/gather_rows/ppermute | solution.py:33
  98.9 14.4 %all_to_all.20.near_ref = bf16[4,672,128]{2,1,0:T(8,128)(2,1)S(1)} all-to-all(bf16[4,672,128]{2,1,0:T(8,128)(2,1)S(1)} %broadcast_in_dim.22), channel_id=1, replica_groups=mesh['yh'=2,'z'=8,'x'=4,'yl'=2,'c'=2] {'x'}, dimensions={0} | all-to-all | bytes 1376256 | tf_op jit(solution)/shard_map/weights/all_to_all | solution.py:45
  113.6 0.9 reshape.171
  114.5 1.9 copy.55
  116.4 1.2 reshape.172
  119.9 1.0 copy-done.3
  121.0 1.0 copy-done.5
  122.0 0.9 copy-done.12
  122.9 0.9 copy-done.14
  123.9 4.4 %project.1 = (bf16[1024,256]{1,0:T(8,128)(2,1)}, f32[1024,128]{1,0:T(8,128)S(1)}, f32[4,8,256]{2,1,0:T(8,128)S(1)}) custom-call(s32[3]{0:T(128)S(1)} %pad_add_fusion.where_ref, bf16[256,1024]{1,0:T(8,128)(2,1)S(1)} %bitcast.118, bf16[256,1024]{1,0:T(8,128)(2,1)S(1)} %copy-done.3, bf16[128,1024]{1,0:T(8,128)(2,1)S(1)} %copy-done.12, ...), custom_call_target="tpu_custom_call" | custom-call | tf_op jit(solution)/shard_map/project/pallas_call | solution.py:295
  128.3 0.8 copy-done.6
  129.4 1.2 collective-permute-start.19
  130.6 0.9 collective-permute-start.21
  131.4 1.1 collective-permute-start.23
  133.1 6.0 %all-to-all-start.1 = ((f32[8,1,1024]{2,1,0:T(1,128)}), f32[8,1,1024]{2,1,0:T(1,128)}, u32[]{:S(2)}, u32[]{:S(2)}) async-start(f32[8,1,1024]{2,1,0:T(1,128)} %broadcast_in_dim.23), calls=%async_computation.1 | async-start | bytes 65536 | tf_op jit(solution)/shard_map/project/all_to_all | solution.py:45
  139.1 0.9 broadcast_select_fusion.1
  141.4 5.8 %all-to-all-done.1 = f32[8,1,1024]{2,1,0:T(1,128)} async-done(((f32[8,1,1024]{2,1,0:T(1,128)}), f32[8,1,1024]{2,1,0:T(1,128)}, u32[]{:S(2)}, u32[]{:S(2)}) %all-to-all-start.1) | async-done | bytes 32800 | tf_op jit(solution)/shard_map/project/all_to_all | solution.py:45
  147.3 0.8 reduce_sum.28
  148.2 8.8 %collective-permute-done.21.refs_4_ = bf16[1024,256]{1,0:T(8,128)(2,1)} collective-permute-done((bf16[1024,256]{1,0:T(8,128)(2,1)}, bf16[1024,256]{1,0:T(8,128)(2,1)}, u32[]{:S(2)}, u32[]{:S(2)}) %collective-permute-start.21) | collective-permute-done | bytes 524320 | tf_op jit(solution)/shard_map/project/ppermute | solution.py:33
  157.7 0.9 collective-permute-start.16
  159.2 3.5 %all-to-all-start.2 = ((f32[8,1,1024]{2,1,0:T(1,128)}), f32[8,1,1024]{2,1,0:T(1,128)S(1)}, u32[]{:S(2)}, u32[]{:S(2)}) async-start(f32[8,1,1024]{2,1,0:T(1,128)} %broadcast_in_dim.24), calls=%async_computation.2 | async-start | bytes 65536 | tf_op jit(solution)/shard_map/project/all_to_all | solution.py:45
  162.7 1.2 multiply_convert_fusion.1.q_ref
  164.0 3.9 %all-to-all-done.2 = f32[8,1,1024]{2,1,0:T(1,128)S(1)} async-done(((f32[8,1,1024]{2,1,0:T(1,128)}), f32[8,1,1024]{2,1,0:T(1,128)S(1)}, u32[]{:S(2)}, u32[]{:S(2)}) %all-to-all-start.2) | async-done | bytes 32800 | tf_op jit(solution)/shard_map/project/all_to_all | solution.py:45
  167.9 1.1 collective-permute-start.27
  169.0 14.7 %attention.1 = bf16[1024,128]{1,0:T(8,128)(2,1)S(1)} custom-call(s32[16]{0:T(128)S(1)} %stack.134.place_ref, bf16[1024,128]{1,0:T(8,128)(2,1)S(1)} %multiply_convert_fusion.1.q_ref, f32[8,1024]{1,0:T(8,128)S(1)} %bitcast.123, bf16[1024,256]{1,0:T(8,128)(2,1)} %get-tuple-element.28.refs_0_, bf16[1024,256]{1,0:T(8,128)(2,1)S(1)} %collective-permute-done.18.refs_1_, ...), custom_call_target="tpu_custom_call" | custom-call | tf_op jit(solution)/shard_map/attention/pallas_call | solution.py:180
  183.8 1.1 collective-permute-start.28
  184.9 1.0 collective-permute-start.25
  185.9 1.7 collective-permute-start.26
  187.8 1.7 collective-permute-done.25
  189.5 1.3 convolution_add_fusion.1
  190.8 1.3 fusion.24
  192.4 23.1 %all_to_all.21 = bf16[8,32,1024]{2,1,0:T(8,128)(2,1)S(1)} all-to-all(bf16[8,32,1024]{2,1,0:T(8,128)(2,1)S(1)} %bitcast.124), channel_id=1, replica_groups=mesh['yh'=2,'z'=8,'x'=4,'yl'=2,'c'=2] {'z'}, dimensions={0} | all-to-all | bytes 1048576 | tf_op jit(solution)/shard_map/lift/all_to_all | solution.py:49
  215.6 1.9 collective-permute-start.29
  217.6 7.2 %collective-permute-done.29 = f32[1,1024]{1,0:T(1,128)S(1)} collective-permute-done((f32[1,1024]{1,0:T(1,128)S(1)}, f32[1,1024]{1,0:T(1,128)S(1)}, u32[]{:S(2)}, u32[]{:S(2)}) %collective-permute-start.29) | collective-permute-done | bytes 4128 | tf_op jit(solution)/shard_map/lift/ppermute | solution.py:28
  224.8 0.9 fusion.5
  (115 shorter events, 9.4 us)
Async XLA Ops:
  0.0 5.8 %copy-start = (bf16[256,4096]{1,0:T(8,128)(2,1)S(1)}, bf16[256,4096]{1,0:T(8,128)(2,1)}, u32[]{:S(2)}) copy-start(bf16[256,4096]{1,0:T(8,128)(2,1)} %param.20) | copy-start | bytes 6291460
  0.0 4.6 %copy-start.17 = (bf16[256,2,256]{2,1,0:T(2,128)(2,1)S(1)}, bf16[256,2,256]{2,1,0:T(2,128)(2,1)}, u32[]{:S(2)}) copy-start(bf16[256,2,256]{2,1,0:T(2,128)(2,1)} %param.19) | copy-start | bytes 786436
  1.4 5.5 %copy-start.21 = (bf16[256,256]{1,0:T(8,128)(2,1)S(1)}, bf16[256,256]{1,0:T(8,128)(2,1)}, u32[]{:S(2)}) copy-start(bf16[256,256]{1,0:T(8,128)(2,1)} %param.18) | copy-start | bytes 393220
  2.7 17.5 %collective-permute-start = (bf16[256,1024]{1,0:T(8,128)(2,1)S(1)}, bf16[256,1024]{1,0:T(8,128)(2,1)}, u32[]{:S(2)}, u32[]{:S(2)}) collective-permute-start(bf16[256,1024]{1,0:T(8,128)(2,1)S(1)} %fusion.4.normed_ref), channel_id=1, source_target_pairs={{0,1},{1,2},{2,3},{3,4},{4,5},{5,6},{6,7},{7,8},{8,9},{9,10},{10,1... | collective-permute-start | bytes 1572872 | tf_op jit(solution)/shard_map/ppermute | solution.py:28
  4.6 15.5 %copy-start.1 = (bf16[256,1024]{1,0:T(8,128)(2,1)S(1)}, bf16[256,1024]{1,0:T(8,128)(2,1)}, u32[]{:S(2)}) copy-start(bf16[256,1024]{1,0:T(8,128)(2,1)} %tokens_ref.1) | copy-start | bytes 1572868
  7.7 40.6 %collective-permute-start.9 = (bf16[1024,256]{1,0:T(8,128)(2,1)}, bf16[1024,256]{1,0:T(8,128)(2,1)}, u32[]{:S(2)}, u32[]{:S(2)}) collective-permute-start(bf16[1024,256]{1,0:T(8,128)(2,1)} %pad_maximum_fusion), channel_id=1, source_target_pairs={{0,0},{16,1},{32,2},{48,3},{64,4},{80,5},{96,6},{112,7},{128,8},{1... | collective-permute-start | bytes 1572872 | tf_op jit(solution)/shard_map/weights/ppermute | solution.py:338
  29.6 0.8 copy-start.9
  30.4 8.3 %collective-permute-start.1 = (bf16[32,1024]{1,0:T(8,128)(2,1)S(1)}, bf16[32,1024]{1,0:T(8,128)(2,1)S(1)}, u32[]{:S(2)}, u32[]{:S(2)}) collective-permute-start(bf16[32,1024]{1,0:T(8,128)(2,1)S(1)} %get-tuple-element.18), channel_id=1, source_target_pairs={{0,64},{16,80},{32,96},{48,112},{64,0},{80,16},{96,32},{112,48},{1... | collective-permute-start | bytes 196616 | tf_op jit(solution)/shard_map/gather_rows/ppermute | solution.py:33
  38.8 14.5 %collective-permute-start.2 = (bf16[2,32,1024]{2,1,0:T(8,128)(2,1)S(1)}, bf16[2,32,1024]{2,1,0:T(8,128)(2,1)S(1)}, u32[]{:S(2)}, u32[]{:S(2)}) collective-permute-start(bf16[2,32,1024]{2,1,0:T(8,128)(2,1)S(1)} %maximum_select_fusion.1), channel_id=1, source_target_pairs={{0,112},{16,0},{32,16},{48,32},{64,48},{80,64},{96,80},{112,96},{1... | collective-permute-start | bytes 393224 | tf_op jit(solution)/shard_map/gather_rows/ppermute | solution.py:33
  46.8 14.7 %collective-permute-start.3 = (bf16[2,32,1024]{2,1,0:T(8,128)(2,1)S(1)}, bf16[2,32,1024]{2,1,0:T(8,128)(2,1)S(1)}, u32[]{:S(2)}, u32[]{:S(2)}) collective-permute-start(bf16[2,32,1024]{2,1,0:T(8,128)(2,1)S(1)} %maximum_select_fusion.1), channel_id=1, source_target_pairs={{0,96},{16,112},{32,0},{48,16},{64,32},{80,48},{96,64},{112,80},{1... | collective-permute-start | bytes 393224 | tf_op jit(solution)/shard_map/gather_rows/ppermute | solution.py:33
  46.8 14.7 %collective-permute-start.4 = (bf16[2,32,1024]{2,1,0:T(8,128)(2,1)S(1)}, bf16[2,32,1024]{2,1,0:T(8,128)(2,1)S(1)}, u32[]{:S(2)}, u32[]{:S(2)}) collective-permute-start(bf16[2,32,1024]{2,1,0:T(8,128)(2,1)S(1)} %maximum_select_fusion.1), channel_id=1, source_target_pairs={{0,16},{16,32},{32,48},{48,64},{64,80},{80,96},{96,112},{112,0},{1... | collective-permute-start | bytes 393224 | tf_op jit(solution)/shard_map/gather_rows/ppermute | solution.py:33
  49.6 12.0 %copy-start.7 = (bf16[1024,256]{1,0:T(8,128)(2,1)S(1)}, bf16[1024,256]{1,0:T(8,128)(2,1)}, u32[]{:S(2)}) copy-start(bf16[1024,256]{1,0:T(8,128)(2,1)} %down_ref.1) | copy-start | bytes 1572868
  49.6 12.0 %copy-start.8 = (bf16[256,1024]{1,0:T(8,128)(2,1)S(1)}, bf16[256,1024]{1,0:T(8,128)(2,1)}, u32[]{:S(2)}) copy-start(bf16[256,1024]{1,0:T(8,128)(2,1)} %up_ref.1) | copy-start | bytes 1572868
  63.3 3.2 %collective-permute-start.10 = (bf16[4,2,672,128]{3,2,1,0:T(8,128)(2,1)S(1)}, bf16[4,2,672,128]{3,2,1,0:T(8,128)(2,1)S(1)}, u32[]{:S(2)}, u32[]{:S(2)}) collective-permute-start(bf16[4,2,672,128]{3,2,1,0:T(8,128)(2,1)S(1)} %get-tuple-element.23), channel_id=1, source_target_pairs={{0,1},{1,0},{2,3},{3,2},{4,5},{5,4},{6,7},{7,6},{8,9},{9,8},{10,11... | collective-permute-start | bytes 4128776 | tf_op jit(solution)/shard_map/weights/ppermute | solution.py:33
  66.8 12.5 %collective-permute-start.13 = (bf16[2,672,128]{2,1,0:T(8,128)(2,1)S(1)}, bf16[2,672,128]{2,1,0:T(8,128)(2,1)S(1)}, u32[]{:S(2)}, u32[]{:S(2)}) collective-permute-start(bf16[2,672,128]{2,1,0:T(8,128)(2,1)S(1)} %get-tuple-element.30), channel_id=1, source_target_pairs={{0,8},{4,12},{8,0},{12,4},{1,9},{5,13},{9,1},{13,5},{2,10},{6,14},... | collective-permute-start | bytes 1032200 | tf_op jit(solution)/shard_map/weights/ppermute | solution.py:33
  68.1 11.8 %collective-permute-start.12 = (bf16[2,672,128]{2,1,0:T(8,128)(2,1)S(1)}, bf16[2,672,128]{2,1,0:T(8,128)(2,1)S(1)}, u32[]{:S(2)}, u32[]{:S(2)}) collective-permute-start(bf16[2,672,128]{2,1,0:T(8,128)(2,1)S(1)} %get-tuple-element.31), channel_id=1, source_target_pairs={{0,12},{4,0},{8,4},{12,8},{1,13},{5,1},{9,5},{13,9},{2,14},{6,2},{... | collective-permute-start | bytes 1032200 | tf_op jit(solution)/shard_map/weights/ppermute | solution.py:33
  68.1 17.8 %collective-permute-start.11 = (bf16[2,672,128]{2,1,0:T(8,128)(2,1)S(1)}, bf16[2,672,128]{2,1,0:T(8,128)(2,1)S(1)}, u32[]{:S(2)}, u32[]{:S(2)}) collective-permute-start(bf16[2,672,128]{2,1,0:T(8,128)(2,1)S(1)} %get-tuple-element.29), channel_id=1, source_target_pairs={{0,4},{4,8},{8,12},{12,0},{1,5},{5,9},{9,13},{13,1},{2,6},{6,10},{... | collective-permute-start | bytes 1032200 | tf_op jit(solution)/shard_map/weights/ppermute | solution.py:33
  70.2 17.6 %collective-permute-start.5 = (bf16[256,1024]{1,0:T(8,128)(2,1)S(1)}, bf16[256,1024]{1,0:T(8,128)(2,1)S(1)}, u32[]{:S(2)}, u32[]{:S(2)}) collective-permute-start(bf16[256,1024]{1,0:T(8,128)(2,1)S(1)} %bitcast.115), channel_id=1, source_target_pairs={{0,130},{2,0},{128,2},{130,128},{1,131},{3,1},{129,3},{131,129},{4... | collective-permute-start | bytes 1572872 | tf_op jit(solution)/shard_map/gather_rows/ppermute | solution.py:33
  71.6 16.3 %collective-permute-start.7 = (bf16[256,1024]{1,0:T(8,128)(2,1)S(1)}, bf16[256,1024]{1,0:T(8,128)(2,1)S(1)}, u32[]{:S(2)}, u32[]{:S(2)}) collective-permute-start(bf16[256,1024]{1,0:T(8,128)(2,1)S(1)} %bitcast.116), channel_id=1, source_target_pairs={{0,2},{2,128},{128,130},{130,0},{1,3},{3,129},{129,131},{131,1},{4... | collective-permute-start | bytes 1572872 | tf_op jit(solution)/shard_map/gather_rows/ppermute | solution.py:33
  86.1 7.3 %collective-permute-start.14 = (bf16[672,128]{1,0:T(8,128)(2,1)S(1)}, bf16[672,128]{1,0:T(8,128)(2,1)S(1)}, u32[]{:S(2)}, u32[]{:S(2)}) collective-permute-start(bf16[672,128]{1,0:T(8,128)(2,1)S(1)} %fusion.13), channel_id=1, source_target_pairs={{0,2},{2,0},{1,3},{3,1},{4,6},{6,4},{5,7},{7,5},{8,10},{10,8},{9,1... | collective-permute-start | bytes 516104 | tf_op jit(solution)/shard_map/weights/ppermute | solution.py:33
  87.8 10.4 %copy-start.2 = (bf16[256,1024]{1,0:T(8,128)(2,1)}, bf16[256,1024]{1,0:T(8,128)(2,1)S(1)}, u32[]{:S(2)}) copy-start(bf16[256,1024]{1,0:T(8,128)(2,1)S(1)} %collective-permute-done.5.above_ref) | copy-start | bytes 1572868
  87.8 10.4 %collective-permute-start.6 = (bf16[128,1024]{1,0:T(8,128)(2,1)S(1)}, bf16[128,1024]{1,0:T(8,128)(2,1)S(1)}, u32[]{:S(2)}, u32[]{:S(2)}) collective-permute-start(bf16[128,1024]{1,0:T(8,128)(2,1)S(1)} %slice.87), channel_id=1, source_target_pairs={{0,130},{2,0},{128,2},{130,128},{1,131},{3,1},{129,3},{131,129},{4... | collective-permute-start | bytes 786440 | tf_op jit(solution)/shard_map/gather_rows/ppermute | solution.py:33
  87.9 25.3 %copy-start.4 = (bf16[256,1024]{1,0:T(8,128)(2,1)}, bf16[256,1024]{1,0:T(8,128)(2,1)S(1)}, u32[]{:S(2)}) copy-start(bf16[256,1024]{1,0:T(8,128)(2,1)S(1)} %collective-permute-done.7.below_ref) | copy-start | bytes 1572868
  87.9 10.2 %collective-permute-start.8 = (bf16[128,1024]{1,0:T(8,128)(2,1)S(1)}, bf16[128,1024]{1,0:T(8,128)(2,1)S(1)}, u32[]{:S(2)}, u32[]{:S(2)}) collective-permute-start(bf16[128,1024]{1,0:T(8,128)(2,1)S(1)} %slice.88), channel_id=1, source_target_pairs={{0,2},{2,128},{128,130},{130,0},{1,3},{3,129},{129,131},{131,1},{4... | collective-permute-start | bytes 786440 | tf_op jit(solution)/shard_map/gather_rows/ppermute | solution.py:33
  98.1 0.7 copy-start.11
  98.2 15.1 %copy-start.13 = (bf16[128,1024]{1,0:T(8,128)(2,1)}, bf16[128,1024]{1,0:T(8,128)(2,1)S(1)}, u32[]{:S(2)}) copy-start(bf16[128,1024]{1,0:T(8,128)(2,1)S(1)} %collective-permute-done.8.bottom_ref) | copy-start | bytes 786436
  113.2 6.7 %collective-permute-start.15 = (bf16[4,672,128]{2,1,0:T(8,128)(2,1)S(1)}, bf16[4,672,128]{2,1,0:T(8,128)(2,1)}, u32[]{:S(2)}, u32[]{:S(2)}) collective-permute-start(bf16[4,672,128]{2,1,0:T(8,128)(2,1)S(1)} %all_to_all.20.near_ref), channel_id=1, source_target_pairs={{0,1},{1,0},{2,3},{3,2},{4,5},{5,4},{6,7},{7,6},{8,9},{9,8},{10,11... | collective-permute-start | bytes 2064392 | tf_op jit(solution)/shard_map/weights/ppermute | solution.py:33
  119.9 1.0 copy-start.3
  121.0 1.0 copy-start.5
  122.0 0.9 copy-start.12
  122.9 0.9 copy-start.14
  128.2 0.8 copy-start.6
  129.0 39.9 %collective-permute-start.18 = (bf16[1024,256]{1,0:T(8,128)(2,1)}, bf16[1024,256]{1,0:T(8,128)(2,1)S(1)}, u32[]{:S(2)}, u32[]{:S(2)}) collective-permute-start(bf16[1024,256]{1,0:T(8,128)(2,1)} %get-tuple-element.28.refs_0_), channel_id=1, source_target_pairs={{0,1},{1,0},{2,3},{3,2},{4,5},{5,4},{6,7},{7,6},{8,9},{9,8},{10,11... | collective-permute-start | bytes 1572872 | tf_op jit(solution)/shard_map/attention/ppermute | solution.py:33
  129.4 18.8 %collective-permute-start.19 = (bf16[1024,256]{1,0:T(8,128)(2,1)}, bf16[1024,256]{1,0:T(8,128)(2,1)}, u32[]{:S(2)}, u32[]{:S(2)}) collective-permute-start(bf16[1024,256]{1,0:T(8,128)(2,1)} %get-tuple-element.28.refs_0_), channel_id=1, source_target_pairs={{0,12},{4,0},{8,4},{12,8},{1,13},{5,1},{9,5},{13,9},{2,14},{6,2},{... | collective-permute-start | bytes 1572872 | tf_op jit(solution)/shard_map/project/ppermute | solution.py:33
  130.6 26.5 %collective-permute-start.21 = (bf16[1024,256]{1,0:T(8,128)(2,1)}, bf16[1024,256]{1,0:T(8,128)(2,1)}, u32[]{:S(2)}, u32[]{:S(2)}) collective-permute-start(bf16[1024,256]{1,0:T(8,128)(2,1)} %get-tuple-element.28.refs_0_), channel_id=1, source_target_pairs={{0,4},{4,8},{8,12},{12,0},{1,5},{5,9},{9,13},{13,1},{2,6},{6,10},{... | collective-permute-start | bytes 1572872 | tf_op jit(solution)/shard_map/project/ppermute | solution.py:33
  131.4 25.6 %collective-permute-start.23 = (bf16[1024,256]{1,0:T(8,128)(2,1)}, bf16[1024,256]{1,0:T(8,128)(2,1)}, u32[]{:S(2)}, u32[]{:S(2)}) collective-permute-start(bf16[1024,256]{1,0:T(8,128)(2,1)} %get-tuple-element.28.refs_0_), channel_id=1, source_target_pairs={{0,8},{4,12},{8,0},{12,4},{1,9},{5,13},{9,1},{13,5},{2,10},{6,14},... | collective-permute-start | bytes 1572872 | tf_op jit(solution)/shard_map/project/ppermute | solution.py:33
  133.1 14.1 %all-to-all-start.1 = ((f32[8,1,1024]{2,1,0:T(1,128)}), f32[8,1,1024]{2,1,0:T(1,128)}, u32[]{:S(2)}, u32[]{:S(2)}) async-start(f32[8,1,1024]{2,1,0:T(1,128)} %broadcast_in_dim.23), calls=%async_computation.1 | async-start | bytes 65536 | tf_op jit(solution)/shard_map/project/all_to_all | solution.py:45
  140.1 0.7 copy-start.15
  140.8 16.9 %collective-permute-start.17 = (bf16[160,1024]{1,0:T(8,128)(2,1)S(1)}, bf16[160,1024]{1,0:T(8,128)(2,1)}, u32[]{:S(2)}, u32[]{:S(2)}) collective-permute-start(bf16[160,1024]{1,0:T(8,128)(2,1)S(1)} %copy_bitcast_fusion), channel_id=1, source_target_pairs={{0,130},{2,0},{128,2},{130,128},{1,131},{3,1},{129,3},{131,129},{4... | collective-permute-start | bytes 983048 | tf_op jit(solution)/shard_map/weights/ppermute | solution.py:33
  148.2 20.8 %collective-permute-start.20 = (bf16[1024,256]{1,0:T(8,128)(2,1)}, bf16[1024,256]{1,0:T(8,128)(2,1)}, u32[]{:S(2)}, u32[]{:S(2)}) collective-permute-start(bf16[1024,256]{1,0:T(8,128)(2,1)} %collective-permute-done.19.refs_2_), channel_id=1, source_target_pairs={{0,1},{1,0},{2,3},{3,2},{4,5},{5,4},{6,7},{7,6},{8,9},{9,8},{10,11... | collective-permute-start | bytes 1572872 | tf_op jit(solution)/shard_map/attention/ppermute | solution.py:33
  157.0 11.9 %collective-permute-start.22 = (bf16[1024,256]{1,0:T(8,128)(2,1)}, bf16[1024,256]{1,0:T(8,128)(2,1)}, u32[]{:S(2)}, u32[]{:S(2)}) collective-permute-start(bf16[1024,256]{1,0:T(8,128)(2,1)} %collective-permute-done.21.refs_4_), channel_id=1, source_target_pairs={{0,1},{1,0},{2,3},{3,2},{4,5},{5,4},{6,7},{7,6},{8,9},{9,8},{10,11... | collective-permute-start | bytes 1572872 | tf_op jit(solution)/shard_map/attention/ppermute | solution.py:33
  157.0 11.9 %collective-permute-start.24 = (bf16[1024,256]{1,0:T(8,128)(2,1)}, bf16[1024,256]{1,0:T(8,128)(2,1)}, u32[]{:S(2)}, u32[]{:S(2)}) collective-permute-start(bf16[1024,256]{1,0:T(8,128)(2,1)} %collective-permute-done.23.refs_6_), channel_id=1, source_target_pairs={{0,1},{1,0},{2,3},{3,2},{4,5},{5,4},{6,7},{7,6},{8,9},{9,8},{10,11... | collective-permute-start | bytes 1572872 | tf_op jit(solution)/shard_map/attention/ppermute | solution.py:33
  157.7 10.2 %collective-permute-start.16 = (bf16[160,1024]{1,0:T(8,128)(2,1)S(1)}, bf16[160,1024]{1,0:T(8,128)(2,1)}, u32[]{:S(2)}, u32[]{:S(2)}) collective-permute-start(bf16[160,1024]{1,0:T(8,128)(2,1)S(1)} %copy_bitcast_fusion), channel_id=1, source_target_pairs={{0,2},{2,128},{128,130},{130,0},{1,3},{3,129},{129,131},{131,1},{4... | collective-permute-start | bytes 983048 | tf_op jit(solution)/shard_map/weights/ppermute | solution.py:33
  159.2 8.7 %all-to-all-start.2 = ((f32[8,1,1024]{2,1,0:T(1,128)}), f32[8,1,1024]{2,1,0:T(1,128)S(1)}, u32[]{:S(2)}, u32[]{:S(2)}) async-start(f32[8,1,1024]{2,1,0:T(1,128)} %broadcast_in_dim.24), calls=%async_computation.2 | async-start | bytes 65536 | tf_op jit(solution)/shard_map/project/all_to_all | solution.py:45
  167.9 24.2 %collective-permute-start.27 = (bf16[160,1024]{1,0:T(8,128)(2,1)}, bf16[160,1024]{1,0:T(8,128)(2,1)S(1)}, u32[]{:S(2)}, u32[]{:S(2)}) collective-permute-start(bf16[160,1024]{1,0:T(8,128)(2,1)} %collective-permute-done.16), channel_id=1, source_target_pairs={{0,2},{2,128},{128,130},{130,0},{1,3},{3,129},{129,131},{131,1},{4... | collective-permute-start | bytes 983048 | tf_op jit(solution)/shard_map/weights/ppermute | solution.py:33
  169.0 18.6 %copy-start.16 = (bf16[4,160,128]{2,1,0:T(8,128)(2,1)S(1)}, bf16[4,160,128]{2,1,0:T(8,128)(2,1)}, u32[]{:S(2)}) copy-start(bf16[4,160,128]{2,1,0:T(8,128)(2,1)} %copy-done.15) | copy-start | bytes 491524
  169.0 18.5 %copy-start.20 = (bf16[256,32]{1,0:T(8,128)(2,1)S(1)}, bf16[256,32]{1,0:T(8,128)(2,1)}, u32[]{:S(2)}) copy-start(bf16[256,32]{1,0:T(8,128)(2,1)} %copy.56) | copy-start | bytes 49156
  183.7 5.8 %copy-start.19 = (bf16[256,32]{1,0:T(8,128)(2,1)S(1)}, bf16[256,32]{1,0:T(8,128)(2,1)}, u32[]{:S(2)}) copy-start(bf16[256,32]{1,0:T(8,128)(2,1)} %copy.57) | copy-start | bytes 49156
  183.8 7.0 %collective-permute-start.28 = (bf16[256,128]{1,0:T(8,128)(2,1)S(1)}, bf16[256,128]{1,0:T(8,128)(2,1)S(1)}, u32[]{:S(2)}, u32[]{:S(2)}) collective-permute-start(bf16[256,128]{1,0:T(8,128)(2,1)S(1)} %get-tuple-element.35), channel_id=1, source_target_pairs={{0,130},{2,0},{128,2},{130,128},{1,131},{3,1},{129,3},{131,129},{4... | collective-permute-start | bytes 196616 | tf_op jit(solution)/shard_map/lift/ppermute | solution.py:33
  184.9 4.6 %collective-permute-start.25 = (bf16[256,128]{1,0:T(8,128)(2,1)S(1)}, bf16[256,128]{1,0:T(8,128)(2,1)S(1)}, u32[]{:S(2)}, u32[]{:S(2)}) collective-permute-start(bf16[256,128]{1,0:T(8,128)(2,1)S(1)} %get-tuple-element.36), channel_id=1, source_target_pairs={{0,2},{2,128},{128,130},{130,0},{1,3},{3,129},{129,131},{131,1},{4... | collective-permute-start | bytes 196616 | tf_op jit(solution)/shard_map/lift/ppermute | solution.py:33
  185.9 6.2 %collective-permute-start.26 = (bf16[256,128]{1,0:T(8,128)(2,1)S(1)}, bf16[256,128]{1,0:T(8,128)(2,1)S(1)}, u32[]{:S(2)}, u32[]{:S(2)}) collective-permute-start(bf16[256,128]{1,0:T(8,128)(2,1)S(1)} %get-tuple-element.34), channel_id=1, source_target_pairs={{0,128},{2,130},{128,0},{130,2},{1,129},{3,131},{129,1},{131,3},{4... | collective-permute-start | bytes 196616 | tf_op jit(solution)/shard_map/lift/ppermute | solution.py:33
  187.8 3.0 %copy-start.18 = (bf16[256,32]{1,0:T(8,128)(2,1)S(1)}, bf16[256,32]{1,0:T(8,128)(2,1)}, u32[]{:S(2)}) copy-start(bf16[256,32]{1,0:T(8,128)(2,1)} %copy.59) | copy-start | bytes 49156
  192.4 32.4 %copy-start.10 = (bf16[256,1024]{1,0:T(8,128)(2,1)S(1)}, bf16[256,1024]{1,0:T(8,128)(2,1)}, u32[]{:S(2)}) copy-start(bf16[256,1024]{1,0:T(8,128)(2,1)} %copy-done.9) | copy-start | bytes 1572868
  215.6 9.1 %collective-permute-start.29 = (f32[1,1024]{1,0:T(1,128)S(1)}, f32[1,1024]{1,0:T(1,128)S(1)}, u32[]{:S(2)}, u32[]{:S(2)}) collective-permute-start(f32[1,1024]{1,0:T(1,128)S(1)} %slice.97), channel_id=1, source_target_pairs={{0,1},{1,2},{2,3},{3,4},{4,5},{5,6},{6,7},{7,8},{8,9},{9,10},{10,1... | collective-permute-start | bytes 12296 | tf_op jit(solution)/shard_map/lift/ppermute | solution.py:28

commit v2 on v1

--- a/solution.py
+++ b/solution.py
@@ -395,12 +395,12 @@
         inverse = by_row(lax.rsqrt(jnp.maximum(squares, 0.0) / wide + epsilon))
         factor = math.log2(math.e) / math.sqrt(HEAD)
         q = (q * (inverse * factor)).astype(bf16)
-        every_inverse = gathered(inverse.reshape(1, n), ("x", "c")).reshape(8, n)
+        every_inverse = gathered(gate(inverse, below).reshape(1, n), ("x", "c")).reshape(8, n)
 
     with jax.named_scope("attention"):
         chunks, places, sources = [], [], []
         for by in (0, 1, 3, 2):
-            mine = near[by]
+            mine = near[by] if by == 0 else gate(near[by], every_inverse)
             other = rotated(mine, "c", 1)
             source = (x + by) % 4
             shift = 128 * (source - x)
@@ -408,13 +408,12 @@
             places += [shift, shift + 32 * (1 - 2 * c)]
             sources += [2 * source + c, 2 * source + 1 - c]
         places = jnp.stack(places + sources).astype(jnp.int32)
-        q = gate(q, (below, above))
         heads = coarse_attention(q, every_inverse, chunks, places)
 
     with jax.named_scope("lift"):
         heads = jnp.swapaxes(heads.reshape(2, 8, 2, run_count, HEAD), 1, 2)
         heads = heads.reshape(4, 8 * run_count, HEAD)
-        slot = lax.dynamic_slice(z_rows, (0, 128 * z), (8 * run_count, 128))
+        slot = lax.dynamic_slice(gate(z_rows, kv), (0, 128 * z), (8 * run_count, 128))
         slot = slot.reshape(4, 2, run_count, 4, 32)
         slots = jnp.transpose(slot, (3, 1, 0, 2, 4)).reshape(4, 8 * run_count, 32)
         total = None

time: 228 us -> 227 us (level)
  waiting for transfers between devices: 74.3 us -> 68.7 us
  starting transfers between devices: 52.2 us -> 54.5 us
    ppermute x27, waiting for transfers between devices: 50.5 us -> 46.2 us  [rotated(): lax.ppermute(array, axis, [(i, (i + by) % size) for i in range(size)])]
    unnamed x49 -> x47, local copies, waits for them, and re-layouts: 6.93 us -> 8.15 us
  transfers between devices with their start and end apart: 32 -> 32, of which waited for: 15 -> 16; matrix products, arithmetic and copies ran while one was open for 9% -> 9% of each run, Pallas kernels for 11% -> 11%
where the time goes in v2:
time: 227 us; the launch traced here: 223 us
  waiting for transfers between devices  68.7 us (30%)
  starting transfers between devices  54.5 us (24%)
  blocking collectives  37.9 us (17%)
  Pallas kernels  30 us (13%)
  local copies, waits for them, and re-layouts  18.3 us (8%)
  other arithmetic  10.2 us (4%)
  matrix products  3.1 us (1%)
    ppermute x27, waiting for transfers between devices, rotated(): lax.ppermute(array, axis, [(i, (i + by) % size) for i in range(size)])  46.2 us
    ppermute x27, starting transfers between devices, rotated(): lax.ppermute(array, axis, [(i, (i + by) % size) for i in range(size)])  36.1 us
    all_to_all x1, blocking collectives, exchanged(): return lax.all_to_all(pieces, axes, split_axis=0, concat_axis=0, tiled=True)  23.5 us
    pallas_call x1, Pallas kernels, coarse_attention(): pl.pallas_call(attention_kernel, out_shape=jax.ShapeDtypeStruct((rows, HE...  14.5 us
    all_to_all x1, blocking collectives, gathered(): return lax.all_to_all(copies, axes, split_axis=0, concat_axis=0, tiled=True)  14.4 us
    ppermute x2, waiting for transfers between devices, from_behind(): return lax.ppermute(array, axis, pairs)  14.1 us
    all_to_all x2, starting transfers between devices, gathered(): return lax.all_to_all(copies, axes, split_axis=0, concat_axis=0, tiled=True)  9.94 us
    pallas_call x1, Pallas kernels, fine_layer(): pl.pallas_call(fine_kernel, out_shape=(jax.ShapeDtypeStruct((rows, width)...  9.48 us
  transfers between devices with their start and end apart: 32, of which 16 were waited for; matrix products, arithmetic and copies ran while one was open for 9% of the time, Pallas kernels for 11%

profile of v2, /device:TPU:16, one launch (start us, length us, event | category | flops | bytes accessed | tf_op | source)
XLA Modules:
  0.0 223.5 jit_solution(11116422948155697511)
XLA Ops:
  0.0 1.4 fusion.2
  1.4 1.3 fusion.4.normed_ref
  2.7 1.9 collective-permute-start
  4.6 1.1 fusion.35
  5.8 1.1 copy_bitcast_fusion.1
  6.9 0.8 pad_maximum_fusion
  7.7 4.7 %collective-permute-start.9 = (bf16[1024,256]{1,0:T(8,128)(2,1)}, bf16[1024,256]{1,0:T(8,128)(2,1)}, u32[]{:S(2)}, u32[]{:S(2)}) collective-permute-start(bf16[1024,256]{1,0:T(8,128)(2,1)} %pad_maximum_fusion), channel_id=1, source_target_pairs={{0,0},{16,1},{32,2},{48,3},{64,4},{80,5},{96,6},{112,7},{128,8},{1... | collective-permute-start | bytes 1572872 | tf_op jit(solution)/shard_map/weights/ppermute | solution.py:338
  13.2 6.9 %collective-permute-done.before_ref = bf16[256,1024]{1,0:T(8,128)(2,1)} collective-permute-done((bf16[256,1024]{1,0:T(8,128)(2,1)S(1)}, bf16[256,1024]{1,0:T(8,128)(2,1)}, u32[]{:S(2)}, u32[]{:S(2)}) %collective-permute-start) | collective-permute-done | bytes 524320 | tf_op jit(solution)/shard_map/ppermute | solution.py:28
  20.1 9.5 %shard_map.109 = (bf16[256,1024]{1,0:T(8,128)(2,1)S(1)}, bf16[32,1024]{1,0:T(8,128)(2,1)S(1)}) custom-call(s32[1]{0:T(128)} %bitcast.first_ref, bf16[256,1024]{1,0:T(8,128)(2,1)S(1)} %copy-done.1, bf16[256,1024]{1,0:T(8,128)(2,1)S(1)} %fusion.4.normed_ref, bf16[256,1024]{1,0:T(8,128)(2,1)} %collective-permute-done.before_ref, bf16[1024,1024]{1,0:T(8,128)(2,1)} %query_ref.1, ...), custom_call_target="tpu_custom_call" | custom-call | tf_op jit(solution)/shard_map/pallas_call | solution.py:111
  29.6 0.8 copy-done.9
  30.4 4.5 %collective-permute-start.1 = (bf16[32,1024]{1,0:T(8,128)(2,1)S(1)}, bf16[32,1024]{1,0:T(8,128)(2,1)S(1)}, u32[]{:S(2)}, u32[]{:S(2)}) collective-permute-start(bf16[32,1024]{1,0:T(8,128)(2,1)S(1)} %get-tuple-element.22), channel_id=1, source_target_pairs={{0,64},{16,80},{32,96},{48,112},{64,0},{80,16},{96,32},{112,48},{1... | collective-permute-start | bytes 196616 | tf_op jit(solution)/shard_map/gather_rows/ppermute | solution.py:33
  35.1 3.7 %collective-permute-done.1 = bf16[32,1024]{1,0:T(8,128)(2,1)S(1)} collective-permute-done((bf16[32,1024]{1,0:T(8,128)(2,1)S(1)}, bf16[32,1024]{1,0:T(8,128)(2,1)S(1)}, u32[]{:S(2)}, u32[]{:S(2)}) %collective-permute-start.1) | collective-permute-done | bytes 65568 | tf_op jit(solution)/shard_map/gather_rows/ppermute | solution.py:33
  38.8 8.0 %collective-permute-start.2 = (bf16[2,32,1024]{2,1,0:T(8,128)(2,1)S(1)}, bf16[2,32,1024]{2,1,0:T(8,128)(2,1)S(1)}, u32[]{:S(2)}, u32[]{:S(2)}) collective-permute-start(bf16[2,32,1024]{2,1,0:T(8,128)(2,1)S(1)} %maximum_select_fusion.1), channel_id=1, source_target_pairs={{0,112},{16,0},{32,16},{48,32},{64,48},{80,64},{96,80},{112,96},{1... | collective-permute-start | bytes 393224 | tf_op jit(solution)/shard_map/gather_rows/ppermute | solution.py:33
  46.7 1.5 collective-permute-start.4
  48.3 1.2 multiply_convert_fusion.pack_ref
  49.6 3.7 %collective-permute-done.2 = bf16[2,32,1024]{2,1,0:T(8,128)(2,1)S(1)} collective-permute-done((bf16[2,32,1024]{2,1,0:T(8,128)(2,1)S(1)}, bf16[2,32,1024]{2,1,0:T(8,128)(2,1)S(1)}, u32[]{:S(2)}, u32[]{:S(2)}) %collective-permute-start.2) | collective-permute-done | bytes 131104 | tf_op jit(solution)/shard_map/gather_rows/ppermute | solution.py:33
  53.3 8.2 %collective-permute-done.3 = bf16[2,32,1024]{2,1,0:T(8,128)(2,1)S(1)} collective-permute-done((bf16[2,32,1024]{2,1,0:T(8,128)(2,1)S(1)}, bf16[2,32,1024]{2,1,0:T(8,128)(2,1)S(1)}, u32[]{:S(2)}, u32[]{:S(2)}) %collective-permute-start.3) | collective-permute-done | bytes 131104 | tf_op jit(solution)/shard_map/gather_rows/ppermute | solution.py:33
  61.6 1.7 weights.1
  63.4 3.1 %collective-permute-done.10 = bf16[4,2,672,128]{3,2,1,0:T(8,128)(2,1)S(1)} collective-permute-done((bf16[4,2,672,128]{3,2,1,0:T(8,128)(2,1)S(1)}, bf16[4,2,672,128]{3,2,1,0:T(8,128)(2,1)S(1)}, u32[]{:S(2)}, u32[]{:S(2)}) %collective-permute-start.10) | collective-permute-done | bytes 1376288 | tf_op jit(solution)/shard_map/weights/ppermute | solution.py:33
  66.8 1.3 collective-permute-start.13
  68.1 2.0 collective-permute-start.11
  70.1 1.4 collective-permute-start.5
  71.6 1.0 collective-permute-start.7
  72.6 6.7 %collective-permute-done.13 = bf16[2,672,128]{2,1,0:T(8,128)(2,1)S(1)} collective-permute-done((bf16[2,672,128]{2,1,0:T(8,128)(2,1)S(1)}, bf16[2,672,128]{2,1,0:T(8,128)(2,1)S(1)}, u32[]{:S(2)}, u32[]{:S(2)}) %collective-permute-start.13) | collective-permute-done | bytes 344096 | tf_op jit(solution)/shard_map/weights/ppermute | solution.py:33
  79.9 6.0 %collective-permute-done.11 = bf16[2,672,128]{2,1,0:T(8,128)(2,1)S(1)} collective-permute-done((bf16[2,672,128]{2,1,0:T(8,128)(2,1)S(1)}, bf16[2,672,128]{2,1,0:T(8,128)(2,1)S(1)}, u32[]{:S(2)}, u32[]{:S(2)}) %collective-permute-start.11) | collective-permute-done | bytes 344096 | tf_op jit(solution)/shard_map/weights/ppermute | solution.py:33
  86.1 1.6 collective-permute-start.14
  87.9 2.1 collective-permute-start.8
  90.0 3.5 %collective-permute-done.14 = bf16[672,128]{1,0:T(8,128)(2,1)S(1)} collective-permute-done((bf16[672,128]{1,0:T(8,128)(2,1)S(1)}, bf16[672,128]{1,0:T(8,128)(2,1)S(1)}, u32[]{:S(2)}, u32[]{:S(2)}) %collective-permute-start.14) | collective-permute-done | bytes 172064 | tf_op jit(solution)/shard_map/weights/ppermute | solution.py:33
  93.5 4.6 %collective-permute-done.6.top_ref = bf16[128,1024]{1,0:T(8,128)(2,1)S(1)} collective-permute-done((bf16[128,1024]{1,0:T(8,128)(2,1)S(1)}, bf16[128,1024]{1,0:T(8,128)(2,1)S(1)}, u32[]{:S(2)}, u32[]{:S(2)}) %collective-permute-start.6) | collective-permute-done | bytes 262176 | tf_op jit(solution)/shard_map/gather_rows/ppermute | solution.py:33
  98.8 14.4 %all_to_all.20.near_ref = bf16[4,672,128]{2,1,0:T(8,128)(2,1)S(1)} all-to-all(bf16[4,672,128]{2,1,0:T(8,128)(2,1)S(1)} %broadcast_in_dim.22), channel_id=1, replica_groups=mesh['yh'=2,'z'=8,'x'=4,'yl'=2,'c'=2] {'x'}, dimensions={0} | all-to-all | bytes 1376256 | tf_op jit(solution)/shard_map/weights/all_to_all | solution.py:45
  113.5 1.9 collective-permute-done.15.far_ref
  115.5 1.0 copy-done.3
  116.5 1.0 copy-done.5
  117.6 0.9 copy-done.12
  118.5 0.9 copy-done.14
  119.5 4.4 %project.1 = (bf16[1024,256]{1,0:T(8,128)(2,1)}, f32[1024,128]{1,0:T(8,128)S(1)}, f32[4,8,256]{2,1,0:T(8,128)S(1)}) custom-call(s32[3]{0:T(128)S(1)} %pad_add_fusion.where_ref, bf16[256,1024]{1,0:T(8,128)(2,1)S(1)} %bitcast.123, bf16[256,1024]{1,0:T(8,128)(2,1)S(1)} %copy-done.3, bf16[128,1024]{1,0:T(8,128)(2,1)S(1)} %copy-done.12, ...), custom_call_target="tpu_custom_call" | custom-call | tf_op jit(solution)/shard_map/project/pallas_call | solution.py:295
  123.8 0.8 copy-done.6
  124.6 1.2 collective-permute-start.18
  125.8 0.9 collective-permute-start.20
  126.6 1.1 collective-permute-start.22
  128.4 6.0 %all-to-all-start.1 = ((f32[8,1,1024]{2,1,0:T(1,128)}), f32[8,1,1024]{2,1,0:T(1,128)S(1)}, u32[]{:S(2)}, u32[]{:S(2)}) async-start(f32[8,1,1024]{2,1,0:T(1,128)} %broadcast_in_dim.23), calls=%async_computation.1 | async-start | bytes 65536 | tf_op jit(solution)/shard_map/project/all_to_all | solution.py:45
  134.4 0.9 broadcast_select_fusion.1
  136.0 0.8 copy_bitcast_fusion
  137.3 1.5 collective-permute-start.16
  138.8 3.6 %all-to-all-done.1 = f32[8,1,1024]{2,1,0:T(1,128)S(1)} async-done(((f32[8,1,1024]{2,1,0:T(1,128)}), f32[8,1,1024]{2,1,0:T(1,128)S(1)}, u32[]{:S(2)}, u32[]{:S(2)}) %all-to-all-start.1) | async-done | bytes 32800 | tf_op jit(solution)/shard_map/project/all_to_all | solution.py:45
  143.2 3.3 %collective-permute-done.16 = bf16[160,1024]{1,0:T(8,128)(2,1)} collective-permute-done((bf16[160,1024]{1,0:T(8,128)(2,1)}, bf16[160,1024]{1,0:T(8,128)(2,1)}, u32[]{:S(2)}, u32[]{:S(2)}) %collective-permute-start.16) | collective-permute-done | bytes 327712 | tf_op jit(solution)/shard_map/weights/ppermute | solution.py:33
  147.1 3.9 %all-to-all-start.2 = ((f32[8,1,1024]{2,1,0:T(1,128)}), f32[8,1,1024]{2,1,0:T(1,128)}, u32[]{:S(2)}, u32[]{:S(2)}) async-start(f32[8,1,1024]{2,1,0:T(1,128)} %broadcast_in_dim.24), calls=%async_computation.2 | async-start | bytes 65536 | tf_op jit(solution)/shard_map/project/all_to_all | solution.py:45
  151.7 4.8 %all-to-all-done.2 = f32[8,1,1024]{2,1,0:T(1,128)} async-done(((f32[8,1,1024]{2,1,0:T(1,128)}), f32[8,1,1024]{2,1,0:T(1,128)}, u32[]{:S(2)}, u32[]{:S(2)}) %all-to-all-start.2) | async-done | bytes 32800 | tf_op jit(solution)/shard_map/project/all_to_all | solution.py:45
  159.7 0.8 copy.75
  160.5 0.8 copy.76
  162.7 0.8 mul.152
  163.5 1.2 multiply_convert_fusion.1.q_ref
  164.8 1.0 collective-permute-start.26
  165.8 14.5 %attention.1 = bf16[1024,128]{1,0:T(8,128)(2,1)S(1)} custom-call(s32[16]{0:T(128)S(1)} %stack.134.place_ref, bf16[1024,128]{1,0:T(8,128)(2,1)S(1)} %multiply_convert_fusion.1.q_ref, f32[8,1024]{1,0:T(8,128)S(1)} %bitcast.129, bf16[1024,256]{1,0:T(8,128)(2,1)} %get-tuple-element.32.refs_0_, bf16[1024,256]{1,0:T(8,128)(2,1)S(1)} %collective-permute-done.17.refs_1_, ...), custom_call_target="tpu_custom_call" | custom-call | tf_op jit(solution)/shard_map/attention/pallas_call | solution.py:180
  180.4 1.2 collective-permute-start.27
  181.6 2.1 collective-permute-start.24
  183.7 2.0 collective-permute-start.25
  186.0 1.3 convolution_add_fusion.1
  187.3 1.3 fusion.24
  188.5 0.9 collective-permute-done.25
  189.8 23.5 %all_to_all.21 = bf16[8,32,1024]{2,1,0:T(8,128)(2,1)S(1)} all-to-all(bf16[8,32,1024]{2,1,0:T(8,128)(2,1)S(1)} %bitcast.130), channel_id=1, replica_groups=mesh['yh'=2,'z'=8,'x'=4,'yl'=2,'c'=2] {'z'}, dimensions={0} | all-to-all | bytes 1048576 | tf_op jit(solution)/shard_map/lift/all_to_all | solution.py:49
  213.4 1.9 collective-permute-start.29
  215.3 7.2 %collective-permute-done.29 = f32[1,1024]{1,0:T(1,128)S(1)} collective-permute-done((f32[1,1024]{1,0:T(1,128)S(1)}, f32[1,1024]{1,0:T(1,128)S(1)}, u32[]{:S(2)}, u32[]{:S(2)}) %collective-permute-start.29) | collective-permute-done | bytes 4128 | tf_op jit(solution)/shard_map/lift/ppermute | solution.py:28
  222.5 0.9 fusion.5
  (116 shorter events, 12.4 us)
Async XLA Ops:
  0.0 5.8 %copy-start = (bf16[256,4096]{1,0:T(8,128)(2,1)S(1)}, bf16[256,4096]{1,0:T(8,128)(2,1)}, u32[]{:S(2)}) copy-start(bf16[256,4096]{1,0:T(8,128)(2,1)} %param.20) | copy-start | bytes 6291460
  0.0 4.6 %copy-start.17 = (bf16[256,2,256]{2,1,0:T(2,128)(2,1)S(1)}, bf16[256,2,256]{2,1,0:T(2,128)(2,1)}, u32[]{:S(2)}) copy-start(bf16[256,2,256]{2,1,0:T(2,128)(2,1)} %param.19) | copy-start | bytes 786436
  1.4 5.5 %copy-start.20 = (bf16[256,256]{1,0:T(8,128)(2,1)S(1)}, bf16[256,256]{1,0:T(8,128)(2,1)}, u32[]{:S(2)}) copy-start(bf16[256,256]{1,0:T(8,128)(2,1)} %param.18) | copy-start | bytes 393220
  2.7 17.5 %collective-permute-start = (bf16[256,1024]{1,0:T(8,128)(2,1)S(1)}, bf16[256,1024]{1,0:T(8,128)(2,1)}, u32[]{:S(2)}, u32[]{:S(2)}) collective-permute-start(bf16[256,1024]{1,0:T(8,128)(2,1)S(1)} %fusion.4.normed_ref), channel_id=1, source_target_pairs={{0,1},{1,2},{2,3},{3,4},{4,5},{5,6},{6,7},{7,8},{8,9},{9,10},{10,1... | collective-permute-start | bytes 1572872 | tf_op jit(solution)/shard_map/ppermute | solution.py:28
  4.6 15.5 %copy-start.1 = (bf16[256,1024]{1,0:T(8,128)(2,1)S(1)}, bf16[256,1024]{1,0:T(8,128)(2,1)}, u32[]{:S(2)}) copy-start(bf16[256,1024]{1,0:T(8,128)(2,1)} %tokens_ref.1) | copy-start | bytes 1572868
  7.7 40.6 %collective-permute-start.9 = (bf16[1024,256]{1,0:T(8,128)(2,1)}, bf16[1024,256]{1,0:T(8,128)(2,1)}, u32[]{:S(2)}, u32[]{:S(2)}) collective-permute-start(bf16[1024,256]{1,0:T(8,128)(2,1)} %pad_maximum_fusion), channel_id=1, source_target_pairs={{0,0},{16,1},{32,2},{48,3},{64,4},{80,5},{96,6},{112,7},{128,8},{1... | collective-permute-start | bytes 1572872 | tf_op jit(solution)/shard_map/weights/ppermute | solution.py:338
  29.6 0.8 copy-start.9
  30.4 8.3 %collective-permute-start.1 = (bf16[32,1024]{1,0:T(8,128)(2,1)S(1)}, bf16[32,1024]{1,0:T(8,128)(2,1)S(1)}, u32[]{:S(2)}, u32[]{:S(2)}) collective-permute-start(bf16[32,1024]{1,0:T(8,128)(2,1)S(1)} %get-tuple-element.22), channel_id=1, source_target_pairs={{0,64},{16,80},{32,96},{48,112},{64,0},{80,16},{96,32},{112,48},{1... | collective-permute-start | bytes 196616 | tf_op jit(solution)/shard_map/gather_rows/ppermute | solution.py:33
  38.8 14.5 %collective-permute-start.2 = (bf16[2,32,1024]{2,1,0:T(8,128)(2,1)S(1)}, bf16[2,32,1024]{2,1,0:T(8,128)(2,1)S(1)}, u32[]{:S(2)}, u32[]{:S(2)}) collective-permute-start(bf16[2,32,1024]{2,1,0:T(8,128)(2,1)S(1)} %maximum_select_fusion.1), channel_id=1, source_target_pairs={{0,112},{16,0},{32,16},{48,32},{64,48},{80,64},{96,80},{112,96},{1... | collective-permute-start | bytes 393224 | tf_op jit(solution)/shard_map/gather_rows/ppermute | solution.py:33
  46.7 14.7 %collective-permute-start.3 = (bf16[2,32,1024]{2,1,0:T(8,128)(2,1)S(1)}, bf16[2,32,1024]{2,1,0:T(8,128)(2,1)S(1)}, u32[]{:S(2)}, u32[]{:S(2)}) collective-permute-start(bf16[2,32,1024]{2,1,0:T(8,128)(2,1)S(1)} %maximum_select_fusion.1), channel_id=1, source_target_pairs={{0,96},{16,112},{32,0},{48,16},{64,32},{80,48},{96,64},{112,80},{1... | collective-permute-start | bytes 393224 | tf_op jit(solution)/shard_map/gather_rows/ppermute | solution.py:33
  46.7 14.7 %collective-permute-start.4 = (bf16[2,32,1024]{2,1,0:T(8,128)(2,1)S(1)}, bf16[2,32,1024]{2,1,0:T(8,128)(2,1)S(1)}, u32[]{:S(2)}, u32[]{:S(2)}) collective-permute-start(bf16[2,32,1024]{2,1,0:T(8,128)(2,1)S(1)} %maximum_select_fusion.1), channel_id=1, source_target_pairs={{0,16},{16,32},{32,48},{48,64},{64,80},{80,96},{96,112},{112,0},{1... | collective-permute-start | bytes 393224 | tf_op jit(solution)/shard_map/gather_rows/ppermute | solution.py:33
  49.6 12.0 %copy-start.7 = (bf16[1024,256]{1,0:T(8,128)(2,1)S(1)}, bf16[1024,256]{1,0:T(8,128)(2,1)}, u32[]{:S(2)}) copy-start(bf16[1024,256]{1,0:T(8,128)(2,1)} %down_ref.1) | copy-start | bytes 1572868
  49.6 12.0 %copy-start.8 = (bf16[256,1024]{1,0:T(8,128)(2,1)S(1)}, bf16[256,1024]{1,0:T(8,128)(2,1)}, u32[]{:S(2)}) copy-start(bf16[256,1024]{1,0:T(8,128)(2,1)} %up_ref.1) | copy-start | bytes 1572868
  63.3 3.2 %collective-permute-start.10 = (bf16[4,2,672,128]{3,2,1,0:T(8,128)(2,1)S(1)}, bf16[4,2,672,128]{3,2,1,0:T(8,128)(2,1)S(1)}, u32[]{:S(2)}, u32[]{:S(2)}) collective-permute-start(bf16[4,2,672,128]{3,2,1,0:T(8,128)(2,1)S(1)} %get-tuple-element.27), channel_id=1, source_target_pairs={{0,1},{1,0},{2,3},{3,2},{4,5},{5,4},{6,7},{7,6},{8,9},{9,8},{10,11... | collective-permute-start | bytes 4128776 | tf_op jit(solution)/shard_map/weights/ppermute | solution.py:33
  66.8 12.5 %collective-permute-start.13 = (bf16[2,672,128]{2,1,0:T(8,128)(2,1)S(1)}, bf16[2,672,128]{2,1,0:T(8,128)(2,1)S(1)}, u32[]{:S(2)}, u32[]{:S(2)}) collective-permute-start(bf16[2,672,128]{2,1,0:T(8,128)(2,1)S(1)} %get-tuple-element.38), channel_id=1, source_target_pairs={{0,8},{4,12},{8,0},{12,4},{1,9},{5,13},{9,1},{13,5},{2,10},{6,14},... | collective-permute-start | bytes 1032200 | tf_op jit(solution)/shard_map/weights/ppermute | solution.py:33
  68.1 11.8 %collective-permute-start.12 = (bf16[2,672,128]{2,1,0:T(8,128)(2,1)S(1)}, bf16[2,672,128]{2,1,0:T(8,128)(2,1)S(1)}, u32[]{:S(2)}, u32[]{:S(2)}) collective-permute-start(bf16[2,672,128]{2,1,0:T(8,128)(2,1)S(1)} %get-tuple-element.39), channel_id=1, source_target_pairs={{0,12},{4,0},{8,4},{12,8},{1,13},{5,1},{9,5},{13,9},{2,14},{6,2},{... | collective-permute-start | bytes 1032200 | tf_op jit(solution)/shard_map/weights/ppermute | solution.py:33
  68.1 17.8 %collective-permute-start.11 = (bf16[2,672,128]{2,1,0:T(8,128)(2,1)S(1)}, bf16[2,672,128]{2,1,0:T(8,128)(2,1)S(1)}, u32[]{:S(2)}, u32[]{:S(2)}) collective-permute-start(bf16[2,672,128]{2,1,0:T(8,128)(2,1)S(1)} %get-tuple-element.37), channel_id=1, source_target_pairs={{0,4},{4,8},{8,12},{12,0},{1,5},{5,9},{9,13},{13,1},{2,6},{6,10},{... | collective-permute-start | bytes 1032200 | tf_op jit(solution)/shard_map/weights/ppermute | solution.py:33
  70.1 17.6 %collective-permute-start.5 = (bf16[256,1024]{1,0:T(8,128)(2,1)S(1)}, bf16[256,1024]{1,0:T(8,128)(2,1)S(1)}, u32[]{:S(2)}, u32[]{:S(2)}) collective-permute-start(bf16[256,1024]{1,0:T(8,128)(2,1)S(1)} %bitcast.121), channel_id=1, source_target_pairs={{0,130},{2,0},{128,2},{130,128},{1,131},{3,1},{129,3},{131,129},{4... | collective-permute-start | bytes 1572872 | tf_op jit(solution)/shard_map/gather_rows/ppermute | solution.py:33
  71.6 16.3 %collective-permute-start.7 = (bf16[256,1024]{1,0:T(8,128)(2,1)S(1)}, bf16[256,1024]{1,0:T(8,128)(2,1)S(1)}, u32[]{:S(2)}, u32[]{:S(2)}) collective-permute-start(bf16[256,1024]{1,0:T(8,128)(2,1)S(1)} %bitcast.122), channel_id=1, source_target_pairs={{0,2},{2,128},{128,130},{130,0},{1,3},{3,129},{129,131},{131,1},{4... | collective-permute-start | bytes 1572872 | tf_op jit(solution)/shard_map/gather_rows/ppermute | solution.py:33
  86.1 7.3 %collective-permute-start.14 = (bf16[672,128]{1,0:T(8,128)(2,1)S(1)}, bf16[672,128]{1,0:T(8,128)(2,1)S(1)}, u32[]{:S(2)}, u32[]{:S(2)}) collective-permute-start(bf16[672,128]{1,0:T(8,128)(2,1)S(1)} %fusion.13), channel_id=1, source_target_pairs={{0,2},{2,0},{1,3},{3,1},{4,6},{6,4},{5,7},{7,5},{8,10},{10,8},{9,1... | collective-permute-start | bytes 516104 | tf_op jit(solution)/shard_map/weights/ppermute | solution.py:33
  87.7 10.4 %copy-start.2 = (bf16[256,1024]{1,0:T(8,128)(2,1)}, bf16[256,1024]{1,0:T(8,128)(2,1)S(1)}, u32[]{:S(2)}) copy-start(bf16[256,1024]{1,0:T(8,128)(2,1)S(1)} %collective-permute-done.5.above_ref) | copy-start | bytes 1572868
  87.8 10.4 %collective-permute-start.6 = (bf16[128,1024]{1,0:T(8,128)(2,1)S(1)}, bf16[128,1024]{1,0:T(8,128)(2,1)S(1)}, u32[]{:S(2)}, u32[]{:S(2)}) collective-permute-start(bf16[128,1024]{1,0:T(8,128)(2,1)S(1)} %slice.87), channel_id=1, source_target_pairs={{0,130},{2,0},{128,2},{130,128},{1,131},{3,1},{129,3},{131,129},{4... | collective-permute-start | bytes 786440 | tf_op jit(solution)/shard_map/gather_rows/ppermute | solution.py:33
  87.9 25.3 %copy-start.4 = (bf16[256,1024]{1,0:T(8,128)(2,1)}, bf16[256,1024]{1,0:T(8,128)(2,1)S(1)}, u32[]{:S(2)}) copy-start(bf16[256,1024]{1,0:T(8,128)(2,1)S(1)} %collective-permute-done.7.below_ref) | copy-start | bytes 1572868
  87.9 10.2 %collective-permute-start.8 = (bf16[128,1024]{1,0:T(8,128)(2,1)S(1)}, bf16[128,1024]{1,0:T(8,128)(2,1)S(1)}, u32[]{:S(2)}, u32[]{:S(2)}) collective-permute-start(bf16[128,1024]{1,0:T(8,128)(2,1)S(1)} %slice.88), channel_id=1, source_target_pairs={{0,2},{2,128},{128,130},{130,0},{1,3},{3,129},{129,131},{131,1},{4... | collective-permute-start | bytes 786440 | tf_op jit(solution)/shard_map/gather_rows/ppermute | solution.py:33
  98.1 0.7 copy-start.11
  98.1 15.1 %copy-start.13 = (bf16[128,1024]{1,0:T(8,128)(2,1)}, bf16[128,1024]{1,0:T(8,128)(2,1)S(1)}, u32[]{:S(2)}) copy-start(bf16[128,1024]{1,0:T(8,128)(2,1)S(1)} %collective-permute-done.8.bottom_ref) | copy-start | bytes 786436
  113.2 2.3 %collective-permute-start.15 = (bf16[4,672,128]{2,1,0:T(8,128)(2,1)S(1)}, bf16[4,672,128]{2,1,0:T(8,128)(2,1)}, u32[]{:S(2)}, u32[]{:S(2)}) collective-permute-start(bf16[4,672,128]{2,1,0:T(8,128)(2,1)S(1)} %all_to_all.20.near_ref), channel_id=1, source_target_pairs={{0,1},{1,0},{2,3},{3,2},{4,5},{5,4},{6,7},{7,6},{8,9},{9,8},{10,11... | collective-permute-start | bytes 2064392 | tf_op jit(solution)/shard_map/weights/ppermute | solution.py:33
  115.5 1.0 copy-start.3
  116.5 1.0 copy-start.5
  117.6 0.9 copy-start.12
  118.5 0.9 copy-start.14
  123.8 0.8 copy-start.6
  124.6 32.7 %collective-permute-start.18 = (bf16[1024,256]{1,0:T(8,128)(2,1)}, bf16[1024,256]{1,0:T(8,128)(2,1)}, u32[]{:S(2)}, u32[]{:S(2)}) collective-permute-start(bf16[1024,256]{1,0:T(8,128)(2,1)} %get-tuple-element.32.refs_0_), channel_id=1, source_target_pairs={{0,12},{4,0},{8,4},{12,8},{1,13},{5,1},{9,5},{13,9},{2,14},{6,2},{... | collective-permute-start | bytes 1572872 | tf_op jit(solution)/shard_map/project/ppermute | solution.py:33
  125.8 31.6 %collective-permute-start.20 = (bf16[1024,256]{1,0:T(8,128)(2,1)}, bf16[1024,256]{1,0:T(8,128)(2,1)}, u32[]{:S(2)}, u32[]{:S(2)}) collective-permute-start(bf16[1024,256]{1,0:T(8,128)(2,1)} %get-tuple-element.32.refs_0_), channel_id=1, source_target_pairs={{0,4},{4,8},{8,12},{12,0},{1,5},{5,9},{9,13},{13,1},{2,6},{6,10},{... | collective-permute-start | bytes 1572872 | tf_op jit(solution)/shard_map/project/ppermute | solution.py:33
  126.6 31.2 %collective-permute-start.22 = (bf16[1024,256]{1,0:T(8,128)(2,1)}, bf16[1024,256]{1,0:T(8,128)(2,1)}, u32[]{:S(2)}, u32[]{:S(2)}) collective-permute-start(bf16[1024,256]{1,0:T(8,128)(2,1)} %get-tuple-element.32.refs_0_), channel_id=1, source_target_pairs={{0,8},{4,12},{8,0},{12,4},{1,9},{5,13},{9,1},{13,5},{2,10},{6,14},... | collective-permute-start | bytes 1572872 | tf_op jit(solution)/shard_map/project/ppermute | solution.py:33
  128.4 14.0 %all-to-all-start.1 = ((f32[8,1,1024]{2,1,0:T(1,128)}), f32[8,1,1024]{2,1,0:T(1,128)S(1)}, u32[]{:S(2)}, u32[]{:S(2)}) async-start(f32[8,1,1024]{2,1,0:T(1,128)} %broadcast_in_dim.23), calls=%async_computation.1 | async-start | bytes 65536 | tf_op jit(solution)/shard_map/project/all_to_all | solution.py:45
  135.3 0.7 copy-start.15
  136.7 50.5 %collective-permute-start.28 = (bf16[160,1024]{1,0:T(8,128)(2,1)}, bf16[160,1024]{1,0:T(8,128)(2,1)}, u32[]{:S(2)}, u32[]{:S(2)}) collective-permute-start(bf16[160,1024]{1,0:T(8,128)(2,1)} %copy_bitcast_fusion), channel_id=1, source_target_pairs={{0,130},{2,0},{128,2},{130,128},{1,131},{3,1},{129,3},{131,129},{4... | collective-permute-start | bytes 983048 | tf_op jit(solution)/shard_map/weights/ppermute | solution.py:33
  137.3 9.2 %collective-permute-start.16 = (bf16[160,1024]{1,0:T(8,128)(2,1)}, bf16[160,1024]{1,0:T(8,128)(2,1)}, u32[]{:S(2)}, u32[]{:S(2)}) collective-permute-start(bf16[160,1024]{1,0:T(8,128)(2,1)} %copy_bitcast_fusion), channel_id=1, source_target_pairs={{0,2},{2,128},{128,130},{130,0},{1,3},{3,129},{129,131},{131,1},{4... | collective-permute-start | bytes 983048 | tf_op jit(solution)/shard_map/weights/ppermute | solution.py:33
  142.6 0.6 copy-start.19
  146.5 18.2 %collective-permute-start.17 = (bf16[1024,256]{1,0:T(8,128)(2,1)}, bf16[1024,256]{1,0:T(8,128)(2,1)S(1)}, u32[]{:S(2)}, u32[]{:S(2)}) collective-permute-start(bf16[1024,256]{1,0:T(8,128)(2,1)} %get-tuple-element.32.refs_0_), channel_id=1, source_target_pairs={{0,1},{1,0},{2,3},{3,2},{4,5},{5,4},{6,7},{7,6},{8,9},{9,8},{10,11... | collective-permute-start | bytes 1572872 | tf_op jit(solution)/shard_map/attention/ppermute | solution.py:33
  147.1 9.4 %all-to-all-start.2 = ((f32[8,1,1024]{2,1,0:T(1,128)}), f32[8,1,1024]{2,1,0:T(1,128)}, u32[]{:S(2)}, u32[]{:S(2)}) async-start(f32[8,1,1024]{2,1,0:T(1,128)} %broadcast_in_dim.24), calls=%async_computation.2 | async-start | bytes 65536 | tf_op jit(solution)/shard_map/project/all_to_all | solution.py:45
  157.3 8.5 %collective-permute-start.19 = (bf16[1024,256]{1,0:T(8,128)(2,1)}, bf16[1024,256]{1,0:T(8,128)(2,1)S(1)}, u32[]{:S(2)}, u32[]{:S(2)}) collective-permute-start(bf16[1024,256]{1,0:T(8,128)(2,1)} %collective-permute-done.18.refs_2_), channel_id=1, source_target_pairs={{0,1},{1,0},{2,3},{3,2},{4,5},{5,4},{6,7},{7,6},{8,9},{9,8},{10,11... | collective-permute-start | bytes 1572872 | tf_op jit(solution)/shard_map/attention/ppermute | solution.py:33
  157.4 8.4 %collective-permute-start.21 = (bf16[1024,256]{1,0:T(8,128)(2,1)}, bf16[1024,256]{1,0:T(8,128)(2,1)}, u32[]{:S(2)}, u32[]{:S(2)}) collective-permute-start(bf16[1024,256]{1,0:T(8,128)(2,1)} %collective-permute-done.20.refs_4_), channel_id=1, source_target_pairs={{0,1},{1,0},{2,3},{3,2},{4,5},{5,4},{6,7},{7,6},{8,9},{9,8},{10,11... | collective-permute-start | bytes 1572872 | tf_op jit(solution)/shard_map/attention/ppermute | solution.py:33
  157.9 7.9 %collective-permute-start.23 = (bf16[1024,256]{1,0:T(8,128)(2,1)}, bf16[1024,256]{1,0:T(8,128)(2,1)}, u32[]{:S(2)}, u32[]{:S(2)}) collective-permute-start(bf16[1024,256]{1,0:T(8,128)(2,1)} %collective-permute-done.22.refs_6_), channel_id=1, source_target_pairs={{0,1},{1,0},{2,3},{3,2},{4,5},{5,4},{6,7},{7,6},{8,9},{9,8},{10,11... | collective-permute-start | bytes 1572872 | tf_op jit(solution)/shard_map/attention/ppermute | solution.py:33
  164.7 20.9 %copy-start.16 = (bf16[4,160,128]{2,1,0:T(8,128)(2,1)S(1)}, bf16[4,160,128]{2,1,0:T(8,128)(2,1)}, u32[]{:S(2)}) copy-start(bf16[4,160,128]{2,1,0:T(8,128)(2,1)} %copy-done.15) | copy-start | bytes 491524
  164.7 20.9 %copy-start.18 = (bf16[256,32]{1,0:T(8,128)(2,1)S(1)}, bf16[256,32]{1,0:T(8,128)(2,1)}, u32[]{:S(2)}) copy-start(bf16[256,32]{1,0:T(8,128)(2,1)} %copy.74) | copy-start | bytes 49156
  164.8 23.8 %collective-permute-start.26 = (bf16[160,1024]{1,0:T(8,128)(2,1)}, bf16[160,1024]{1,0:T(8,128)(2,1)S(1)}, u32[]{:S(2)}, u32[]{:S(2)}) collective-permute-start(bf16[160,1024]{1,0:T(8,128)(2,1)} %collective-permute-done.16), channel_id=1, source_target_pairs={{0,2},{2,128},{128,130},{130,0},{1,3},{3,129},{129,131},{131,1},{4... | collective-permute-start | bytes 983048 | tf_op jit(solution)/shard_map/weights/ppermute | solution.py:33
  180.4 6.9 %collective-permute-start.27 = (bf16[256,128]{1,0:T(8,128)(2,1)S(1)}, bf16[256,128]{1,0:T(8,128)(2,1)S(1)}, u32[]{:S(2)}, u32[]{:S(2)}) collective-permute-start(bf16[256,128]{1,0:T(8,128)(2,1)S(1)} %get-tuple-element.43), channel_id=1, source_target_pairs={{0,130},{2,0},{128,2},{130,128},{1,131},{3,1},{129,3},{131,129},{4... | collective-permute-start | bytes 196616 | tf_op jit(solution)/shard_map/lift/ppermute | solution.py:33
  181.6 4.4 %collective-permute-start.24 = (bf16[256,128]{1,0:T(8,128)(2,1)S(1)}, bf16[256,128]{1,0:T(8,128)(2,1)S(1)}, u32[]{:S(2)}, u32[]{:S(2)}) collective-permute-start(bf16[256,128]{1,0:T(8,128)(2,1)S(1)} %get-tuple-element.44), channel_id=1, source_target_pairs={{0,2},{2,128},{128,130},{130,0},{1,3},{3,129},{129,131},{131,1},{4... | collective-permute-start | bytes 196616 | tf_op jit(solution)/shard_map/lift/ppermute | solution.py:33
  183.7 5.8 %collective-permute-start.25 = (bf16[256,128]{1,0:T(8,128)(2,1)S(1)}, bf16[256,128]{1,0:T(8,128)(2,1)S(1)}, u32[]{:S(2)}, u32[]{:S(2)}) collective-permute-start(bf16[256,128]{1,0:T(8,128)(2,1)S(1)} %get-tuple-element.42), channel_id=1, source_target_pairs={{0,128},{2,130},{128,0},{130,2},{1,129},{3,131},{129,1},{131,3},{4... | collective-permute-start | bytes 196616 | tf_op jit(solution)/shard_map/lift/ppermute | solution.py:33
  189.8 32.8 %copy-start.10 = (bf16[256,1024]{1,0:T(8,128)(2,1)S(1)}, bf16[256,1024]{1,0:T(8,128)(2,1)}, u32[]{:S(2)}) copy-start(bf16[256,1024]{1,0:T(8,128)(2,1)} %copy-done.9) | copy-start | bytes 1572868
  213.4 9.1 %collective-permute-start.29 = (f32[1,1024]{1,0:T(1,128)S(1)}, f32[1,1024]{1,0:T(1,128)S(1)}, u32[]{:S(2)}, u32[]{:S(2)}) collective-permute-start(f32[1,1024]{1,0:T(1,128)S(1)} %slice.97), channel_id=1, source_target_pairs={{0,1},{1,2},{2,3},{3,4},{4,5},{5,6},{6,7},{7,8},{8,9},{9,10},{10,1... | collective-permute-start | bytes 12296 | tf_op jit(solution)/shard_map/lift/ppermute | solution.py:28

commit v3 on v2

--- a/solution.py
+++ b/solution.py
@@ -246,7 +246,7 @@
 
 def project_kernel(
     where_ref, own_ref, above_ref, top_ref, bottom_ref, below_ref, near_ref, far_ref,
-    kv_ref, q_ref, squares_ref, weight_ref,
+    kv_ref, q_ref, squares_ref, slots_ref, weight_ref,
 ):
     core, slot_at, y = where_ref[0], where_ref[1], where_ref[2]
     half = weight_ref.shape[0] // 2
@@ -267,6 +267,13 @@
         (opposite, opposite_slot),
         (below_ref[...], below_ref[:, lanes]),
     )
+    own_slot = own_ref[:, lanes]
+    for k in range(4):
+        for a in range(4):
+            for h in range(2):
+                at = slice((h * 4 + a) * 32, (h * 4 + a) * 32 + 32)
+                part = slice((a * 2 + h) * 32, (a * 2 + h) * 32 + 32)
+                slots_ref[(y + 4 - k) % 4, at, :] = own_slot[part, 32 * k : 32 * k + 32]
     for i, (rows, slot) in enumerate(groups):
         product = dot(rows, weight)
         squares = product[:, 3 * HEAD :] * slot.astype(f32)
@@ -298,9 +305,10 @@
             jax.ShapeDtypeStruct((n, 2 * HEAD), bf16),
             jax.ShapeDtypeStruct((n, HEAD), f32),
             jax.ShapeDtypeStruct((4, 8, n // 4), f32),
+            jax.ShapeDtypeStruct((4, n // 4, 32), bf16),
         ),
         in_specs=[pl.BlockSpec(memory_space=pltpu.SMEM)] + [whole] * 7,
-        out_specs=(whole, whole, whole),
+        out_specs=(whole, whole, whole, whole),
         scratch_shapes=[pltpu.VMEM((width, 4 * HEAD), bf16)],
         compiler_params=pltpu.CompilerParams(vmem_limit_bytes=40 << 20),
     )(where, *rows, near, far)
@@ -377,7 +385,7 @@
 
     with jax.named_scope("project"):
         where = jnp.stack([c, 128 * z, y]).astype(jnp.int32)
-        kv, q, squares = projected(where, y_rows, near_half, far_half)
+        kv, q, squares, slots = projected(where, y_rows, near_half, far_half)
         n = kv.shape[0]
 
         def in_order(parts):
@@ -395,7 +403,7 @@
         inverse = by_row(lax.rsqrt(jnp.maximum(squares, 0.0) / wide + epsilon))
         factor = math.log2(math.e) / math.sqrt(HEAD)
         q = (q * (inverse * factor)).astype(bf16)
-        every_inverse = gathered(gate(inverse, below).reshape(1, n), ("x", "c")).reshape(8, n)
+        every_inverse = gathered(gate(inverse, (below, q)).reshape(1, n), ("x", "c")).reshape(8, n)
 
     with jax.named_scope("attention"):
         chunks, places, sources = [], [], []
@@ -413,16 +421,12 @@
     with jax.named_scope("lift"):
         heads = jnp.swapaxes(heads.reshape(2, 8, 2, run_count, HEAD), 1, 2)
         heads = heads.reshape(4, 8 * run_count, HEAD)
-        slot = lax.dynamic_slice(gate(z_rows, kv), (0, 128 * z), (8 * run_count, 128))
-        slot = slot.reshape(4, 2, run_count, 4, 32)
-        slots = jnp.transpose(slot, (3, 1, 0, 2, 4)).reshape(4, 8 * run_count, 32)
         total = None
         for by in range(4):
             part = lax.dynamic_index_in_dim(heads, (y + by) % 4, 0, keepdims=False)
             if by:
                 part = rotated(part, ("yh", "yl"), by)
-            slot = lax.dynamic_index_in_dim(slots, (y + 4 - by) % 4, 0, keepdims=False)
-            product = dot(jnp.concatenate([part, slot], 1), seconds[by])
+            product = dot(jnp.concatenate([part, slots[by]], 1), seconds[by])
             total = product if total is None else total + product
         lifted = exchanged(total.astype(bf16).reshape(8, run_count, width), ("z",))
         lifted = jnp.sum(lifted.astype(f32), axis=0)

time: 227 us -> 220 us (0.969); the launches traced: 223 us -> 219 us
  local copies, waits for them, and re-layouts: 18.3 us -> 13.6 us
  starting transfers between devices: 54.5 us -> 57.1 us
    squeeze x5 -> x1, local copies, waits for them, and re-layouts: 3.13 us -> 0.02 us  [body(): product = dot(jnp.concatenate([part, slots[by]], 1), seconds[by])]
    ppermute x27, starting transfers between devices: 36.1 us -> 38.8 us  [rotated(): lax.ppermute(array, axis, [(i, (i + by) % size) for i in range(size)])]
    unnamed x47 -> x45, local copies, waits for them, and re-layouts: 8.15 us -> 8.49 us
  transfers between devices with their start and end apart: 32 -> 32, of which waited for: 16 -> 18; matrix products, arithmetic and copies ran while one was open for 9% -> 6% of each run, Pallas kernels for 11% -> 11%
where the time goes in v3:
time: 220 us; the launch traced here: 219 us
  waiting for transfers between devices  67.7 us (31%)
  starting transfers between devices  57.1 us (26%)
  blocking collectives  37.6 us (17%)
  Pallas kernels  30.3 us (14%)
  local copies, waits for them, and re-layouts  13.6 us (6%)
  other arithmetic  10.3 us (5%)
    ppermute x27, waiting for transfers between devices, rotated(): lax.ppermute(array, axis, [(i, (i + by) % size) for i in range(size)])  45.2 us
    ppermute x27, starting transfers between devices, rotated(): lax.ppermute(array, axis, [(i, (i + by) % size) for i in range(size)])  38.8 us
    all_to_all x1, blocking collectives, exchanged(): return lax.all_to_all(pieces, axes, split_axis=0, concat_axis=0, tiled=True)  23.2 us
    pallas_call x1, Pallas kernels, coarse_attention(): pl.pallas_call(attention_kernel, out_shape=jax.ShapeDtypeStruct((rows, HE...  14.7 us
    all_to_all x1, blocking collectives, gathered(): return lax.all_to_all(copies, axes, split_axis=0, concat_axis=0, tiled=True)  14.3 us
    ppermute x2, waiting for transfers between devices, from_behind(): return lax.ppermute(array, axis, pairs)  12.5 us
    all_to_all x2, waiting for transfers between devices, gathered(): return lax.all_to_all(copies, axes, split_axis=0, concat_axis=0, tiled=True)  9.99 us
    all_to_all x2, starting transfers between devices, gathered(): return lax.all_to_all(copies, axes, split_axis=0, concat_axis=0, tiled=True)  9.72 us
  transfers between devices with their start and end apart: 32, of which 18 were waited for; matrix products, arithmetic and copies ran while one was open for 6% of the time, Pallas kernels for 11%

profile of v3, /device:TPU:16, one launch (start us, length us, event | category | flops | bytes accessed | tf_op | source)
XLA Modules:
  0.0 219.2 jit_solution(8702138721085414681)
XLA Ops:
  0.0 1.4 fusion.2
  1.4 1.2 fusion.4.normed_ref
  2.6 1.9 collective-permute-start
  4.6 1.1 fusion.35
  5.8 1.1 copy_bitcast_fusion.1
  6.8 1.7 pad_maximum_fusion
  8.6 4.7 %collective-permute-start.9 = (bf16[1024,256]{1,0:T(8,128)(2,1)}, bf16[1024,256]{1,0:T(8,128)(2,1)}, u32[]{:S(2)}, u32[]{:S(2)}) collective-permute-start(bf16[1024,256]{1,0:T(8,128)(2,1)} %pad_maximum_fusion), channel_id=1, source_target_pairs={{0,0},{16,1},{32,2},{48,3},{64,4},{80,5},{96,6},{112,7},{128,8},{1... | collective-permute-start | bytes 1572872 | tf_op jit(solution)/shard_map/weights/ppermute | solution.py:346
  13.3 0.8 dynamic_slice.27
  14.1 5.3 %collective-permute-done.before_ref = bf16[256,1024]{1,0:T(8,128)(2,1)} collective-permute-done((bf16[256,1024]{1,0:T(8,128)(2,1)S(1)}, bf16[256,1024]{1,0:T(8,128)(2,1)}, u32[]{:S(2)}, u32[]{:S(2)}) %collective-permute-start) | collective-permute-done | bytes 524320 | tf_op jit(solution)/shard_map/ppermute | solution.py:28
  19.4 9.5 %shard_map.109 = (bf16[256,1024]{1,0:T(8,128)(2,1)S(1)}, bf16[32,1024]{1,0:T(8,128)(2,1)S(1)}) custom-call(s32[1]{0:T(128)} %bitcast.first_ref, bf16[256,1024]{1,0:T(8,128)(2,1)S(1)} %copy-done.1, bf16[256,1024]{1,0:T(8,128)(2,1)S(1)} %fusion.4.normed_ref, bf16[256,1024]{1,0:T(8,128)(2,1)} %collective-permute-done.before_ref, bf16[1024,1024]{1,0:T(8,128)(2,1)} %query_ref.1, ...), custom_call_target="tpu_custom_call" | custom-call | tf_op jit(solution)/shard_map/pallas_call | solution.py:111
  28.9 0.8 copy-done.9
  29.7 5.3 %collective-permute-start.1 = (bf16[32,1024]{1,0:T(8,128)(2,1)S(1)}, bf16[32,1024]{1,0:T(8,128)(2,1)S(1)}, u32[]{:S(2)}, u32[]{:S(2)}) collective-permute-start(bf16[32,1024]{1,0:T(8,128)(2,1)S(1)} %get-tuple-element.22), channel_id=1, source_target_pairs={{0,64},{16,80},{32,96},{48,112},{64,0},{80,16},{96,32},{112,48},{1... | collective-permute-start | bytes 196616 | tf_op jit(solution)/shard_map/gather_rows/ppermute | solution.py:33
  35.0 3.0 %collective-permute-done.1 = bf16[32,1024]{1,0:T(8,128)(2,1)S(1)} collective-permute-done((bf16[32,1024]{1,0:T(8,128)(2,1)S(1)}, bf16[32,1024]{1,0:T(8,128)(2,1)S(1)}, u32[]{:S(2)}, u32[]{:S(2)}) %collective-permute-start.1) | collective-permute-done | bytes 65568 | tf_op jit(solution)/shard_map/gather_rows/ppermute | solution.py:33
  38.0 9.6 %collective-permute-start.2 = (bf16[2,32,1024]{2,1,0:T(8,128)(2,1)S(1)}, bf16[2,32,1024]{2,1,0:T(8,128)(2,1)S(1)}, u32[]{:S(2)}, u32[]{:S(2)}) collective-permute-start(bf16[2,32,1024]{2,1,0:T(8,128)(2,1)S(1)} %maximum_select_fusion.1), channel_id=1, source_target_pairs={{0,112},{16,0},{32,16},{48,32},{64,48},{80,64},{96,80},{112,96},{1... | collective-permute-start | bytes 393224 | tf_op jit(solution)/shard_map/gather_rows/ppermute | solution.py:33
  47.6 1.5 collective-permute-start.4
  49.2 1.2 multiply_convert_fusion.pack_ref
  50.5 3.7 %collective-permute-done.2 = bf16[2,32,1024]{2,1,0:T(8,128)(2,1)S(1)} collective-permute-done((bf16[2,32,1024]{2,1,0:T(8,128)(2,1)S(1)}, bf16[2,32,1024]{2,1,0:T(8,128)(2,1)S(1)}, u32[]{:S(2)}, u32[]{:S(2)}) %collective-permute-start.2) | collective-permute-done | bytes 131104 | tf_op jit(solution)/shard_map/gather_rows/ppermute | solution.py:33
  54.2 8.2 %collective-permute-done.3 = bf16[2,32,1024]{2,1,0:T(8,128)(2,1)S(1)} collective-permute-done((bf16[2,32,1024]{2,1,0:T(8,128)(2,1)S(1)}, bf16[2,32,1024]{2,1,0:T(8,128)(2,1)S(1)}, u32[]{:S(2)}, u32[]{:S(2)}) %collective-permute-start.3) | collective-permute-done | bytes 131104 | tf_op jit(solution)/shard_map/gather_rows/ppermute | solution.py:33
  62.5 1.7 weights.1
  64.3 3.1 %collective-permute-done.10 = bf16[4,2,672,128]{3,2,1,0:T(8,128)(2,1)S(1)} collective-permute-done((bf16[4,2,672,128]{3,2,1,0:T(8,128)(2,1)S(1)}, bf16[4,2,672,128]{3,2,1,0:T(8,128)(2,1)S(1)}, u32[]{:S(2)}, u32[]{:S(2)}) %collective-permute-start.10) | collective-permute-done | bytes 1376288 | tf_op jit(solution)/shard_map/weights/ppermute | solution.py:33
  67.7 1.3 collective-permute-start.13
  69.0 2.0 collective-permute-start.11
  71.0 1.4 collective-permute-start.5
  72.4 1.0 collective-permute-start.7
  73.5 6.8 %collective-permute-done.13 = bf16[2,672,128]{2,1,0:T(8,128)(2,1)S(1)} collective-permute-done((bf16[2,672,128]{2,1,0:T(8,128)(2,1)S(1)}, bf16[2,672,128]{2,1,0:T(8,128)(2,1)S(1)}, u32[]{:S(2)}, u32[]{:S(2)}) %collective-permute-start.13) | collective-permute-done | bytes 344096 | tf_op jit(solution)/shard_map/weights/ppermute | solution.py:33
  80.8 6.0 %collective-permute-done.11 = bf16[2,672,128]{2,1,0:T(8,128)(2,1)S(1)} collective-permute-done((bf16[2,672,128]{2,1,0:T(8,128)(2,1)S(1)}, bf16[2,672,128]{2,1,0:T(8,128)(2,1)S(1)}, u32[]{:S(2)}, u32[]{:S(2)}) %collective-permute-start.11) | collective-permute-done | bytes 344096 | tf_op jit(solution)/shard_map/weights/ppermute | solution.py:33
  87.0 1.6 collective-permute-start.14
  88.7 2.1 collective-permute-start.8
  90.8 3.5 %collective-permute-done.14 = bf16[672,128]{1,0:T(8,128)(2,1)S(1)} collective-permute-done((bf16[672,128]{1,0:T(8,128)(2,1)S(1)}, bf16[672,128]{1,0:T(8,128)(2,1)S(1)}, u32[]{:S(2)}, u32[]{:S(2)}) %collective-permute-start.14) | collective-permute-done | bytes 172064 | tf_op jit(solution)/shard_map/weights/ppermute | solution.py:33
  94.4 4.6 %collective-permute-done.6.top_ref = bf16[128,1024]{1,0:T(8,128)(2,1)S(1)} collective-permute-done((bf16[128,1024]{1,0:T(8,128)(2,1)S(1)}, bf16[128,1024]{1,0:T(8,128)(2,1)S(1)}, u32[]{:S(2)}, u32[]{:S(2)}) %collective-permute-start.6) | collective-permute-done | bytes 262176 | tf_op jit(solution)/shard_map/gather_rows/ppermute | solution.py:33
  99.0 0.7 copy-done.11
  99.7 0.7 copy-done.13
  100.5 14.3 %all_to_all.20.near_ref = bf16[4,672,128]{2,1,0:T(8,128)(2,1)S(1)} all-to-all(bf16[4,672,128]{2,1,0:T(8,128)(2,1)S(1)} %broadcast_in_dim.22), channel_id=1, replica_groups=mesh['yh'=2,'z'=8,'x'=4,'yl'=2,'c'=2] {'x'}, dimensions={0} | all-to-all | bytes 1376256 | tf_op jit(solution)/shard_map/weights/all_to_all | solution.py:45
  115.0 2.2 %collective-permute-done.15.far_ref = bf16[4,672,128]{2,1,0:T(8,128)(2,1)} collective-permute-done((bf16[4,672,128]{2,1,0:T(8,128)(2,1)S(1)}, bf16[4,672,128]{2,1,0:T(8,128)(2,1)}, u32[]{:S(2)}, u32[]{:S(2)}) %collective-permute-start.15) | collective-permute-done | bytes 688160 | tf_op jit(solution)/shard_map/weights/ppermute | solution.py:33
  117.2 1.0 copy-done.3
  118.2 1.0 copy-done.5
  119.2 0.9 copy-done.12
  120.2 0.9 copy-done.14
  121.1 4.4 %project.1 = (bf16[1024,256]{1,0:T(8,128)(2,1)}, f32[1024,128]{1,0:T(8,128)S(1)}, f32[4,8,256]{2,1,0:T(8,128)S(1)}, bf16[4,256,32]{2,1,0:T(8,128)(2,1)S(1)}) custom-call(s32[3]{0:T(128)S(1)} %pad_add_fusion.where_ref, bf16[256,1024]{1,0:T(8,128)(2,1)S(1)} %bitcast.120, bf16[256,1024]{1,0:T(8,128)(2,1)S(1)} %copy-done.3, bf16[128,1024]{1,0:T(8,128)(2,1)S(1)} %copy-done.12, ...), custom_call_target="tpu_custom_call" | custom-call | tf_op jit(solution)/shard_map/project/pallas_call | solution.py:302
  125.6 0.8 copy-done.6
  126.4 0.7 copy-done.15
  127.1 1.2 collective-permute-start.18
  128.3 0.9 collective-permute-start.20
  129.1 1.1 collective-permute-start.22
  130.8 6.0 %all-to-all-start.1 = ((f32[8,1,1024]{2,1,0:T(1,128)}), f32[8,1,1024]{2,1,0:T(1,128)S(1)}, u32[]{:S(2)}, u32[]{:S(2)}) async-start(f32[8,1,1024]{2,1,0:T(1,128)} %broadcast_in_dim.23), calls=%async_computation.1 | async-start | bytes 65536 | tf_op jit(solution)/shard_map/project/all_to_all | solution.py:45
  136.8 0.9 broadcast_select_fusion.1
  138.5 0.8 copy_bitcast_fusion
  139.8 5.0 %all-to-all-done.1 = f32[8,1,1024]{2,1,0:T(1,128)S(1)} async-done(((f32[8,1,1024]{2,1,0:T(1,128)}), f32[8,1,1024]{2,1,0:T(1,128)S(1)}, u32[]{:S(2)}, u32[]{:S(2)}) %all-to-all-start.1) | async-done | bytes 32800 | tf_op jit(solution)/shard_map/project/all_to_all | solution.py:45
  145.3 1.2 multiply_convert_fusion.1.q_ref
  146.6 1.6 collective-permute-done.16
  148.8 3.7 %all-to-all-start.2 = ((f32[8,1,1024]{2,1,0:T(1,128)}), f32[8,1,1024]{2,1,0:T(1,128)S(1)}, u32[]{:S(2)}, u32[]{:S(2)}) async-start(f32[8,1,1024]{2,1,0:T(1,128)} %broadcast_in_dim.24), calls=%async_computation.2 | async-start | bytes 65536 | tf_op jit(solution)/shard_map/project/all_to_all | solution.py:45
  153.0 4.9 %all-to-all-done.2 = f32[8,1,1024]{2,1,0:T(1,128)S(1)} async-done(((f32[8,1,1024]{2,1,0:T(1,128)}), f32[8,1,1024]{2,1,0:T(1,128)S(1)}, u32[]{:S(2)}, u32[]{:S(2)}) %all-to-all-start.2) | async-done | bytes 32800 | tf_op jit(solution)/shard_map/project/all_to_all | solution.py:45
  158.8 1.1 collective-permute-start.28
  160.0 1.3 collective-permute-start.26
  161.8 14.7 %attention.1 = bf16[1024,128]{1,0:T(8,128)(2,1)S(1)} custom-call(s32[16]{0:T(128)S(1)} %stack.134.place_ref, bf16[1024,128]{1,0:T(8,128)(2,1)S(1)} %multiply_convert_fusion.1.q_ref, f32[8,1024]{1,0:T(8,128)S(1)} %bitcast.125, bf16[1024,256]{1,0:T(8,128)(2,1)} %get-tuple-element.32.refs_0_, bf16[1024,256]{1,0:T(8,128)(2,1)} %collective-permute-done.17.refs_1_, ...), custom_call_target="tpu_custom_call" | custom-call | tf_op jit(solution)/shard_map/attention/pallas_call | solution.py:180
  176.7 1.5 collective-permute-start.27
  178.2 0.7 collective-permute-start.24
  178.9 3.3 %collective-permute-start.25 = (bf16[256,128]{1,0:T(8,128)(2,1)S(1)}, bf16[256,128]{1,0:T(8,128)(2,1)S(1)}, u32[]{:S(2)}, u32[]{:S(2)}) collective-permute-start(bf16[256,128]{1,0:T(8,128)(2,1)S(1)} %get-tuple-element.42), channel_id=1, source_target_pairs={{0,128},{2,130},{128,0},{130,2},{1,129},{3,131},{129,1},{131,3},{4... | collective-permute-start | bytes 196616 | tf_op jit(solution)/shard_map/lift/ppermute | solution.py:33
  183.0 1.3 convolution_add_fusion.1
  184.6 0.9 collective-permute-done.25
  185.7 23.2 %all_to_all.21 = bf16[8,32,1024]{2,1,0:T(8,128)(2,1)S(1)} all-to-all(bf16[8,32,1024]{2,1,0:T(8,128)(2,1)S(1)} %bitcast.126), channel_id=1, replica_groups=mesh['yh'=2,'z'=8,'x'=4,'yl'=2,'c'=2] {'z'}, dimensions={0} | all-to-all | bytes 1048576 | tf_op jit(solution)/shard_map/lift/all_to_all | solution.py:49
  209.0 1.9 collective-permute-start.29
  211.0 7.2 %collective-permute-done.29 = f32[1,1024]{1,0:T(1,128)S(1)} collective-permute-done((f32[1,1024]{1,0:T(1,128)S(1)}, f32[1,1024]{1,0:T(1,128)S(1)}, u32[]{:S(2)}, u32[]{:S(2)}) %collective-permute-start.29) | collective-permute-done | bytes 4128 | tf_op jit(solution)/shard_map/lift/ppermute | solution.py:28
  218.2 0.9 fusion.5
  (106 shorter events, 8.1 us)
Async XLA Ops:
  0.0 5.7 %copy-start = (bf16[256,4096]{1,0:T(8,128)(2,1)S(1)}, bf16[256,4096]{1,0:T(8,128)(2,1)}, u32[]{:S(2)}) copy-start(bf16[256,4096]{1,0:T(8,128)(2,1)} %param.20) | copy-start | bytes 6291460
  0.0 4.6 %copy-start.19 = (bf16[256,2,256]{2,1,0:T(2,128)(2,1)S(1)}, bf16[256,2,256]{2,1,0:T(2,128)(2,1)}, u32[]{:S(2)}) copy-start(bf16[256,2,256]{2,1,0:T(2,128)(2,1)} %param.19) | copy-start | bytes 786436
  2.6 16.7 %collective-permute-start = (bf16[256,1024]{1,0:T(8,128)(2,1)S(1)}, bf16[256,1024]{1,0:T(8,128)(2,1)}, u32[]{:S(2)}, u32[]{:S(2)}) collective-permute-start(bf16[256,1024]{1,0:T(8,128)(2,1)S(1)} %fusion.4.normed_ref), channel_id=1, source_target_pairs={{0,1},{1,2},{2,3},{3,4},{4,5},{5,6},{6,7},{7,8},{8,9},{9,10},{10,1... | collective-permute-start | bytes 1572872 | tf_op jit(solution)/shard_map/ppermute | solution.py:28
  4.6 14.8 %copy-start.1 = (bf16[256,1024]{1,0:T(8,128)(2,1)S(1)}, bf16[256,1024]{1,0:T(8,128)(2,1)}, u32[]{:S(2)}) copy-start(bf16[256,1024]{1,0:T(8,128)(2,1)} %tokens_ref.1) | copy-start | bytes 1572868
  8.6 40.6 %collective-permute-start.9 = (bf16[1024,256]{1,0:T(8,128)(2,1)}, bf16[1024,256]{1,0:T(8,128)(2,1)}, u32[]{:S(2)}, u32[]{:S(2)}) collective-permute-start(bf16[1024,256]{1,0:T(8,128)(2,1)} %pad_maximum_fusion), channel_id=1, source_target_pairs={{0,0},{16,1},{32,2},{48,3},{64,4},{80,5},{96,6},{112,7},{128,8},{1... | collective-permute-start | bytes 1572872 | tf_op jit(solution)/shard_map/weights/ppermute | solution.py:346
  28.9 0.8 copy-start.9
  29.7 8.3 %collective-permute-start.1 = (bf16[32,1024]{1,0:T(8,128)(2,1)S(1)}, bf16[32,1024]{1,0:T(8,128)(2,1)S(1)}, u32[]{:S(2)}, u32[]{:S(2)}) collective-permute-start(bf16[32,1024]{1,0:T(8,128)(2,1)S(1)} %get-tuple-element.22), channel_id=1, source_target_pairs={{0,64},{16,80},{32,96},{48,112},{64,0},{80,16},{96,32},{112,48},{1... | collective-permute-start | bytes 196616 | tf_op jit(solution)/shard_map/gather_rows/ppermute | solution.py:33
  38.0 16.1 %collective-permute-start.2 = (bf16[2,32,1024]{2,1,0:T(8,128)(2,1)S(1)}, bf16[2,32,1024]{2,1,0:T(8,128)(2,1)S(1)}, u32[]{:S(2)}, u32[]{:S(2)}) collective-permute-start(bf16[2,32,1024]{2,1,0:T(8,128)(2,1)S(1)} %maximum_select_fusion.1), channel_id=1, source_target_pairs={{0,112},{16,0},{32,16},{48,32},{64,48},{80,64},{96,80},{112,96},{1... | collective-permute-start | bytes 393224 | tf_op jit(solution)/shard_map/gather_rows/ppermute | solution.py:33
  47.6 14.7 %collective-permute-start.3 = (bf16[2,32,1024]{2,1,0:T(8,128)(2,1)S(1)}, bf16[2,32,1024]{2,1,0:T(8,128)(2,1)S(1)}, u32[]{:S(2)}, u32[]{:S(2)}) collective-permute-start(bf16[2,32,1024]{2,1,0:T(8,128)(2,1)S(1)} %maximum_select_fusion.1), channel_id=1, source_target_pairs={{0,96},{16,112},{32,0},{48,16},{64,32},{80,48},{96,64},{112,80},{1... | collective-permute-start | bytes 393224 | tf_op jit(solution)/shard_map/gather_rows/ppermute | solution.py:33
  47.6 14.8 %collective-permute-start.4 = (bf16[2,32,1024]{2,1,0:T(8,128)(2,1)S(1)}, bf16[2,32,1024]{2,1,0:T(8,128)(2,1)S(1)}, u32[]{:S(2)}, u32[]{:S(2)}) collective-permute-start(bf16[2,32,1024]{2,1,0:T(8,128)(2,1)S(1)} %maximum_select_fusion.1), channel_id=1, source_target_pairs={{0,16},{16,32},{32,48},{48,64},{64,80},{80,96},{96,112},{112,0},{1... | collective-permute-start | bytes 393224 | tf_op jit(solution)/shard_map/gather_rows/ppermute | solution.py:33
  50.4 12.1 %copy-start.7 = (bf16[1024,256]{1,0:T(8,128)(2,1)S(1)}, bf16[1024,256]{1,0:T(8,128)(2,1)}, u32[]{:S(2)}) copy-start(bf16[1024,256]{1,0:T(8,128)(2,1)} %down_ref.1) | copy-start | bytes 1572868
  50.5 12.1 %copy-start.8 = (bf16[256,1024]{1,0:T(8,128)(2,1)S(1)}, bf16[256,1024]{1,0:T(8,128)(2,1)}, u32[]{:S(2)}) copy-start(bf16[256,1024]{1,0:T(8,128)(2,1)} %up_ref.1) | copy-start | bytes 1572868
  64.2 3.2 %collective-permute-start.10 = (bf16[4,2,672,128]{3,2,1,0:T(8,128)(2,1)S(1)}, bf16[4,2,672,128]{3,2,1,0:T(8,128)(2,1)S(1)}, u32[]{:S(2)}, u32[]{:S(2)}) collective-permute-start(bf16[4,2,672,128]{3,2,1,0:T(8,128)(2,1)S(1)} %get-tuple-element.27), channel_id=1, source_target_pairs={{0,1},{1,0},{2,3},{3,2},{4,5},{5,4},{6,7},{7,6},{8,9},{9,8},{10,11... | collective-permute-start | bytes 4128776 | tf_op jit(solution)/shard_map/weights/ppermute | solution.py:33
  67.7 12.5 %collective-permute-start.13 = (bf16[2,672,128]{2,1,0:T(8,128)(2,1)S(1)}, bf16[2,672,128]{2,1,0:T(8,128)(2,1)S(1)}, u32[]{:S(2)}, u32[]{:S(2)}) collective-permute-start(bf16[2,672,128]{2,1,0:T(8,128)(2,1)S(1)} %get-tuple-element.38), channel_id=1, source_target_pairs={{0,8},{4,12},{8,0},{12,4},{1,9},{5,13},{9,1},{13,5},{2,10},{6,14},... | collective-permute-start | bytes 1032200 | tf_op jit(solution)/shard_map/weights/ppermute | solution.py:33
  69.0 11.8 %collective-permute-start.12 = (bf16[2,672,128]{2,1,0:T(8,128)(2,1)S(1)}, bf16[2,672,128]{2,1,0:T(8,128)(2,1)S(1)}, u32[]{:S(2)}, u32[]{:S(2)}) collective-permute-start(bf16[2,672,128]{2,1,0:T(8,128)(2,1)S(1)} %get-tuple-element.39), channel_id=1, source_target_pairs={{0,12},{4,0},{8,4},{12,8},{1,13},{5,1},{9,5},{13,9},{2,14},{6,2},{... | collective-permute-start | bytes 1032200 | tf_op jit(solution)/shard_map/weights/ppermute | solution.py:33
  69.0 17.8 %collective-permute-start.11 = (bf16[2,672,128]{2,1,0:T(8,128)(2,1)S(1)}, bf16[2,672,128]{2,1,0:T(8,128)(2,1)S(1)}, u32[]{:S(2)}, u32[]{:S(2)}) collective-permute-start(bf16[2,672,128]{2,1,0:T(8,128)(2,1)S(1)} %get-tuple-element.37), channel_id=1, source_target_pairs={{0,4},{4,8},{8,12},{12,0},{1,5},{5,9},{9,13},{13,1},{2,6},{6,10},{... | collective-permute-start | bytes 1032200 | tf_op jit(solution)/shard_map/weights/ppermute | solution.py:33
  71.0 17.6 %collective-permute-start.5 = (bf16[256,1024]{1,0:T(8,128)(2,1)S(1)}, bf16[256,1024]{1,0:T(8,128)(2,1)S(1)}, u32[]{:S(2)}, u32[]{:S(2)}) collective-permute-start(bf16[256,1024]{1,0:T(8,128)(2,1)S(1)} %bitcast.118), channel_id=1, source_target_pairs={{0,130},{2,0},{128,2},{130,128},{1,131},{3,1},{129,3},{131,129},{4... | collective-permute-start | bytes 1572872 | tf_op jit(solution)/shard_map/gather_rows/ppermute | solution.py:33
  72.4 16.3 %collective-permute-start.7 = (bf16[256,1024]{1,0:T(8,128)(2,1)S(1)}, bf16[256,1024]{1,0:T(8,128)(2,1)S(1)}, u32[]{:S(2)}, u32[]{:S(2)}) collective-permute-start(bf16[256,1024]{1,0:T(8,128)(2,1)S(1)} %bitcast.119), channel_id=1, source_target_pairs={{0,2},{2,128},{128,130},{130,0},{1,3},{3,129},{129,131},{131,1},{4... | collective-permute-start | bytes 1572872 | tf_op jit(solution)/shard_map/gather_rows/ppermute | solution.py:33
  87.0 7.3 %collective-permute-start.14 = (bf16[672,128]{1,0:T(8,128)(2,1)S(1)}, bf16[672,128]{1,0:T(8,128)(2,1)S(1)}, u32[]{:S(2)}, u32[]{:S(2)}) collective-permute-start(bf16[672,128]{1,0:T(8,128)(2,1)S(1)} %fusion.13), channel_id=1, source_target_pairs={{0,2},{2,0},{1,3},{3,1},{4,6},{6,4},{5,7},{7,5},{8,10},{10,8},{9,1... | collective-permute-start | bytes 516104 | tf_op jit(solution)/shard_map/weights/ppermute | solution.py:33
  88.6 11.1 %copy-start.2 = (bf16[256,1024]{1,0:T(8,128)(2,1)}, bf16[256,1024]{1,0:T(8,128)(2,1)S(1)}, u32[]{:S(2)}) copy-start(bf16[256,1024]{1,0:T(8,128)(2,1)S(1)} %collective-permute-done.5.above_ref) | copy-start | bytes 1572868
  88.6 10.4 %collective-permute-start.6 = (bf16[128,1024]{1,0:T(8,128)(2,1)S(1)}, bf16[128,1024]{1,0:T(8,128)(2,1)S(1)}, u32[]{:S(2)}, u32[]{:S(2)}) collective-permute-start(bf16[128,1024]{1,0:T(8,128)(2,1)S(1)} %slice.103), channel_id=1, source_target_pairs={{0,130},{2,0},{128,2},{130,128},{1,131},{3,1},{129,3},{131,129},{4... | collective-permute-start | bytes 786440 | tf_op jit(solution)/shard_map/gather_rows/ppermute | solution.py:33
  88.7 26.2 %copy-start.4 = (bf16[256,1024]{1,0:T(8,128)(2,1)}, bf16[256,1024]{1,0:T(8,128)(2,1)S(1)}, u32[]{:S(2)}) copy-start(bf16[256,1024]{1,0:T(8,128)(2,1)S(1)} %collective-permute-done.7.below_ref) | copy-start | bytes 1572868
  88.7 11.0 %collective-permute-start.8 = (bf16[128,1024]{1,0:T(8,128)(2,1)S(1)}, bf16[128,1024]{1,0:T(8,128)(2,1)S(1)}, u32[]{:S(2)}, u32[]{:S(2)}) collective-permute-start(bf16[128,1024]{1,0:T(8,128)(2,1)S(1)} %slice.104), channel_id=1, source_target_pairs={{0,2},{2,128},{128,130},{130,0},{1,3},{3,129},{129,131},{131,1},{4... | collective-permute-start | bytes 786440 | tf_op jit(solution)/shard_map/gather_rows/ppermute | solution.py:33
  99.0 0.7 copy-start.11
  99.7 0.7 copy-start.13
  114.9 2.3 %collective-permute-start.15 = (bf16[4,672,128]{2,1,0:T(8,128)(2,1)S(1)}, bf16[4,672,128]{2,1,0:T(8,128)(2,1)}, u32[]{:S(2)}, u32[]{:S(2)}) collective-permute-start(bf16[4,672,128]{2,1,0:T(8,128)(2,1)S(1)} %all_to_all.20.near_ref), channel_id=1, source_target_pairs={{0,1},{1,0},{2,3},{3,2},{4,5},{5,4},{6,7},{7,6},{8,9},{9,8},{10,11... | collective-permute-start | bytes 2064392 | tf_op jit(solution)/shard_map/weights/ppermute | solution.py:33
  117.2 1.0 copy-start.3
  118.2 1.0 copy-start.5
  119.2 0.9 copy-start.12
  120.2 0.9 copy-start.14
  125.6 0.8 copy-start.6
  126.4 0.7 copy-start.15
  127.1 30.9 %collective-permute-start.18 = (bf16[1024,256]{1,0:T(8,128)(2,1)}, bf16[1024,256]{1,0:T(8,128)(2,1)S(1)}, u32[]{:S(2)}, u32[]{:S(2)}) collective-permute-start(bf16[1024,256]{1,0:T(8,128)(2,1)} %get-tuple-element.32.refs_0_), channel_id=1, source_target_pairs={{0,12},{4,0},{8,4},{12,8},{1,13},{5,1},{9,5},{13,9},{2,14},{6,2},{... | collective-permute-start | bytes 1572872 | tf_op jit(solution)/shard_map/project/ppermute | solution.py:33
  128.3 29.9 %collective-permute-start.20 = (bf16[1024,256]{1,0:T(8,128)(2,1)}, bf16[1024,256]{1,0:T(8,128)(2,1)}, u32[]{:S(2)}, u32[]{:S(2)}) collective-permute-start(bf16[1024,256]{1,0:T(8,128)(2,1)} %get-tuple-element.32.refs_0_), channel_id=1, source_target_pairs={{0,4},{4,8},{8,12},{12,0},{1,5},{5,9},{9,13},{13,1},{2,6},{6,10},{... | collective-permute-start | bytes 1572872 | tf_op jit(solution)/shard_map/project/ppermute | solution.py:33
  129.1 29.5 %collective-permute-start.22 = (bf16[1024,256]{1,0:T(8,128)(2,1)}, bf16[1024,256]{1,0:T(8,128)(2,1)}, u32[]{:S(2)}, u32[]{:S(2)}) collective-permute-start(bf16[1024,256]{1,0:T(8,128)(2,1)} %get-tuple-element.32.refs_0_), channel_id=1, source_target_pairs={{0,8},{4,12},{8,0},{12,4},{1,9},{5,13},{9,1},{13,5},{2,10},{6,14},... | collective-permute-start | bytes 1572872 | tf_op jit(solution)/shard_map/project/ppermute | solution.py:33
  130.8 14.0 %all-to-all-start.1 = ((f32[8,1,1024]{2,1,0:T(1,128)}), f32[8,1,1024]{2,1,0:T(1,128)S(1)}, u32[]{:S(2)}, u32[]{:S(2)}) async-start(f32[8,1,1024]{2,1,0:T(1,128)} %broadcast_in_dim.23), calls=%async_computation.1 | async-start | bytes 65536 | tf_op jit(solution)/shard_map/project/all_to_all | solution.py:45
  137.8 0.7 copy-start.17
  137.8 22.2 %copy-start.16 = (bf16[4,256,32]{2,1,0:T(8,128)(2,1)S(1)}, bf16[4,256,32]{2,1,0:T(8,128)(2,1)}, u32[]{:S(2)}) copy-start(bf16[4,256,32]{2,1,0:T(8,128)(2,1)} %copy-done.15) | copy-start | bytes 196612
  139.2 9.0 %collective-permute-start.16 = (bf16[160,1024]{1,0:T(8,128)(2,1)}, bf16[160,1024]{1,0:T(8,128)(2,1)}, u32[]{:S(2)}, u32[]{:S(2)}) collective-permute-start(bf16[160,1024]{1,0:T(8,128)(2,1)} %copy_bitcast_fusion), channel_id=1, source_target_pairs={{0,2},{2,128},{128,130},{130,0},{1,3},{3,129},{129,131},{131,1},{4... | collective-permute-start | bytes 983048 | tf_op jit(solution)/shard_map/weights/ppermute | solution.py:33
  148.8 9.2 %all-to-all-start.2 = ((f32[8,1,1024]{2,1,0:T(1,128)}), f32[8,1,1024]{2,1,0:T(1,128)S(1)}, u32[]{:S(2)}, u32[]{:S(2)}) async-start(f32[8,1,1024]{2,1,0:T(1,128)} %broadcast_in_dim.24), calls=%async_computation.2 | async-start | bytes 65536 | tf_op jit(solution)/shard_map/project/all_to_all | solution.py:45
  152.5 7.4 %collective-permute-start.17 = (bf16[1024,256]{1,0:T(8,128)(2,1)}, bf16[1024,256]{1,0:T(8,128)(2,1)}, u32[]{:S(2)}, u32[]{:S(2)}) collective-permute-start(bf16[1024,256]{1,0:T(8,128)(2,1)} %get-tuple-element.32.refs_0_), channel_id=1, source_target_pairs={{0,1},{1,0},{2,3},{3,2},{4,5},{5,4},{6,7},{7,6},{8,9},{9,8},{10,11... | collective-permute-start | bytes 1572872 | tf_op jit(solution)/shard_map/attention/ppermute | solution.py:33
  158.0 3.3 %collective-permute-start.19 = (bf16[1024,256]{1,0:T(8,128)(2,1)S(1)}, bf16[1024,256]{1,0:T(8,128)(2,1)}, u32[]{:S(2)}, u32[]{:S(2)}) collective-permute-start(bf16[1024,256]{1,0:T(8,128)(2,1)S(1)} %collective-permute-done.18.refs_2_), channel_id=1, source_target_pairs={{0,1},{1,0},{2,3},{3,2},{4,5},{5,4},{6,7},{7,6},{8,9},{9,8},{10,11... | collective-permute-start | bytes 1572872 | tf_op jit(solution)/shard_map/attention/ppermute | solution.py:33
  158.1 3.1 %collective-permute-start.21 = (bf16[1024,256]{1,0:T(8,128)(2,1)}, bf16[1024,256]{1,0:T(8,128)(2,1)}, u32[]{:S(2)}, u32[]{:S(2)}) collective-permute-start(bf16[1024,256]{1,0:T(8,128)(2,1)} %collective-permute-done.20.refs_4_), channel_id=1, source_target_pairs={{0,1},{1,0},{2,3},{3,2},{4,5},{5,4},{6,7},{7,6},{8,9},{9,8},{10,11... | collective-permute-start | bytes 1572872 | tf_op jit(solution)/shard_map/attention/ppermute | solution.py:33
  158.6 3.2 %collective-permute-start.23 = (bf16[1024,256]{1,0:T(8,128)(2,1)}, bf16[1024,256]{1,0:T(8,128)(2,1)}, u32[]{:S(2)}, u32[]{:S(2)}) collective-permute-start(bf16[1024,256]{1,0:T(8,128)(2,1)} %collective-permute-done.22.refs_6_), channel_id=1, source_target_pairs={{0,1},{1,0},{2,3},{3,2},{4,5},{5,4},{6,7},{7,6},{8,9},{9,8},{10,11... | collective-permute-start | bytes 1572872 | tf_op jit(solution)/shard_map/attention/ppermute | solution.py:33
  158.8 25.4 %collective-permute-start.28 = (bf16[160,1024]{1,0:T(8,128)(2,1)}, bf16[160,1024]{1,0:T(8,128)(2,1)S(1)}, u32[]{:S(2)}, u32[]{:S(2)}) collective-permute-start(bf16[160,1024]{1,0:T(8,128)(2,1)} %copy_bitcast_fusion), channel_id=1, source_target_pairs={{0,130},{2,0},{128,2},{130,128},{1,131},{3,1},{129,3},{131,129},{4... | collective-permute-start | bytes 983048 | tf_op jit(solution)/shard_map/weights/ppermute | solution.py:33
  160.0 22.2 %copy-start.18 = (bf16[4,160,128]{2,1,0:T(8,128)(2,1)S(1)}, bf16[4,160,128]{2,1,0:T(8,128)(2,1)}, u32[]{:S(2)}) copy-start(bf16[4,160,128]{2,1,0:T(8,128)(2,1)} %copy-done.17) | copy-start | bytes 491524
  160.0 24.6 %collective-permute-start.26 = (bf16[160,1024]{1,0:T(8,128)(2,1)}, bf16[160,1024]{1,0:T(8,128)(2,1)S(1)}, u32[]{:S(2)}, u32[]{:S(2)}) collective-permute-start(bf16[160,1024]{1,0:T(8,128)(2,1)} %collective-permute-done.16), channel_id=1, source_target_pairs={{0,2},{2,128},{128,130},{130,0},{1,3},{3,129},{129,131},{131,1},{4... | collective-permute-start | bytes 983048 | tf_op jit(solution)/shard_map/weights/ppermute | solution.py:33
  176.7 7.6 %collective-permute-start.27 = (bf16[256,128]{1,0:T(8,128)(2,1)S(1)}, bf16[256,128]{1,0:T(8,128)(2,1)S(1)}, u32[]{:S(2)}, u32[]{:S(2)}) collective-permute-start(bf16[256,128]{1,0:T(8,128)(2,1)S(1)} %get-tuple-element.43), channel_id=1, source_target_pairs={{0,130},{2,0},{128,2},{130,128},{1,131},{3,1},{129,3},{131,129},{4... | collective-permute-start | bytes 196616 | tf_op jit(solution)/shard_map/lift/ppermute | solution.py:33
  178.2 4.8 %collective-permute-start.24 = (bf16[256,128]{1,0:T(8,128)(2,1)S(1)}, bf16[256,128]{1,0:T(8,128)(2,1)S(1)}, u32[]{:S(2)}, u32[]{:S(2)}) collective-permute-start(bf16[256,128]{1,0:T(8,128)(2,1)S(1)} %get-tuple-element.44), channel_id=1, source_target_pairs={{0,2},{2,128},{128,130},{130,0},{1,3},{3,129},{129,131},{131,1},{4... | collective-permute-start | bytes 196616 | tf_op jit(solution)/shard_map/lift/ppermute | solution.py:33
  178.9 6.6 %collective-permute-start.25 = (bf16[256,128]{1,0:T(8,128)(2,1)S(1)}, bf16[256,128]{1,0:T(8,128)(2,1)S(1)}, u32[]{:S(2)}, u32[]{:S(2)}) collective-permute-start(bf16[256,128]{1,0:T(8,128)(2,1)S(1)} %get-tuple-element.42), channel_id=1, source_target_pairs={{0,128},{2,130},{128,0},{130,2},{1,129},{3,131},{129,1},{131,3},{4... | collective-permute-start | bytes 196616 | tf_op jit(solution)/shard_map/lift/ppermute | solution.py:33
  185.7 32.5 %copy-start.10 = (bf16[256,1024]{1,0:T(8,128)(2,1)S(1)}, bf16[256,1024]{1,0:T(8,128)(2,1)}, u32[]{:S(2)}) copy-start(bf16[256,1024]{1,0:T(8,128)(2,1)} %copy-done.9) | copy-start | bytes 1572868
  209.0 9.1 %collective-permute-start.29 = (f32[1,1024]{1,0:T(1,128)S(1)}, f32[1,1024]{1,0:T(1,128)S(1)}, u32[]{:S(2)}, u32[]{:S(2)}) collective-permute-start(f32[1,1024]{1,0:T(1,128)S(1)} %slice.113), channel_id=1, source_target_pairs={{0,1},{1,2},{2,3},{3,4},{4,5},{5,6},{6,7},{7,8},{8,9},{9,10},{10,1... | collective-permute-start | bytes 12296 | tf_op jit(solution)/shard_map/lift/ppermute | solution.py:28

commit v4 on v3

--- a/solution.py
+++ b/solution.py
@@ -311,7 +311,7 @@
         out_specs=(whole, whole, whole, whole),
         scratch_shapes=[pltpu.VMEM((width, 4 * HEAD), bf16)],
         compiler_params=pltpu.CompilerParams(vmem_limit_bytes=40 << 20),
-    )(where, *rows, near, far)
+    )(where, *[in_hbm(r) for r in rows], near, far)
 
 
 def body(

time: 220 us -> 214 us (0.973)
  local copies, waits for them, and re-layouts: 13.6 us -> 9.16 us
    unnamed x45 -> x47, local copies, waits for them, and re-layouts: 8.49 us -> 3.13 us
  transfers between devices with their start and end apart: 32 -> 32, of which waited for: 18 -> 16; matrix products, arithmetic and copies ran while one was open for 6% -> 5% of each run, Pallas kernels for 11% -> 11%
where the time goes in v4:
time: 214 us; the launch traced here: 213 us
  waiting for transfers between devices  66.9 us (31%)
  starting transfers between devices  57.9 us (27%)
  blocking collectives  37.7 us (18%)
  Pallas kernels  30.5 us (14%)
  local copies, waits for them, and re-layouts  9.16 us (4%)
  other arithmetic  8.67 us (4%)
    ppermute x27, waiting for transfers between devices, rotated(): lax.ppermute(array, axis, [(i, (i + by) % size) for i in range(size)])  43.6 us
    ppermute x27, starting transfers between devices, rotated(): lax.ppermute(array, axis, [(i, (i + by) % size) for i in range(size)])  39.7 us
    all_to_all x1, blocking collectives, exchanged(): return lax.all_to_all(pieces, axes, split_axis=0, concat_axis=0, tiled=True)  23.4 us
    pallas_call x1, Pallas kernels, coarse_attention(): pl.pallas_call(attention_kernel, out_shape=jax.ShapeDtypeStruct((rows, HE...  14.5 us
    all_to_all x1, blocking collectives, gathered(): return lax.all_to_all(copies, axes, split_axis=0, concat_axis=0, tiled=True)  14.3 us
    ppermute x2, waiting for transfers between devices, from_behind(): return lax.ppermute(array, axis, pairs)  12.5 us
    all_to_all x2, waiting for transfers between devices, gathered(): return lax.all_to_all(copies, axes, split_axis=0, concat_axis=0, tiled=True)  10.8 us
    all_to_all x2, starting transfers between devices, gathered(): return lax.all_to_all(copies, axes, split_axis=0, concat_axis=0, tiled=True)  9.72 us
  transfers between devices with their start and end apart: 32, of which 16 were waited for; matrix products, arithmetic and copies ran while one was open for 5% of the time, Pallas kernels for 11%

profile of v4, /device:TPU:16, one launch (start us, length us, event | category | flops | bytes accessed | tf_op | source)
XLA Modules:
  0.0 212.7 jit_solution(8984000118906413449)
XLA Ops:
  0.0 1.4 fusion.2
  1.4 1.2 fusion.4.normed_ref
  2.6 1.9 collective-permute-start
  4.6 1.1 fusion.35
  5.8 1.1 copy_bitcast_fusion.1
  6.8 1.7 pad_maximum_fusion
  8.6 4.7 %collective-permute-start.9 = (bf16[1024,256]{1,0:T(8,128)(2,1)}, bf16[1024,256]{1,0:T(8,128)(2,1)}, u32[]{:S(2)}, u32[]{:S(2)}) collective-permute-start(bf16[1024,256]{1,0:T(8,128)(2,1)} %pad_maximum_fusion), channel_id=1, source_target_pairs={{0,0},{16,1},{32,2},{48,3},{64,4},{80,5},{96,6},{112,7},{128,8},{1... | collective-permute-start | bytes 1572872 | tf_op jit(solution)/shard_map/weights/ppermute | solution.py:346
  13.3 0.8 dynamic_slice.27
  14.1 5.3 %collective-permute-done.before_ref = bf16[256,1024]{1,0:T(8,128)(2,1)} collective-permute-done((bf16[256,1024]{1,0:T(8,128)(2,1)S(1)}, bf16[256,1024]{1,0:T(8,128)(2,1)}, u32[]{:S(2)}, u32[]{:S(2)}) %collective-permute-start) | collective-permute-done | bytes 524320 | tf_op jit(solution)/shard_map/ppermute | solution.py:28
  19.4 9.5 %shard_map.109 = (bf16[256,1024]{1,0:T(8,128)(2,1)S(1)}, bf16[32,1024]{1,0:T(8,128)(2,1)S(1)}) custom-call(s32[1]{0:T(128)} %bitcast.first_ref, bf16[256,1024]{1,0:T(8,128)(2,1)S(1)} %copy-done.1, bf16[256,1024]{1,0:T(8,128)(2,1)S(1)} %fusion.4.normed_ref, bf16[256,1024]{1,0:T(8,128)(2,1)} %collective-permute-done.before_ref, bf16[1024,1024]{1,0:T(8,128)(2,1)} %query_ref.1, ...), custom_call_target="tpu_custom_call" | custom-call | tf_op jit(solution)/shard_map/pallas_call | solution.py:111
  28.9 0.8 copy-done.5
  29.7 5.3 %collective-permute-start.1 = (bf16[32,1024]{1,0:T(8,128)(2,1)S(1)}, bf16[32,1024]{1,0:T(8,128)(2,1)S(1)}, u32[]{:S(2)}, u32[]{:S(2)}) collective-permute-start(bf16[32,1024]{1,0:T(8,128)(2,1)S(1)} %get-tuple-element.22), channel_id=1, source_target_pairs={{0,64},{16,80},{32,96},{48,112},{64,0},{80,16},{96,32},{112,48},{1... | collective-permute-start | bytes 196616 | tf_op jit(solution)/shard_map/gather_rows/ppermute | solution.py:33
  35.0 3.0 %collective-permute-done.1 = bf16[32,1024]{1,0:T(8,128)(2,1)S(1)} collective-permute-done((bf16[32,1024]{1,0:T(8,128)(2,1)S(1)}, bf16[32,1024]{1,0:T(8,128)(2,1)S(1)}, u32[]{:S(2)}, u32[]{:S(2)}) %collective-permute-start.1) | collective-permute-done | bytes 65568 | tf_op jit(solution)/shard_map/gather_rows/ppermute | solution.py:33
  38.0 9.6 %collective-permute-start.2 = (bf16[2,32,1024]{2,1,0:T(8,128)(2,1)S(1)}, bf16[2,32,1024]{2,1,0:T(8,128)(2,1)S(1)}, u32[]{:S(2)}, u32[]{:S(2)}) collective-permute-start(bf16[2,32,1024]{2,1,0:T(8,128)(2,1)S(1)} %maximum_select_fusion.1), channel_id=1, source_target_pairs={{0,112},{16,0},{32,16},{48,32},{64,48},{80,64},{96,80},{112,96},{1... | collective-permute-start | bytes 393224 | tf_op jit(solution)/shard_map/gather_rows/ppermute | solution.py:33
  47.6 1.5 collective-permute-start.4
  49.2 1.2 multiply_convert_fusion.pack_ref
  50.5 3.7 %collective-permute-done.2 = bf16[2,32,1024]{2,1,0:T(8,128)(2,1)S(1)} collective-permute-done((bf16[2,32,1024]{2,1,0:T(8,128)(2,1)S(1)}, bf16[2,32,1024]{2,1,0:T(8,128)(2,1)S(1)}, u32[]{:S(2)}, u32[]{:S(2)}) %collective-permute-start.2) | collective-permute-done | bytes 131104 | tf_op jit(solution)/shard_map/gather_rows/ppermute | solution.py:33
  54.1 8.2 %collective-permute-done.3 = bf16[2,32,1024]{2,1,0:T(8,128)(2,1)S(1)} collective-permute-done((bf16[2,32,1024]{2,1,0:T(8,128)(2,1)S(1)}, bf16[2,32,1024]{2,1,0:T(8,128)(2,1)S(1)}, u32[]{:S(2)}, u32[]{:S(2)}) %collective-permute-start.3) | collective-permute-done | bytes 131104 | tf_op jit(solution)/shard_map/gather_rows/ppermute | solution.py:33
  62.5 1.7 weights.1
  64.3 3.1 %collective-permute-done.10 = bf16[4,2,672,128]{3,2,1,0:T(8,128)(2,1)S(1)} collective-permute-done((bf16[4,2,672,128]{3,2,1,0:T(8,128)(2,1)S(1)}, bf16[4,2,672,128]{3,2,1,0:T(8,128)(2,1)S(1)}, u32[]{:S(2)}, u32[]{:S(2)}) %collective-permute-start.10) | collective-permute-done | bytes 1376288 | tf_op jit(solution)/shard_map/weights/ppermute | solution.py:33
  67.7 1.3 collective-permute-start.13
  68.9 2.0 collective-permute-start.11
  71.0 1.4 collective-permute-start.5
  72.4 1.3 collective-permute-start.7
  73.7 6.5 %collective-permute-done.13 = bf16[2,672,128]{2,1,0:T(8,128)(2,1)S(1)} collective-permute-done((bf16[2,672,128]{2,1,0:T(8,128)(2,1)S(1)}, bf16[2,672,128]{2,1,0:T(8,128)(2,1)S(1)}, u32[]{:S(2)}, u32[]{:S(2)}) %collective-permute-start.13) | collective-permute-done | bytes 344096 | tf_op jit(solution)/shard_map/weights/ppermute | solution.py:33
  80.2 0.5 collective-permute-done.12
  80.7 6.0 %collective-permute-done.11 = bf16[2,672,128]{2,1,0:T(8,128)(2,1)S(1)} collective-permute-done((bf16[2,672,128]{2,1,0:T(8,128)(2,1)S(1)}, bf16[2,672,128]{2,1,0:T(8,128)(2,1)S(1)}, u32[]{:S(2)}, u32[]{:S(2)}) %collective-permute-start.11) | collective-permute-done | bytes 344096 | tf_op jit(solution)/shard_map/weights/ppermute | solution.py:33
  87.0 1.6 collective-permute-start.14
  88.8 2.1 collective-permute-start.8
  90.8 3.5 %collective-permute-done.14 = bf16[672,128]{1,0:T(8,128)(2,1)S(1)} collective-permute-done((bf16[672,128]{1,0:T(8,128)(2,1)S(1)}, bf16[672,128]{1,0:T(8,128)(2,1)S(1)}, u32[]{:S(2)}, u32[]{:S(2)}) %collective-permute-start.14) | collective-permute-done | bytes 172064 | tf_op jit(solution)/shard_map/weights/ppermute | solution.py:33
  94.4 4.6 %collective-permute-done.6.top_ref = bf16[128,1024]{1,0:T(8,128)(2,1)S(1)} collective-permute-done((bf16[128,1024]{1,0:T(8,128)(2,1)S(1)}, bf16[128,1024]{1,0:T(8,128)(2,1)S(1)}, u32[]{:S(2)}, u32[]{:S(2)}) %collective-permute-start.6) | collective-permute-done | bytes 262176 | tf_op jit(solution)/shard_map/gather_rows/ppermute | solution.py:33
  99.1 14.3 %all_to_all.20.near_ref = bf16[4,672,128]{2,1,0:T(8,128)(2,1)S(1)} all-to-all(bf16[4,672,128]{2,1,0:T(8,128)(2,1)S(1)} %broadcast_in_dim.22), channel_id=1, replica_groups=mesh['yh'=2,'z'=8,'x'=4,'yl'=2,'c'=2] {'x'}, dimensions={0} | all-to-all | bytes 1376256 | tf_op jit(solution)/shard_map/weights/all_to_all | solution.py:45
  113.7 2.0 collective-permute-done.15.far_ref
  115.7 4.9 %project.1 = (bf16[1024,256]{1,0:T(8,128)(2,1)}, f32[1024,128]{1,0:T(8,128)S(1)}, f32[4,8,256]{2,1,0:T(8,128)S(1)}, bf16[4,256,32]{2,1,0:T(8,128)(2,1)S(1)}) custom-call(s32[3]{0:T(128)S(1)} %pad_add_fusion.where_ref, bf16[256,1024]{1,0:T(8,128)(2,1)} %bitcast.126, bf16[256,1024]{1,0:T(8,128)(2,1)} %copy-done.13, bf16[128,1024]{1,0:T(8,128)(2,1)} %copy-done.19, ...), custom_call_target="tpu_custom_call" | custom-call | tf_op jit(solution)/shard_map/project/pallas_call | solution.py:302
  120.6 0.8 copy-done.2
  121.4 0.7 copy-done.7
  122.1 1.2 collective-permute-start.18
  123.2 0.9 collective-permute-start.20
  124.1 1.1 collective-permute-start.22
  125.2 0.6 broadcast_in_dim.23
  125.8 6.0 %all-to-all-start.1 = ((f32[8,1,1024]{2,1,0:T(1,128)}), f32[8,1,1024]{2,1,0:T(1,128)S(1)}, u32[]{:S(2)}, u32[]{:S(2)}) async-start(f32[8,1,1024]{2,1,0:T(1,128)} %broadcast_in_dim.23), calls=%async_computation.1 | async-start | bytes 65536 | tf_op jit(solution)/shard_map/project/all_to_all | solution.py:45
  131.8 0.7 copy-done.9
  132.6 1.4 collective-permute-start.16
  133.9 5.9 %all-to-all-done.1 = f32[8,1,1024]{2,1,0:T(1,128)S(1)} async-done(((f32[8,1,1024]{2,1,0:T(1,128)}), f32[8,1,1024]{2,1,0:T(1,128)S(1)}, u32[]{:S(2)}, u32[]{:S(2)}) %all-to-all-start.1) | async-done | bytes 32800 | tf_op jit(solution)/shard_map/project/all_to_all | solution.py:45
  140.3 1.2 multiply_convert_fusion.1.q_ref
  141.5 0.7 broadcast_in_dim.24
  142.3 3.7 %all-to-all-start.2 = ((f32[8,1,1024]{2,1,0:T(1,128)}), f32[8,1,1024]{2,1,0:T(1,128)S(1)}, u32[]{:S(2)}, u32[]{:S(2)}) async-start(f32[8,1,1024]{2,1,0:T(1,128)} %broadcast_in_dim.24), calls=%async_computation.2 | async-start | bytes 65536 | tf_op jit(solution)/shard_map/project/all_to_all | solution.py:45
  146.0 0.5 collective-permute-start.17
  146.5 4.9 %all-to-all-done.2 = f32[8,1,1024]{2,1,0:T(1,128)S(1)} async-done(((f32[8,1,1024]{2,1,0:T(1,128)}), f32[8,1,1024]{2,1,0:T(1,128)S(1)}, u32[]{:S(2)}, u32[]{:S(2)}) %all-to-all-start.2) | async-done | bytes 32800 | tf_op jit(solution)/shard_map/project/all_to_all | solution.py:45
  151.6 0.5 collective-permute-start.21
  152.3 1.4 collective-permute-start.28
  153.7 1.0 slice_bitcast_fusion.2
  154.6 1.0 collective-permute-start.26
  155.7 14.5 %attention.1 = bf16[1024,128]{1,0:T(8,128)(2,1)S(1)} custom-call(s32[16]{0:T(128)S(1)} %stack.134.place_ref, bf16[1024,128]{1,0:T(8,128)(2,1)S(1)} %multiply_convert_fusion.1.q_ref, f32[8,1024]{1,0:T(8,128)S(1)} %bitcast.122, bf16[1024,256]{1,0:T(8,128)(2,1)} %get-tuple-element.32.refs_0_, bf16[1024,256]{1,0:T(8,128)(2,1)S(1)} %collective-permute-done.17.refs_1_, ...), custom_call_target="tpu_custom_call" | custom-call | tf_op jit(solution)/shard_map/attention/pallas_call | solution.py:180
  170.3 1.8 collective-permute-start.27
  172.1 0.8 collective-permute-start.24
  172.9 2.6 %collective-permute-start.25 = (bf16[256,128]{1,0:T(8,128)(2,1)S(1)}, bf16[256,128]{1,0:T(8,128)(2,1)S(1)}, u32[]{:S(2)}, u32[]{:S(2)}) collective-permute-start(bf16[256,128]{1,0:T(8,128)(2,1)S(1)} %get-tuple-element.42), channel_id=1, source_target_pairs={{0,128},{2,130},{128,0},{130,2},{1,129},{3,131},{129,1},{131,3},{4... | collective-permute-start | bytes 196616 | tf_op jit(solution)/shard_map/lift/ppermute | solution.py:33
  175.9 0.5 collective-permute-done.24
  176.4 0.3 convolution_add_fusion.1
  177.0 1.8 collective-permute-done.25
  179.1 23.4 %all_to_all.21 = bf16[8,32,1024]{2,1,0:T(8,128)(2,1)S(1)} all-to-all(bf16[8,32,1024]{2,1,0:T(8,128)(2,1)S(1)} %bitcast.123), channel_id=1, replica_groups=mesh['yh'=2,'z'=8,'x'=4,'yl'=2,'c'=2] {'z'}, dimensions={0} | all-to-all | bytes 1048576 | tf_op jit(solution)/shard_map/lift/all_to_all | solution.py:49
  202.6 1.9 collective-permute-start.29
  204.6 7.2 %collective-permute-done.29 = f32[1,1024]{1,0:T(1,128)S(1)} collective-permute-done((f32[1,1024]{1,0:T(1,128)S(1)}, f32[1,1024]{1,0:T(1,128)S(1)}, u32[]{:S(2)}, u32[]{:S(2)}) %collective-permute-start.29) | collective-permute-done | bytes 4128 | tf_op jit(solution)/shard_map/lift/ppermute | solution.py:28
  211.8 0.9 fusion.5
  (108 shorter events, 3.3 us)
Async XLA Ops:
  0.0 5.7 %copy-start = (bf16[256,4096]{1,0:T(8,128)(2,1)S(1)}, bf16[256,4096]{1,0:T(8,128)(2,1)}, u32[]{:S(2)}) copy-start(bf16[256,4096]{1,0:T(8,128)(2,1)} %param.20) | copy-start | bytes 6291460
  0.0 4.6 %copy-start.15 = (bf16[256,2,256]{2,1,0:T(2,128)(2,1)S(1)}, bf16[256,2,256]{2,1,0:T(2,128)(2,1)}, u32[]{:S(2)}) copy-start(bf16[256,2,256]{2,1,0:T(2,128)(2,1)} %param.19) | copy-start | bytes 786436
  2.6 16.7 %collective-permute-start = (bf16[256,1024]{1,0:T(8,128)(2,1)S(1)}, bf16[256,1024]{1,0:T(8,128)(2,1)}, u32[]{:S(2)}, u32[]{:S(2)}) collective-permute-start(bf16[256,1024]{1,0:T(8,128)(2,1)S(1)} %fusion.4.normed_ref), channel_id=1, source_target_pairs={{0,1},{1,2},{2,3},{3,4},{4,5},{5,6},{6,7},{7,8},{8,9},{9,10},{10,1... | collective-permute-start | bytes 1572872 | tf_op jit(solution)/shard_map/ppermute | solution.py:28
  4.6 14.8 %copy-start.1 = (bf16[256,1024]{1,0:T(8,128)(2,1)S(1)}, bf16[256,1024]{1,0:T(8,128)(2,1)}, u32[]{:S(2)}) copy-start(bf16[256,1024]{1,0:T(8,128)(2,1)} %tokens_ref.1) | copy-start | bytes 1572868
  8.6 40.6 %collective-permute-start.9 = (bf16[1024,256]{1,0:T(8,128)(2,1)}, bf16[1024,256]{1,0:T(8,128)(2,1)}, u32[]{:S(2)}, u32[]{:S(2)}) collective-permute-start(bf16[1024,256]{1,0:T(8,128)(2,1)} %pad_maximum_fusion), channel_id=1, source_target_pairs={{0,0},{16,1},{32,2},{48,3},{64,4},{80,5},{96,6},{112,7},{128,8},{1... | collective-permute-start | bytes 1572872 | tf_op jit(solution)/shard_map/weights/ppermute | solution.py:346
  28.9 0.8 copy-start.5
  29.7 8.3 %collective-permute-start.1 = (bf16[32,1024]{1,0:T(8,128)(2,1)S(1)}, bf16[32,1024]{1,0:T(8,128)(2,1)S(1)}, u32[]{:S(2)}, u32[]{:S(2)}) collective-permute-start(bf16[32,1024]{1,0:T(8,128)(2,1)S(1)} %get-tuple-element.22), channel_id=1, source_target_pairs={{0,64},{16,80},{32,96},{48,112},{64,0},{80,16},{96,32},{112,48},{1... | collective-permute-start | bytes 196616 | tf_op jit(solution)/shard_map/gather_rows/ppermute | solution.py:33
  38.0 16.1 %collective-permute-start.2 = (bf16[2,32,1024]{2,1,0:T(8,128)(2,1)S(1)}, bf16[2,32,1024]{2,1,0:T(8,128)(2,1)S(1)}, u32[]{:S(2)}, u32[]{:S(2)}) collective-permute-start(bf16[2,32,1024]{2,1,0:T(8,128)(2,1)S(1)} %maximum_select_fusion.1), channel_id=1, source_target_pairs={{0,112},{16,0},{32,16},{48,32},{64,48},{80,64},{96,80},{112,96},{1... | collective-permute-start | bytes 393224 | tf_op jit(solution)/shard_map/gather_rows/ppermute | solution.py:33
  47.6 14.7 %collective-permute-start.3 = (bf16[2,32,1024]{2,1,0:T(8,128)(2,1)S(1)}, bf16[2,32,1024]{2,1,0:T(8,128)(2,1)S(1)}, u32[]{:S(2)}, u32[]{:S(2)}) collective-permute-start(bf16[2,32,1024]{2,1,0:T(8,128)(2,1)S(1)} %maximum_select_fusion.1), channel_id=1, source_target_pairs={{0,96},{16,112},{32,0},{48,16},{64,32},{80,48},{96,64},{112,80},{1... | collective-permute-start | bytes 393224 | tf_op jit(solution)/shard_map/gather_rows/ppermute | solution.py:33
  47.6 14.8 %collective-permute-start.4 = (bf16[2,32,1024]{2,1,0:T(8,128)(2,1)S(1)}, bf16[2,32,1024]{2,1,0:T(8,128)(2,1)S(1)}, u32[]{:S(2)}, u32[]{:S(2)}) collective-permute-start(bf16[2,32,1024]{2,1,0:T(8,128)(2,1)S(1)} %maximum_select_fusion.1), channel_id=1, source_target_pairs={{0,16},{16,32},{32,48},{48,64},{64,80},{80,96},{96,112},{112,0},{1... | collective-permute-start | bytes 393224 | tf_op jit(solution)/shard_map/gather_rows/ppermute | solution.py:33
  50.4 12.1 %copy-start.3 = (bf16[1024,256]{1,0:T(8,128)(2,1)S(1)}, bf16[1024,256]{1,0:T(8,128)(2,1)}, u32[]{:S(2)}) copy-start(bf16[1024,256]{1,0:T(8,128)(2,1)} %down_ref.1) | copy-start | bytes 1572868
  50.5 12.1 %copy-start.4 = (bf16[256,1024]{1,0:T(8,128)(2,1)S(1)}, bf16[256,1024]{1,0:T(8,128)(2,1)}, u32[]{:S(2)}) copy-start(bf16[256,1024]{1,0:T(8,128)(2,1)} %up_ref.1) | copy-start | bytes 1572868
  62.5 9.9 %copy-start.8 = (bf16[4,2,32,1024]{3,2,1,0:T(8,128)(2,1)}, bf16[4,2,32,1024]{3,2,1,0:T(8,128)(2,1)S(1)}, u32[]{:S(2)}) copy-start(bf16[4,2,32,1024]{3,2,1,0:T(8,128)(2,1)S(1)} %constant_dynamic-slice_fusion.1) | copy-start | bytes 1572868
  64.2 3.2 %collective-permute-start.10 = (bf16[4,2,672,128]{3,2,1,0:T(8,128)(2,1)S(1)}, bf16[4,2,672,128]{3,2,1,0:T(8,128)(2,1)S(1)}, u32[]{:S(2)}, u32[]{:S(2)}) collective-permute-start(bf16[4,2,672,128]{3,2,1,0:T(8,128)(2,1)S(1)} %get-tuple-element.27), channel_id=1, source_target_pairs={{0,1},{1,0},{2,3},{3,2},{4,5},{5,4},{6,7},{7,6},{8,9},{9,8},{10,11... | collective-permute-start | bytes 4128776 | tf_op jit(solution)/shard_map/weights/ppermute | solution.py:33
  67.7 12.5 %collective-permute-start.13 = (bf16[2,672,128]{2,1,0:T(8,128)(2,1)S(1)}, bf16[2,672,128]{2,1,0:T(8,128)(2,1)S(1)}, u32[]{:S(2)}, u32[]{:S(2)}) collective-permute-start(bf16[2,672,128]{2,1,0:T(8,128)(2,1)S(1)} %get-tuple-element.38), channel_id=1, source_target_pairs={{0,8},{4,12},{8,0},{12,4},{1,9},{5,13},{9,1},{13,5},{2,10},{6,14},... | collective-permute-start | bytes 1032200 | tf_op jit(solution)/shard_map/weights/ppermute | solution.py:33
  68.9 11.8 %collective-permute-start.12 = (bf16[2,672,128]{2,1,0:T(8,128)(2,1)S(1)}, bf16[2,672,128]{2,1,0:T(8,128)(2,1)S(1)}, u32[]{:S(2)}, u32[]{:S(2)}) collective-permute-start(bf16[2,672,128]{2,1,0:T(8,128)(2,1)S(1)} %get-tuple-element.39), channel_id=1, source_target_pairs={{0,12},{4,0},{8,4},{12,8},{1,13},{5,1},{9,5},{13,9},{2,14},{6,2},{... | collective-permute-start | bytes 1032200 | tf_op jit(solution)/shard_map/weights/ppermute | solution.py:33
  68.9 17.8 %collective-permute-start.11 = (bf16[2,672,128]{2,1,0:T(8,128)(2,1)S(1)}, bf16[2,672,128]{2,1,0:T(8,128)(2,1)S(1)}, u32[]{:S(2)}, u32[]{:S(2)}) collective-permute-start(bf16[2,672,128]{2,1,0:T(8,128)(2,1)S(1)} %get-tuple-element.37), channel_id=1, source_target_pairs={{0,4},{4,8},{8,12},{12,0},{1,5},{5,9},{9,13},{13,1},{2,6},{6,10},{... | collective-permute-start | bytes 1032200 | tf_op jit(solution)/shard_map/weights/ppermute | solution.py:33
  71.0 17.6 %collective-permute-start.5 = (bf16[256,1024]{1,0:T(8,128)(2,1)S(1)}, bf16[256,1024]{1,0:T(8,128)(2,1)S(1)}, u32[]{:S(2)}, u32[]{:S(2)}) collective-permute-start(bf16[256,1024]{1,0:T(8,128)(2,1)S(1)} %bitcast.124), channel_id=1, source_target_pairs={{0,130},{2,0},{128,2},{130,128},{1,131},{3,1},{129,3},{131,129},{4... | collective-permute-start | bytes 1572872 | tf_op jit(solution)/shard_map/gather_rows/ppermute | solution.py:33
  72.4 16.3 %collective-permute-start.7 = (bf16[256,1024]{1,0:T(8,128)(2,1)S(1)}, bf16[256,1024]{1,0:T(8,128)(2,1)S(1)}, u32[]{:S(2)}, u32[]{:S(2)}) collective-permute-start(bf16[256,1024]{1,0:T(8,128)(2,1)S(1)} %bitcast.125), channel_id=1, source_target_pairs={{0,2},{2,128},{128,130},{130,0},{1,3},{3,129},{129,131},{131,1},{4... | collective-permute-start | bytes 1572872 | tf_op jit(solution)/shard_map/gather_rows/ppermute | solution.py:33
  87.0 7.3 %collective-permute-start.14 = (bf16[672,128]{1,0:T(8,128)(2,1)S(1)}, bf16[672,128]{1,0:T(8,128)(2,1)S(1)}, u32[]{:S(2)}, u32[]{:S(2)}) collective-permute-start(bf16[672,128]{1,0:T(8,128)(2,1)S(1)} %fusion.13), channel_id=1, source_target_pairs={{0,2},{2,0},{1,3},{3,1},{4,6},{6,4},{5,7},{7,5},{8,10},{10,8},{9,1... | collective-permute-start | bytes 516104 | tf_op jit(solution)/shard_map/weights/ppermute | solution.py:33
  88.6 24.9 %copy-start.13 = (bf16[256,1024]{1,0:T(8,128)(2,1)}, bf16[256,1024]{1,0:T(8,128)(2,1)S(1)}, u32[]{:S(2)}) copy-start(bf16[256,1024]{1,0:T(8,128)(2,1)S(1)} %collective-permute-done.5.above_ref) | copy-start | bytes 1572868
  88.6 10.4 %collective-permute-start.6 = (bf16[128,1024]{1,0:T(8,128)(2,1)S(1)}, bf16[128,1024]{1,0:T(8,128)(2,1)S(1)}, u32[]{:S(2)}, u32[]{:S(2)}) collective-permute-start(bf16[128,1024]{1,0:T(8,128)(2,1)S(1)} %slice.103), channel_id=1, source_target_pairs={{0,130},{2,0},{128,2},{130,128},{1,131},{3,1},{129,3},{131,129},{4... | collective-permute-start | bytes 786440 | tf_op jit(solution)/shard_map/gather_rows/ppermute | solution.py:33
  88.7 24.7 %copy-start.14 = (bf16[256,1024]{1,0:T(8,128)(2,1)}, bf16[256,1024]{1,0:T(8,128)(2,1)S(1)}, u32[]{:S(2)}) copy-start(bf16[256,1024]{1,0:T(8,128)(2,1)S(1)} %collective-permute-done.7.below_ref) | copy-start | bytes 1572868
  88.8 10.3 %collective-permute-start.8 = (bf16[128,1024]{1,0:T(8,128)(2,1)S(1)}, bf16[128,1024]{1,0:T(8,128)(2,1)S(1)}, u32[]{:S(2)}, u32[]{:S(2)}) collective-permute-start(bf16[128,1024]{1,0:T(8,128)(2,1)S(1)} %slice.104), channel_id=1, source_target_pairs={{0,2},{2,128},{128,130},{130,0},{1,3},{3,129},{129,131},{131,1},{4... | collective-permute-start | bytes 786440 | tf_op jit(solution)/shard_map/gather_rows/ppermute | solution.py:33
  99.0 14.4 %copy-start.19 = (bf16[128,1024]{1,0:T(8,128)(2,1)}, bf16[128,1024]{1,0:T(8,128)(2,1)S(1)}, u32[]{:S(2)}) copy-start(bf16[128,1024]{1,0:T(8,128)(2,1)S(1)} %collective-permute-done.6.top_ref) | copy-start | bytes 786436
  99.0 14.4 %copy-start.20 = (bf16[128,1024]{1,0:T(8,128)(2,1)}, bf16[128,1024]{1,0:T(8,128)(2,1)S(1)}, u32[]{:S(2)}) copy-start(bf16[128,1024]{1,0:T(8,128)(2,1)S(1)} %collective-permute-done.8.bottom_ref) | copy-start | bytes 786436
  113.5 2.2 %collective-permute-start.15 = (bf16[4,672,128]{2,1,0:T(8,128)(2,1)S(1)}, bf16[4,672,128]{2,1,0:T(8,128)(2,1)S(1)}, u32[]{:S(2)}, u32[]{:S(2)}) collective-permute-start(bf16[4,672,128]{2,1,0:T(8,128)(2,1)S(1)} %all_to_all.20.near_ref), channel_id=1, source_target_pairs={{0,1},{1,0},{2,3},{3,2},{4,5},{5,4},{6,7},{7,6},{8,9},{9,8},{10,11... | collective-permute-start | bytes 2064392 | tf_op jit(solution)/shard_map/weights/ppermute | solution.py:33
  120.6 0.8 copy-start.2
  121.3 0.7 copy-start.7
  122.1 29.4 %collective-permute-start.18 = (bf16[1024,256]{1,0:T(8,128)(2,1)}, bf16[1024,256]{1,0:T(8,128)(2,1)}, u32[]{:S(2)}, u32[]{:S(2)}) collective-permute-start(bf16[1024,256]{1,0:T(8,128)(2,1)} %get-tuple-element.32.refs_0_), channel_id=1, source_target_pairs={{0,12},{4,0},{8,4},{12,8},{1,13},{5,1},{9,5},{13,9},{2,14},{6,2},{... | collective-permute-start | bytes 1572872 | tf_op jit(solution)/shard_map/project/ppermute | solution.py:33
  123.2 28.3 %collective-permute-start.20 = (bf16[1024,256]{1,0:T(8,128)(2,1)}, bf16[1024,256]{1,0:T(8,128)(2,1)}, u32[]{:S(2)}, u32[]{:S(2)}) collective-permute-start(bf16[1024,256]{1,0:T(8,128)(2,1)} %get-tuple-element.32.refs_0_), channel_id=1, source_target_pairs={{0,4},{4,8},{8,12},{12,0},{1,5},{5,9},{9,13},{13,1},{2,6},{6,10},{... | collective-permute-start | bytes 1572872 | tf_op jit(solution)/shard_map/project/ppermute | solution.py:33
  124.1 28.0 %collective-permute-start.22 = (bf16[1024,256]{1,0:T(8,128)(2,1)}, bf16[1024,256]{1,0:T(8,128)(2,1)}, u32[]{:S(2)}, u32[]{:S(2)}) collective-permute-start(bf16[1024,256]{1,0:T(8,128)(2,1)} %get-tuple-element.32.refs_0_), channel_id=1, source_target_pairs={{0,8},{4,12},{8,0},{12,4},{1,9},{5,13},{9,1},{13,5},{2,10},{6,14},... | collective-permute-start | bytes 1572872 | tf_op jit(solution)/shard_map/project/ppermute | solution.py:33
  125.8 14.0 %all-to-all-start.1 = ((f32[8,1,1024]{2,1,0:T(1,128)}), f32[8,1,1024]{2,1,0:T(1,128)S(1)}, u32[]{:S(2)}, u32[]{:S(2)}) async-start(f32[8,1,1024]{2,1,0:T(1,128)} %broadcast_in_dim.23), calls=%async_computation.1 | async-start | bytes 65536 | tf_op jit(solution)/shard_map/project/all_to_all | solution.py:45
  131.8 0.7 copy-start.9
  131.8 0.7 copy-start.11
  132.6 9.7 %copy-start.18 = (bf16[160,1024]{1,0:T(8,128)(2,1)}, bf16[160,1024]{1,0:T(8,128)(2,1)S(1)}, u32[]{:S(2)}) copy-start(bf16[160,1024]{1,0:T(8,128)(2,1)S(1)} %copy_bitcast_fusion) | copy-start | bytes 983044
  132.6 9.0 %collective-permute-start.16 = (bf16[160,1024]{1,0:T(8,128)(2,1)S(1)}, bf16[160,1024]{1,0:T(8,128)(2,1)S(1)}, u32[]{:S(2)}, u32[]{:S(2)}) collective-permute-start(bf16[160,1024]{1,0:T(8,128)(2,1)S(1)} %copy_bitcast_fusion), channel_id=1, source_target_pairs={{0,2},{2,128},{128,130},{130,0},{1,3},{3,129},{129,131},{131,1},{4... | collective-permute-start | bytes 983048 | tf_op jit(solution)/shard_map/weights/ppermute | solution.py:33
  141.5 0.7 copy-start.16
  142.3 9.2 %all-to-all-start.2 = ((f32[8,1,1024]{2,1,0:T(1,128)}), f32[8,1,1024]{2,1,0:T(1,128)S(1)}, u32[]{:S(2)}, u32[]{:S(2)}) async-start(f32[8,1,1024]{2,1,0:T(1,128)} %broadcast_in_dim.24), calls=%async_computation.2 | async-start | bytes 65536 | tf_op jit(solution)/shard_map/project/all_to_all | solution.py:45
  146.0 8.6 %collective-permute-start.17 = (bf16[1024,256]{1,0:T(8,128)(2,1)}, bf16[1024,256]{1,0:T(8,128)(2,1)S(1)}, u32[]{:S(2)}, u32[]{:S(2)}) collective-permute-start(bf16[1024,256]{1,0:T(8,128)(2,1)} %get-tuple-element.32.refs_0_), channel_id=1, source_target_pairs={{0,1},{1,0},{2,3},{3,2},{4,5},{5,4},{6,7},{7,6},{8,9},{9,8},{10,11... | collective-permute-start | bytes 1572872 | tf_op jit(solution)/shard_map/attention/ppermute | solution.py:33
  151.5 4.2 %collective-permute-start.19 = (bf16[1024,256]{1,0:T(8,128)(2,1)}, bf16[1024,256]{1,0:T(8,128)(2,1)S(1)}, u32[]{:S(2)}, u32[]{:S(2)}) collective-permute-start(bf16[1024,256]{1,0:T(8,128)(2,1)} %collective-permute-done.18.refs_2_), channel_id=1, source_target_pairs={{0,1},{1,0},{2,3},{3,2},{4,5},{5,4},{6,7},{7,6},{8,9},{9,8},{10,11... | collective-permute-start | bytes 1572872 | tf_op jit(solution)/shard_map/attention/ppermute | solution.py:33
  151.6 4.1 %collective-permute-start.21 = (bf16[1024,256]{1,0:T(8,128)(2,1)}, bf16[1024,256]{1,0:T(8,128)(2,1)}, u32[]{:S(2)}, u32[]{:S(2)}) collective-permute-start(bf16[1024,256]{1,0:T(8,128)(2,1)} %collective-permute-done.20.refs_4_), channel_id=1, source_target_pairs={{0,1},{1,0},{2,3},{3,2},{4,5},{5,4},{6,7},{7,6},{8,9},{9,8},{10,11... | collective-permute-start | bytes 1572872 | tf_op jit(solution)/shard_map/attention/ppermute | solution.py:33
  152.1 3.6 %collective-permute-start.23 = (bf16[1024,256]{1,0:T(8,128)(2,1)}, bf16[1024,256]{1,0:T(8,128)(2,1)}, u32[]{:S(2)}, u32[]{:S(2)}) collective-permute-start(bf16[1024,256]{1,0:T(8,128)(2,1)} %collective-permute-done.22.refs_6_), channel_id=1, source_target_pairs={{0,1},{1,0},{2,3},{3,2},{4,5},{5,4},{6,7},{7,6},{8,9},{9,8},{10,11... | collective-permute-start | bytes 1572872 | tf_op jit(solution)/shard_map/attention/ppermute | solution.py:33
  152.3 24.4 %collective-permute-start.28 = (bf16[160,1024]{1,0:T(8,128)(2,1)}, bf16[160,1024]{1,0:T(8,128)(2,1)S(1)}, u32[]{:S(2)}, u32[]{:S(2)}) collective-permute-start(bf16[160,1024]{1,0:T(8,128)(2,1)} %copy-done.18), channel_id=1, source_target_pairs={{0,130},{2,0},{128,2},{130,128},{1,131},{3,1},{129,3},{131,129},{4... | collective-permute-start | bytes 983048 | tf_op jit(solution)/shard_map/weights/ppermute | solution.py:33
  154.6 20.9 %copy-start.10 = (bf16[4,160,128]{2,1,0:T(8,128)(2,1)S(1)}, bf16[4,160,128]{2,1,0:T(8,128)(2,1)}, u32[]{:S(2)}) copy-start(bf16[4,160,128]{2,1,0:T(8,128)(2,1)} %copy-done.9) | copy-start | bytes 491524
  154.6 20.9 %copy-start.12 = (bf16[4,160,128]{2,1,0:T(8,128)(2,1)S(1)}, bf16[4,160,128]{2,1,0:T(8,128)(2,1)}, u32[]{:S(2)}) copy-start(bf16[4,160,128]{2,1,0:T(8,128)(2,1)} %copy-done.11) | copy-start | bytes 491524
  154.6 22.3 %collective-permute-start.26 = (bf16[160,1024]{1,0:T(8,128)(2,1)}, bf16[160,1024]{1,0:T(8,128)(2,1)S(1)}, u32[]{:S(2)}, u32[]{:S(2)}) collective-permute-start(bf16[160,1024]{1,0:T(8,128)(2,1)} %copy-done.16), channel_id=1, source_target_pairs={{0,2},{2,128},{128,130},{130,0},{1,3},{3,129},{129,131},{131,1},{4... | collective-permute-start | bytes 983048 | tf_op jit(solution)/shard_map/weights/ppermute | solution.py:33
  170.2 6.2 %copy-start.17 = (bf16[160,1024]{1,0:T(8,128)(2,1)S(1)}, bf16[160,1024]{1,0:T(8,128)(2,1)}, u32[]{:S(2)}) copy-start(bf16[160,1024]{1,0:T(8,128)(2,1)} %copy-done.16) | copy-start | bytes 983044
  170.3 6.4 %collective-permute-start.27 = (bf16[256,128]{1,0:T(8,128)(2,1)S(1)}, bf16[256,128]{1,0:T(8,128)(2,1)S(1)}, u32[]{:S(2)}, u32[]{:S(2)}) collective-permute-start(bf16[256,128]{1,0:T(8,128)(2,1)S(1)} %get-tuple-element.43), channel_id=1, source_target_pairs={{0,130},{2,0},{128,2},{130,128},{1,131},{3,1},{129,3},{131,129},{4... | collective-permute-start | bytes 196616 | tf_op jit(solution)/shard_map/lift/ppermute | solution.py:33
  172.1 4.3 %collective-permute-start.24 = (bf16[256,128]{1,0:T(8,128)(2,1)S(1)}, bf16[256,128]{1,0:T(8,128)(2,1)S(1)}, u32[]{:S(2)}, u32[]{:S(2)}) collective-permute-start(bf16[256,128]{1,0:T(8,128)(2,1)S(1)} %get-tuple-element.44), channel_id=1, source_target_pairs={{0,2},{2,128},{128,130},{130,0},{1,3},{3,129},{129,131},{131,1},{4... | collective-permute-start | bytes 196616 | tf_op jit(solution)/shard_map/lift/ppermute | solution.py:33
  172.9 5.9 %collective-permute-start.25 = (bf16[256,128]{1,0:T(8,128)(2,1)S(1)}, bf16[256,128]{1,0:T(8,128)(2,1)S(1)}, u32[]{:S(2)}, u32[]{:S(2)}) collective-permute-start(bf16[256,128]{1,0:T(8,128)(2,1)S(1)} %get-tuple-element.42), channel_id=1, source_target_pairs={{0,128},{2,130},{128,0},{130,2},{1,129},{3,131},{129,1},{131,3},{4... | collective-permute-start | bytes 196616 | tf_op jit(solution)/shard_map/lift/ppermute | solution.py:33
  179.1 32.7 %copy-start.6 = (bf16[256,1024]{1,0:T(8,128)(2,1)S(1)}, bf16[256,1024]{1,0:T(8,128)(2,1)}, u32[]{:S(2)}) copy-start(bf16[256,1024]{1,0:T(8,128)(2,1)} %copy-done.5) | copy-start | bytes 1572868
  202.6 9.1 %collective-permute-start.29 = (f32[1,1024]{1,0:T(1,128)S(1)}, f32[1,1024]{1,0:T(1,128)S(1)}, u32[]{:S(2)}, u32[]{:S(2)}) collective-permute-start(f32[1,1024]{1,0:T(1,128)S(1)} %slice.113), channel_id=1, source_target_pairs={{0,1},{1,2},{2,3},{3,4},{4,5},{5,6},{6,7},{7,8},{8,9},{9,10},{10,1... | collective-permute-start | bytes 12296 | tf_op jit(solution)/shard_map/lift/ppermute | solution.py:28
